TPU v7x, 32 devices: a whole 2x2x4 slice. The times are simulated.
32 devices in a mesh: patch: 4 (over y, x), curve: 8 (over z, core).
Axes of the slice: x: 2, y: 2, z: 4, core: 2. Of those that a mesh axis runs over, the one named last changes fastest.
Arguments:
- points: bfloat16 [8, 4, 256, 512], P('curve', 'patch'), may hold values from -6 to 6
- norm_gain_one: float32 [512], replicated, may hold values from 0.4 to 2.5, as said below
- qkv_one: bfloat16 [512, 1536], replicated, may hold values from -0.25 to 0.25
- out_one: bfloat16 [512, 512], replicated, may hold values from -0.25 to 0.25
- hilbert_pos: int32 [8, 4, 256], P('curve', 'patch'), may hold values from 0 to 2047, as said below
- norm_gain_two: float32 [512], replicated, may hold values from 0.4 to 2.5, as said below
- qkv_two: bfloat16 [512, 1536], replicated, may hold values from -0.25 to 0.25
- out_two: bfloat16 [512, 512], replicated, may hold values from -0.25 to 0.25
- hilbert_seg: int32 [4, 8, 256], P('patch', 'curve'), may hold values from 0 to 7, never falling along the last dimension, each value on 1 to 128 neighbouring positions
- out_grad: bfloat16 [4, 8, 256, 512], P('patch', 'curve'), may hold values from -6 to 6
Outputs:
- point_grad: bfloat16 [8, 4, 256, 512], P('curve', 'patch')
Inputs may be any that keep to these rules, and one draw needn't show every extreme that they name: `hilbert_pos`: for each index p of the second dimension, the values over all c and i form a permutation of 0 to 2047. From the points of one device at most 64 have q // 256 equal to any one value, and in every draw some device sends exactly 64 to some owner. `hilbert_seg`: within one device's slots the numbers never fall; a patch holds at most 128 slots. `norm_gain_one`: positive gains. `norm_gain_two`: positive gains.
All inputs are finite; a program needn't handle non-finite values.
Results may differ from a plain program's by a relative error of at most 0.02.
Values may be sent and summed in bfloat16 or wider, within the bound.
No kernel may reach another device: no remote copies, remote signals or barrier semaphores. Data moves between devices by JAX's collectives and lax.ppermute only.
A program may use at most 64 MiB of HBM per device.

v0:
```python
import functools
import math

import jax
import jax.numpy as jnp
from jax import lax
from jax.experimental import pallas as pl
from jax.experimental.pallas import tpu as pltpu
from jax.sharding import PartitionSpec as P


HEADS = 16
EPS = 1e-06
LANES = 128
MASKED = -1e30
MOST_PERMUTES = 16
F32 = jnp.float32
BF16 = jnp.bfloat16
LOG2E = math.log2(math.e)


def dot_nn(left, right):
    return lax.dot_general(left, right, (((1,), (0,)), ((), ())), preferred_element_type=F32)


def dot_nt(left, right):
    return lax.dot_general(left, right, (((1,), (1,)), ((), ())), preferred_element_type=F32)


def dot_tn(left, right):
    return lax.dot_general(left, right, (((0,), (0,)), ((), ())), preferred_element_type=F32)


def norm_rows(rows, gain):
    wide = rows.astype(F32)
    power = jnp.mean(wide * wide, axis=-1, keepdims=True)
    return (wide * lax.rsqrt(power + EPS) * gain).astype(BF16)


def norm_pull(rows, gain, cotangent):
    wide = rows.astype(F32)
    power = jnp.mean(wide * wide, axis=-1, keepdims=True)
    inverse = lax.rsqrt(power + EPS)
    scaled = cotangent.astype(F32) * gain
    along = jnp.mean(scaled * wide, axis=-1, keepdims=True)
    return (inverse * scaled - wide * (inverse * inverse * inverse * along)).astype(BF16)


def head_mask(rows, index, depth):
    return lax.broadcasted_iota(jnp.int32, (rows, LANES), 1) // depth == index


def only(mask, tile):
    return jnp.where(mask, tile, jnp.zeros_like(tile))


def tile_at(t):
    return pl.ds(pl.multiple_of(t * LANES, LANES), LANES)


def vmem_call(body, outs, scratch=(), flops=0, moved=0, **more):
    params = pltpu.CompilerParams(vmem_limit_bytes=24 << 20, **more.pop("params", {}))
    return pl.pallas_call(
        body,
        out_shape=outs,
        scratch_shapes=scratch,
        compiler_params=params,
        cost_estimate=pl.CostEstimate(flops=flops, bytes_accessed=moved, transcendentals=0),
        **more,
    )


HBM_SPEC = pl.BlockSpec(memory_space=pltpu.MemorySpace.HBM)
SMEM_SPEC = pl.BlockSpec(memory_space=pltpu.MemorySpace.SMEM)
VMEM_SPEC = pl.BlockSpec(memory_space=pltpu.MemorySpace.VMEM)
LOW, HIGH = 2.0**-60, 2.0**100


def column(row):
    return jnp.transpose(jnp.broadcast_to(row.astype(F32), (LANES, row.shape[1])))[:, :1]


def start_all(pairs, sems):
    copies = [pltpu.make_async_copy(src, dst, sems.at[i]) for i, (src, dst) in enumerate(pairs)]
    for copy in copies:
        copy.start()
    return copies


def flip_tile(tile):
    return jnp.transpose(tile)


def with_ones(tile):
    return jnp.concatenate([tile, jnp.ones_like(tile)], axis=1)


def unshifted(depth, t, q_tile, k_tile, v_tile, weights_ref):
    count = q_tile.shape[0]
    scale = depth ** (-0.5) * LOG2E
    right = with_ones(v_tile)
    mixed = jnp.zeros((count, LANES), F32)
    sums = jnp.zeros((count, LANES), F32)
    for j in range(LANES // depth):
        mask = head_mask(count, j, depth)
        scores = dot_nt(only(mask, q_tile), k_tile)
        shifted = jnp.exp2(scores * scale).astype(BF16)
        weights_ref[t * (LANES // depth) + j] = shifted
        both = dot_nn(shifted, right)
        mixed = jnp.where(mask, both[:, :LANES], mixed)
        sums = jnp.where(mask, both[:, LANES:], sums)
    return mixed, sums


def route_body(chunks, capacity, me_ref, target_ref, slot_ref, at_ref):
    count = target_ref.shape[1]
    slots = 2 * count
    target = target_ref[...]
    shift = count.bit_length() - 1
    owner = lax.shift_right_logical(target, jnp.full_like(target, shift))
    offset = target - lax.shift_left(owner, jnp.full_like(target, shift))
    same = column(owner) == owner.astype(F32)
    earlier = lax.broadcasted_iota(jnp.int32, (count, count), 0) < (
        lax.broadcasted_iota(jnp.int32, (count, count), 1)
    )
    ranking = jnp.sum(jnp.where(same & earlier, 1.0, 0.0), axis=0, keepdims=True).astype(jnp.int32)
    lane = owner if chunks == 1 else lax.bitwise_xor(owner, jnp.full_like(owner, me_ref[0]))
    slot_ref[...] = lane * capacity + ranking
    hit = column(lane * capacity + ranking) == (
        lax.broadcasted_iota(jnp.int32, (count, slots), 1).astype(F32)
    )
    at = jnp.sum(jnp.where(hit, column(offset) - count, 0.0), axis=0, keepdims=True) + count
    at_ref[...] = at.astype(at_ref.dtype)


def prep_body(depth, *refs):
    x_ref, gain_ref, w_ref = refs[:3]
    q_ref, k_ref, v_ref, weights_ref, mixed_ref, sums_ref = refs[3:]
    width = x_ref.shape[1]
    normed = norm_rows(x_ref[...], gain_ref[...])
    q_ref[...] = dot_nn(normed, w_ref[:, :width]).astype(BF16)
    k_ref[...] = dot_nn(normed, w_ref[:, width : 2 * width]).astype(BF16)
    v_ref[...] = dot_nn(normed, w_ref[:, 2 * width :]).astype(BF16)

    def tile_step(t, carry):
        at = tile_at(t)
        mixed_ref[:, at], sums_ref[:, at] = unshifted(
            depth, t, q_ref[:, at], k_ref[:, at], v_ref[:, at], weights_ref
        )
        return carry

    lax.fori_loop(0, width // LANES, tile_step, 0)


def middle_body(depth, *refs):
    x_ref, gain_ref, w_ref, q_ref, mixed_in_ref, sums_in_ref = refs[:6]
    k_ref, v_ref, weights_ref, mixed_ref, sums_ref = refs[6:]
    width = x_ref.shape[1]
    normed = norm_rows(x_ref[...], gain_ref[...])
    k_ref[...] = dot_nn(normed, w_ref[:, width : 2 * width]).astype(BF16)
    v_ref[...] = dot_nn(normed, w_ref[:, 2 * width :]).astype(BF16)

    def tile_step(t, carry):
        at = tile_at(t)
        mixed, sums = unshifted(depth, t, q_ref[:, at], k_ref[:, at], v_ref[:, at], weights_ref)
        mixed_ref[:, at] = mixed + mixed_in_ref[:, at]
        sums_ref[:, at] = sums + sums_in_ref[:, at]
        return carry

    lax.fori_loop(0, width // LANES, tile_step, 0)


def forward_body(early, peers, chunks, capacity, depth, *refs):
    x_ref, gain_ref, w_ref, out_w_ref, slot_ref, at_ref, q_ref, mixed_in_ref, sums_in_ref = refs[:9]
    refs = refs[9:]
    early_keys, early_values, refs = refs[:early], refs[early : 2 * early], refs[2 * early :]
    others, refs = refs[: peers + 1 - early], refs[peers + 1 - early + early :]
    keys_ref, values_ref, weights_ref, mixed_ref, inverse_ref, lse_ref = refs[:6]
    early_weights, refs = refs[6 : 6 + early], refs[6 + early :]
    sends, (safe, out_sems) = refs[:chunks], refs[chunks:]
    count, width = x_ref.shape
    heads = LANES // depth
    for index, other in enumerate(others):
        rows = slice(index * count, (index + 1) * count)
        normed = norm_rows(other[...], gain_ref[...])
        keys_ref[rows] = dot_nn(normed, w_ref[:, width : 2 * width]).astype(BF16)
        values_ref[rows] = dot_nn(normed, w_ref[:, 2 * width :]).astype(BF16)

    def finish_tile(t, at, mixed, sums, tops):
        inverse = 1.0 / sums
        mixed_ref[:, at] = (mixed * inverse).astype(BF16)
        inverse_ref[:, at] = inverse
        flipped = flip_tile(tops + jnp.log(sums) * LOG2E)
        for j in range(heads):
            lse_ref[pl.ds(t * heads + j, 1)] = flipped[j * depth : j * depth + 1]

    def fast_step(t, bad):
        at = tile_at(t)
        mixed, sums = unshifted(
            depth, t, q_ref[:, at], keys_ref[:, at], values_ref[:, at], weights_ref
        )
        mixed += mixed_in_ref[:, at]
        sums += sums_in_ref[:, at]
        finish_tile(t, at, mixed, sums, 0.0)
        return jnp.where((sums >= LOW) & (sums <= HIGH), bad, 1.0)

    bad = lax.fori_loop(0, width // LANES, fast_step, jnp.zeros((count, LANES), F32))

    @pl.when(jnp.max(bad) > 0.0)
    def _():
        scale = depth ** (-0.5) * LOG2E

        def safe_step(t, carry):
            at = tile_at(t)
            keys = jnp.concatenate([ref[:, at] for ref in early_keys + (keys_ref,)], axis=0)
            values = jnp.concatenate([ref[:, at] for ref in early_values + (values_ref,)], axis=0)
            right = with_ones(values)
            mixed = jnp.zeros((count, LANES), F32)
            sums = jnp.ones((count, LANES), F32)
            tops = jnp.zeros((count, LANES), F32)
            for j in range(heads):
                mask = head_mask(count, j, depth)
                scores = dot_nt(only(mask, q_ref[:, at]), keys)
                top = jnp.max(scores, axis=-1, keepdims=True) * scale
                shifted = jnp.exp2(scores * scale - top).astype(BF16)
                weights_ref[t * heads + j] = shifted[:, early * count :]
                for index in range(early):
                    part = shifted[:, index * count : (index + 1) * count]
                    safe[index, t * heads + j] = part
                both = dot_nn(shifted, right)
                mixed = jnp.where(mask, both[:, :LANES], mixed)
                sums = jnp.where(mask, both[:, LANES:], sums)
                tops = jnp.where(mask, top, tops)
            finish_tile(t, at, mixed, sums, tops)
            return carry

        lax.fori_loop(0, width // LANES, safe_step, 0)
        pairs = [(safe.at[index], early_weights[index]) for index in range(early)]
        for copy in start_all(pairs, out_sems):
            copy.wait()

    moved = (x_ref[...].astype(F32) + dot_nn(mixed_ref[...], out_w_ref[...])).astype(BF16)
    slots = 2 * count
    picked = (lax.broadcasted_iota(jnp.int32, (slots, count), 0) == slot_ref[...]).astype(F32)
    leaving = dot_nn(picked.astype(BF16), moved).astype(BF16)
    if chunks == 1:
        sends[0][...] = leaving
    else:
        tail = sends[0].shape[0] - capacity * (width // LANES)
        line = jnp.broadcast_to(at_ref[...], (tail, slots)).astype(BF16)
        for m, send in enumerate(sends):
            part = slice(m * capacity, (m + 1) * capacity)
            for t in range(width // LANES):
                tile = leaving[part, t * LANES : (t + 1) * LANES]
                send[t * capacity : (t + 1) * capacity] = tile
            padding = jnp.zeros((tail, LANES - capacity), BF16)
            send[send.shape[0] - tail :] = jnp.concatenate([line[:, part], padding], axis=1)


def second_body(chunks, depth, *refs):
    land_ref, seg_ref, gain_ref, w_ref, out_w_ref, grad_ref = refs[:6]
    arrived = refs[6 : 6 + chunks]
    sends = refs[6 + chunks : 6 + 2 * chunks]
    packed, packed_grad, mixed_grad, bias = refs[6 + 2 * chunks :]
    count, width = grad_ref.shape
    slots = 2 * count
    size = slots // chunks
    mixed_grad[...] = dot_nt(grad_ref[...], out_w_ref[...]).astype(BF16)
    bias[...] = jnp.where(column(seg_ref[...]) == seg_ref[...].astype(F32), 0.0, MASKED)
    if chunks == 1:
        landing = land_ref[...].astype(F32)
        rows = arrived[0][...]
    else:
        ends = [piece[size * (width // LANES) :].astype(F32)[:1, :size] for piece in arrived]
        landing = jnp.concatenate(ends, axis=1)
        rows = []
        for piece in arrived:
            tiles = [piece[t * size : (t + 1) * size] for t in range(width // LANES)]
            rows.append(jnp.concatenate(tiles, axis=1))
        rows = jnp.concatenate(rows, axis=0)
    place = lax.broadcasted_iota(jnp.int32, (count, slots), 0).astype(F32) == landing
    place = place.astype(F32)
    hilbert = dot_nn(place.astype(BF16), rows).astype(BF16)
    normed = norm_rows(hilbert, gain_ref[...])
    packed[...] = dot_nn(normed, w_ref[...]).astype(BF16)
    scale = depth ** (-0.5)

    def tile_step(t, carry):
        at = tile_at(t)
        k_at = tile_at(t + width // LANES)
        v_at = tile_at(t + 2 * (width // LANES))
        q_tile = packed[:, at]
        k_tile = packed[:, k_at]
        v_tile = packed[:, v_at]
        g_tile = mixed_grad[:, at]
        k_flipped = flip_tile(k_tile)
        heads = LANES // depth
        masks = [head_mask(count, j, depth) for j in range(heads)]
        stacked = (heads, count, count)
        k_heads = jnp.concatenate([only(mask, k_tile) for mask in masks], axis=0)
        v_heads = jnp.concatenate([only(mask, v_tile) for mask in masks], axis=0)
        scores = dot_nt(k_heads, q_tile).reshape(stacked) * (scale * LOG2E) + bias[...][None]
        weight_grad = dot_nt(v_heads, g_tile).reshape(stacked)
        shifted = jnp.exp2(scores - jnp.max(scores, axis=1, keepdims=True))
        weights = shifted * (1.0 / jnp.sum(shifted, axis=1, keepdims=True))
        carried = jnp.sum(weights * weight_grad, axis=1, keepdims=True)
        score_grad = (weights * (weight_grad - carried)).astype(BF16)
        dk_heads = dot_nn(score_grad.reshape(heads * count, count), q_tile)
        dv_heads = dot_nn(weights.astype(BF16).reshape(heads * count, count), g_tile)
        dk, dv, dq = dk_heads[:count], dv_heads[:count], []
        for j in range(heads):
            part = slice(j * count, (j + 1) * count)
            dk = jnp.where(masks[j], dk_heads[part], dk)
            dv = jnp.where(masks[j], dv_heads[part], dv)
            dq.append(dot_nn(k_flipped[j * depth : (j + 1) * depth], score_grad[j]))
        dq = jnp.transpose(jnp.concatenate(dq, axis=0))
        packed_grad[:, at] = (dq * scale).astype(BF16)
        packed_grad[:, k_at] = (dk * scale).astype(BF16)
        packed_grad[:, v_at] = dv.astype(BF16)
        return carry

    lax.fori_loop(0, width // LANES, tile_step, 0)
    normed_grad = dot_nt(packed_grad[...], w_ref[...]).astype(BF16)
    total = grad_ref[...].astype(F32) + norm_pull(hilbert, gain_ref[...], normed_grad).astype(F32)
    back = lax.broadcasted_iota(jnp.int32, (slots, count), 1).astype(F32) == column(landing)
    returning = dot_nn(back.astype(F32).astype(BF16), total.astype(BF16)).astype(BF16)
    for m, send in enumerate(sends):
        send[...] = returning[m * size : (m + 1) * size]


def queries_body(peers, *refs):
    gain_ref, w_ref, q_ref = refs[:3]
    others = refs[3 : 3 + peers]
    out_ref = refs[3 + peers]
    count, width = q_ref.shape
    out_ref[:count] = q_ref[...]
    for index, other in enumerate(others):
        rows = slice((index + 1) * count, (index + 2) * count)
        normed = norm_rows(other[...], gain_ref[...])
        out_ref[rows] = dot_nn(normed, w_ref[:, :width]).astype(BF16)


def spread(rows, width):
    heads = rows.shape[0]
    pick = lax.broadcasted_iota(jnp.int32, (heads, width), 1) // (width // heads) == (
        lax.broadcasted_iota(jnp.int32, (heads, width), 0)
    )
    return dot_tn(rows, pick.astype(F32).astype(BF16))


def weights_flipped_body(peers, depth, *refs):
    k_ref, queries_ref = refs[:2]
    lse_refs = refs[2 : 3 + peers]
    out_ref = refs[3 + peers]
    scale = depth ** (-0.5) * LOG2E
    heads = LANES // depth
    count = k_ref.shape[0]

    def tile_step(t, carry):
        at = tile_at(t)
        for j in range(heads):
            mask = head_mask(count, j, depth)
            scores = dot_nt(only(mask, k_ref[:, at]), queries_ref[:, at])
            h = t * heads + j
            line = jnp.concatenate([ref[pl.ds(h, 1)] for ref in lse_refs], axis=1)
            out_ref[h] = jnp.exp2(scores * scale - line).astype(BF16)
        return carry

    lax.fori_loop(0, k_ref.shape[1] // LANES, tile_step, 0)


def home_body(chunks, depth, *refs):
    slot_ref, mixed_ref, out_w_ref = refs[:3]
    home = refs[3 : 3 + chunks]
    moved_ref, grad_ref = refs[3 + chunks :]
    count, width = moved_ref.shape
    slots = 2 * count
    take = lax.broadcasted_iota(jnp.int32, (count, slots), 1).astype(F32) == column(slot_ref[...])
    take = take.astype(F32).astype(BF16)
    moved = dot_nn(take, jnp.concatenate([piece[...] for piece in home], axis=0)).astype(BF16)
    moved_ref[...] = moved
    grad = dot_nt(moved, out_w_ref[...]).astype(BF16)
    grad_ref[:count] = grad
    product = grad.astype(F32) * mixed_ref[...].astype(F32)
    high = product.astype(BF16)
    low = (product - high.astype(F32)).astype(BF16)
    heads = width // depth
    pick = lax.broadcasted_iota(jnp.int32, (heads, width), 1) // depth == (
        lax.broadcasted_iota(jnp.int32, (heads, width), 0)
    )
    pick = pick.astype(F32).astype(BF16)
    rows = dot_nt(pick, high) + dot_nt(pick, low)
    rows_high = rows.astype(BF16)
    grad_ref[count:, :count] = rows_high
    grad_ref[count:, count:] = (rows - rows_high.astype(F32)).astype(BF16)


def key_tile(depth, t, v_tile, weights_ref, columns, queries, grads, deltas_ref):
    count = v_tile.shape[0]
    heads = LANES // depth
    dk = jnp.zeros((count, LANES), F32)
    dv = jnp.zeros((count, LANES), F32)
    for j in range(heads):
        h = t * heads + j
        mask = head_mask(count, j, depth)
        weights = weights_ref[h, :, columns]
        weight_grad = dot_nt(only(mask, v_tile), grads)
        delta = deltas_ref[pl.ds(h, 1)]
        score_grad = (weights.astype(F32) * (weight_grad - delta)).astype(BF16)
        dv = jnp.where(mask, dot_nn(weights, grads), dv)
        dk = jnp.where(mask, dot_nn(score_grad, queries), dk)
    return dk, dv


def halves(lines):
    half = lines.shape[1] // 2
    return lines[:, :half], lines[:, half:]


def query_grad_body(parts, depth, *refs):
    weights_refs, refs = refs[:parts], refs[parts:]
    keys_refs, refs = refs[:parts], refs[parts:]
    values_refs, refs = refs[:parts], refs[parts:]
    inverse_ref, flipped_ref, grad_ref, q_ref = refs[:4]
    out_ref, dk_ref, dv_ref, lines, wide = refs[4:]
    count, width = out_ref.shape
    heads = LANES // depth
    high, low = halves(grad_ref[count:])
    lines[...] = high.astype(F32) + low.astype(F32)
    wide[...] = spread(high, width) + spread(low, width)

    def tile_step(t, carry):
        at = tile_at(t)
        g_tile = grad_ref[:count, at]
        delta_tile = wide[:, at]
        keys = jnp.concatenate([ref[:, at] for ref in keys_refs], axis=0)
        values = jnp.concatenate([ref[:, at] for ref in values_refs], axis=0)
        dq = jnp.zeros((count, LANES), F32)
        for j in range(heads):
            mask = head_mask(count, j, depth)
            weight_grad = dot_nt(only(mask, g_tile), values)
            delta = delta_tile[:, j * depth : j * depth + 1]
            weights = jnp.concatenate([ref[t * heads + j] for ref in weights_refs], axis=1)
            score_grad = (weights.astype(F32) * (weight_grad - delta)).astype(BF16)
            dq = jnp.where(mask, dot_nn(score_grad, keys), dq)
        out_ref[:, at] = (dq * (inverse_ref[:, at] * depth ** (-0.5))).astype(BF16)
        dk_ref[:, at], dv_ref[:, at] = key_tile(
            depth,
            t,
            values_refs[0][:, at],
            flipped_ref,
            slice(0, count),
            q_ref[:, at],
            g_tile,
            lines,
        )
        return carry

    lax.fori_loop(0, width // LANES, tile_step, 0)


def key_middle_body(index, depth, *refs):
    flipped_ref, v_ref, queries_ref, dk_in_ref, dv_in_ref, grad_ref = refs[:6]
    dk_ref, dv_ref, lines = refs[6:]
    count, width = v_ref.shape
    high, low = halves(grad_ref[count:])
    lines[...] = high.astype(F32) + low.astype(F32)
    rows = slice(index * count, (index + 1) * count)

    def tile_step(t, carry):
        at = tile_at(t)
        dk, dv = key_tile(
            depth,
            t,
            v_ref[:, at],
            flipped_ref,
            rows,
            queries_ref[rows, at],
            grad_ref[:count, at],
            lines,
        )
        dk_ref[:, at] = dk + dk_in_ref[:, at]
        dv_ref[:, at] = dv + dv_in_ref[:, at]
        return carry

    lax.fori_loop(0, width // LANES, tile_step, 0)


def key_grad_body(early, peers, depth, *refs):
    flipped_ref, v_ref, queries_ref, dq_ref, dk_ref, dv_ref = refs[:6]
    x_ref, gain_ref, w_ref, moved_ref = refs[6:10]
    others = refs[10 : 11 + peers - early]
    out_ref, packed_grad, grads, lines = refs[11 + peers - early :]
    count, width = x_ref.shape
    packed_grad[:, :width] = dq_ref[...]
    for i, other in enumerate(others):
        rows = slice(i * count, (i + 1) * count)
        grads[rows] = other[:count]
        high, low = halves(other[count:])
        lines[:, rows] = high.astype(F32) + low.astype(F32)

    def tile_step(t, carry):
        at = tile_at(t)
        dk, dv = key_tile(
            depth,
            t,
            v_ref[:, at],
            flipped_ref,
            slice(early * count, (peers + 1) * count),
            queries_ref[early * count :, at],
            grads[:, at],
            lines,
        )
        dk = (dk + dk_ref[:, at]) * depth ** (-0.5)
        packed_grad[:, tile_at(t + width // LANES)] = dk.astype(BF16)
        packed_grad[:, tile_at(t + 2 * (width // LANES))] = (dv + dv_ref[:, at]).astype(BF16)
        return carry

    lax.fori_loop(0, width // LANES, tile_step, 0)
    normed_grad = dot_nt(packed_grad[...], w_ref[...]).astype(BF16)
    path = norm_pull(x_ref[...], gain_ref[...], normed_grad)
    out_ref[...] = (moved_ref[...].astype(F32) + path.astype(F32)).astype(BF16)


def single_first(size):
    return sorted(range(1, size), key=lambda step: (step.bit_count(), -step))


def by_xor(array, axis, step):
    size = lax.axis_size(axis)
    return lax.ppermute(array, axis, [(i, i ^ step) for i in range(size)])


def exchange(pieces, axis):
    if len(pieces) == 1:
        size = lax.axis_size(axis)
        stacked = pieces[0].reshape((size, -1) + pieces[0].shape[1:])
        got = lax.all_to_all(stacked, axis, split_axis=0, concat_axis=0, tiled=True)
        return [got.reshape(pieces[0].shape)]
    return [pieces[0]] + [by_xor(pieces[m], axis, m) for m in range(1, len(pieces))]


def shards(
    points, gain_one, qkv_one, out_one, hilbert_pos, gain_two, qkv_two, out_two, segments, out_grad
):
    count, width = points.shape[2:]
    depth = width // HEADS
    tiles = width // LANES
    patch_size = lax.axis_size("patch")
    curve_size = lax.axis_size("curve")
    peers = patch_size - 1
    total = patch_size * count
    slots = 2 * count
    capacity = slots // curve_size
    chunks = curve_size if curve_size <= MOST_PERMUTES else 1
    rows_bf16 = jax.ShapeDtypeStruct((count, width), BF16)
    all_bf16 = jax.ShapeDtypeStruct((total, width), BF16)
    chunk_bf16 = jax.ShapeDtypeStruct((slots // chunks, width), BF16)

    x = points.reshape(count, width)
    steps = single_first(patch_size)
    others = [by_xor(x, "patch", m) for m in steps]
    gain_one = gain_one.reshape(1, width)
    gain_two = gain_two.reshape(1, width)

    def shape(kind, *dims):
        return jax.ShapeDtypeStruct(dims, kind)

    me = lax.axis_index("curve").astype(jnp.int32).reshape(1)
    slot, leaving_at = vmem_call(
        functools.partial(route_body, chunks, capacity),
        (shape(jnp.int32, 1, count), shape(jnp.int32 if chunks == 1 else F32, 1, slots)),
        flops=1 << 20,
        moved=1 << 12,
        in_specs=[SMEM_SPEC, VMEM_SPEC],
    )(me, hilbert_pos.reshape(1, count))
    x_then, slot, leaving_at = lax.optimization_barrier((x, slot, leaving_at))
    landing = leaving_at
    if chunks == 1:
        landing = lax.all_to_all(
            leaving_at.reshape(curve_size, 1, capacity),
            "curve",
            split_axis=0,
            concat_axis=0,
            tiled=True,
        ).reshape(1, slots)

    rows_f32 = shape(F32, count, width)
    lines_f32 = shape(F32, HEADS, count)
    square = shape(BF16, HEADS, count, count)
    dma = pltpu.SemaphoreType.DMA
    q, k, v, own_weights, sum_mixed, sums = vmem_call(
        functools.partial(prep_body, depth),
        (rows_bf16,) * 3 + (square,) + (rows_f32,) * 2,
        flops=2 << 30,
        moved=4 << 20,
    )(x_then, gain_one, qkv_one)
    early_keys, early_values, early_weights = [k], [v], [own_weights]
    if peers > 1:
        k_next, v_next, weights_next, sum_mixed, sums = vmem_call(
            functools.partial(middle_body, depth),
            (rows_bf16,) * 2 + (square,) + (rows_f32,) * 2,
            flops=2 << 30,
            moved=4 << 20,
        )(others[0], gain_one, qkv_one, q, sum_mixed, sums)
        early_keys.append(k_next)
        early_values.append(v_next)
        early_weights.append(weights_next)
    early = len(early_keys)
    late = peers + 1 - early
    late_bf16 = shape(BF16, late * count, width)
    embedded = shape(BF16, capacity * tiles + 8, LANES)
    sent = chunk_bf16 if chunks == 1 else embedded
    first_weights = 9 + 2 * early + late
    results = vmem_call(
        functools.partial(forward_body, early, peers, chunks, capacity, depth),
        (late_bf16, late_bf16, shape(BF16, HEADS, count, late * count))
        + (rows_bf16, rows_f32, lines_f32)
        + (square,) * early
        + (sent,) * chunks,
        [
            pltpu.VMEM((early,) + square.shape, BF16),
            dma((early,)),
        ],
        flops=8 << 30,
        moved=8 << 20,
        in_specs=[VMEM_SPEC] * first_weights + [HBM_SPEC] * early,
        out_specs=(VMEM_SPEC,) * 6 + (HBM_SPEC,) * early + (VMEM_SPEC,) * chunks,
        input_output_aliases={first_weights + index: 6 + index for index in range(early)},
    )(
        x,
        gain_one,
        qkv_one,
        out_one,
        slot,
        leaving_at,
        q,
        sum_mixed,
        sums,
        *early_keys,
        *early_values,
        *others[early - 1 :],
        *early_weights,
    )
    late_keys, late_values, late_weights, mixed, inverse, lse = results[:6]
    all_weights = list(results[6 : 6 + early]) + [late_weights]
    all_keys, all_values = early_keys + [late_keys], early_values + [late_values]
    arrived = exchange(results[6 + early :], "curve")
    lse_all = [lse] + [by_xor(lse, "patch", m) for m in steps]

    queries_all = vmem_call(
        functools.partial(queries_body, peers),
        all_bf16,
        flops=1 << 29,
        moved=3 << 20,
        in_specs=[VMEM_SPEC] * (3 + peers),
    )(gain_one, qkv_one, q, *others)
    flipped = vmem_call(
        functools.partial(weights_flipped_body, peers, depth),
        shape(BF16, HEADS, count, total),
        flops=4 << 30,
        moved=10 << 20,
    )(k, queries_all, *lse_all)

    returning = vmem_call(
        functools.partial(second_body, chunks, depth),
        (chunk_bf16,) * chunks,
        [
            pltpu.VMEM((count, 3 * width), BF16),
            pltpu.VMEM((count, 3 * width), BF16),
            pltpu.VMEM((count, width), BF16),
            pltpu.VMEM((count, count), F32),
        ],
        flops=8 << 30,
        moved=4 << 20,
    )(
        landing,
        segments.reshape(1, count),
        gain_two,
        qkv_two,
        out_two,
        out_grad.reshape(count, width),
        *arrived,
    )
    home = exchange(returning, "curve")

    moved_grad, grad_own = vmem_call(
        functools.partial(home_body, chunks, depth),
        (rows_bf16, shape(BF16, count + HEADS, width)),
        flops=1 << 29,
        moved=2 << 20,
    )(slot, mixed, out_one, *home)
    grads = [by_xor(grad_own, "patch", m) for m in steps]

    query_grad, key_grad, value_grad = vmem_call(
        functools.partial(query_grad_body, len(all_keys), depth),
        (rows_bf16, rows_f32, rows_f32),
        [pltpu.VMEM((HEADS, count), F32), pltpu.VMEM((count, width), F32)],
        flops=8 << 30,
        moved=10 << 20,
    )(*all_weights, *all_keys, *all_values, inverse, flipped, grad_own, q)
    for index in range(1, early):
        key_grad, value_grad = vmem_call(
            functools.partial(key_middle_body, index, depth),
            (rows_f32, rows_f32),
            [pltpu.VMEM((HEADS, count), F32)],
            flops=2 << 30,
            moved=4 << 20,
        )(flipped, v, queries_all, key_grad, value_grad, grads[index - 1])
    result = vmem_call(
        functools.partial(key_grad_body, early, peers, depth),
        rows_bf16,
        [
            pltpu.VMEM((count, 3 * width), BF16),
            pltpu.VMEM((late * count, width), BF16),
            pltpu.VMEM((HEADS, late * count), F32),
        ],
        flops=8 << 30,
        moved=14 << 20,
    )(
        flipped,
        v,
        queries_all,
        query_grad,
        key_grad,
        value_grad,
        x,
        gain_one,
        qkv_one,
        moved_grad,
        *grads[early - 1 :],
    )
    return result.reshape(points.shape)


def solution(mesh):
    in_specs = (
        P("curve", "patch", None, None),
        P(),
        P(),
        P(),
        P("curve", "patch", None),
        P(),
        P(),
        P(),
        P("patch", "curve", None),
        P("patch", "curve", None, None),
    )
    out_specs = P("curve", "patch", None, None)

    return jax.shard_map(shards, mesh=mesh, in_specs=in_specs, out_specs=out_specs, check_vma=False)
```

profile of v0, /device:TPU:0, one launch (start us, length us, event | category | flops | bytes accessed | tf_op | source)
XLA Modules:
  0.0 86.0 jit_solution(6021900063639716027)
XLA Ops:
  0.0 3.0 %collective-permute-start = (bf16[256,512]{1,0:T(8,128)(2,1)}, bf16[256,512]{1,0:T(8,128)(2,1)S(1)}, u32[]{:S(2)}, u32[]{:S(2)}) collective-permute-start(bf16[256,512]{1,0:T(8,128)(2,1)} %bitcast.14), channel_id=1, source_target_pairs={{0,16},{8,24},{16,0},{24,8},{1,17},{9,25},{17,1},{25,9},{2,18},{10... | collective-permute-start | bytes 786440 | tf_op jit(solution)/shard_map/ppermute | solution.py:531
  3.0 1.5 %collective-permute-start.1 = (bf16[256,512]{1,0:T(8,128)(2,1)}, bf16[256,512]{1,0:T(8,128)(2,1)S(1)}, u32[]{:S(2)}, u32[]{:S(2)}) collective-permute-start(bf16[256,512]{1,0:T(8,128)(2,1)} %bitcast.15), channel_id=1, source_target_pairs={{0,8},{8,0},{16,24},{24,16},{1,9},{9,1},{17,25},{25,17},{2,10},{10... | collective-permute-start | bytes 786440 | tf_op jit(solution)/shard_map/ppermute | solution.py:531
  5.6 1.4 %copy-done = bf16[512,1536]{1,0:T(8,128)(2,1)S(1)} copy-done((bf16[512,1536]{1,0:T(8,128)(2,1)S(1)}, bf16[512,1536]{1,0:T(8,128)(2,1)}, u32[]{:S(2)}) %copy-start) | copy-done | bytes 1572888
  7.7 0.9 %copy-done.8 = bf16[1,1,256,512]{3,2,1,0:T(8,128)(2,1)S(1)} copy-done((bf16[1,1,256,512]{3,2,1,0:T(8,128)(2,1)S(1)}, bf16[1,1,256,512]{3,2,1,0:T(8,128)(2,1)}, u32[]{:S(2)}) %copy-start.8) | copy-done | bytes 262168
  8.6 2.9 %shard_map.101 = (bf16[256,512]{1,0:T(8,128)(2,1)S(1)}, bf16[256,512]{1,0:T(8,128)(2,1)S(1)}, bf16[256,512]{1,0:T(8,128)(2,1)S(1)}, bf16[16,256,256]{2,1,0:T(8,1...) custom-call(bf16[256,512]{1,0:T(8,128)(2,1)S(1)} %bitcast.17, f32[1,512]{1,0:T(1,128)S(1)} %bitcast.8, ...), custom_call_target="tpu_custom_call" | custom-call | flops 2147483648 | bytes 4194304 | tf_op jit(solution)/shard_map/pallas_call | solution.py:592
  11.5 2.7 %shard_map.103 = (bf16[256,512]{1,0:T(8,128)(2,1)S(1)}, bf16[256,512]{1,0:T(8,128)(2,1)S(1)}, bf16[16,256,256]{2,1,0:T(8,128)(2,1)S(1)}, f32[256,512]{1,0:T(8,128)S(1)}, f32[256,512]{1,0:T(8,128)S(1)}) custom-call(bf16[256,512]{1,0:T(8,128)(2,1)S(1)} %collective-permute-done.refs_3_.refs_0_, f32[1,512]{1,0:T(1,128)S(1)} %bitcast.9, ...), custom_call_target="tpu_custom_call" | custom-call | flops 2147483648 | bytes 4194304 | tf_op jit(solution)/shard_map/pallas_call | solution.py:600
  14.3 2.0 %collective-permute-done.2.refs_5_.refs_14_ = bf16[256,512]{1,0:T(8,128)(2,1)S(1)} collective-permute-done((bf16[256,512]{1,0:T(8,128)(2,1)}, bf16[256,512]{1,0:T(8,128)(2,1)S(1)}, u32[]{:S(2)}, u32[]{:S(2)}) %collective-permute-start.2) | collective-permute-done | bytes 262176 | tf_op jit(solution)/shard_map/ppermute | solution.py:531
  16.4 5.3 %shard_map.104 = (bf16[512,512]{1,0:T(8,128)(2,1)S(1)}, bf16[512,512]{1,0:T(8,128)(2,1)S(1)}, bf16[16,256,512]{2,1,0:T(8,128)(2,1)S(1)}, bf16[256,512]{1,0:T(8,1...) custom-call(bf16[256,512]{1,0:T(8,128)(2,1)S(1)} %bitcast.18, ...), custom_call_target="tpu_custom_call", output_to_operand_aliasing={{6}: (15, {}), {7}: (16, {})} | custom-call | flops 8589934592 | bytes 8388608 | tf_op jit(solution)/shard_map/pallas_call | solution.py:615
  21.7 1.2 %collective-permute-start.10 = (bf16[264,128]{1,0:T(8,128)(2,1)S(1)}, bf16[264,128]{1,0:T(8,128)(2,1)S(1)}, u32[]{:S(2)}, u32[]{:S(2)}) collective-permute-start(bf16[264,128]{1,0:T(8,128)(2,1)S(1)} %get-tuple-element.81), channel_id=1, source_target_pairs={{0,5},{1,4},{2,7},{3,6},{4,1},{5,0},{6,3},{7,2},{8,13},{9,12},{10,... | collective-permute-start | bytes 202760 | tf_op jit(solution)/shard_map/ppermute | solution.py:531
  22.8 2.8 %collective-permute-start.11 = (bf16[264,128]{1,0:T(8,128)(2,1)S(1)}, bf16[264,128]{1,0:T(8,128)(2,1)S(1)}, u32[]{:S(2)}, u32[]{:S(2)}) collective-permute-start(bf16[264,128]{1,0:T(8,128)(2,1)S(1)} %get-tuple-element.82), channel_id=1, source_target_pairs={{0,6},{1,7},{2,4},{3,5},{4,2},{5,3},{6,0},{7,1},{8,14},{9,15},{10,... | collective-permute-start | bytes 202760 | tf_op jit(solution)/shard_map/ppermute | solution.py:531
  25.6 2.2 %collective-permute-start.12 = (bf16[264,128]{1,0:T(8,128)(2,1)S(1)}, bf16[264,128]{1,0:T(8,128)(2,1)S(1)}, u32[]{:S(2)}, u32[]{:S(2)}) collective-permute-start(bf16[264,128]{1,0:T(8,128)(2,1)S(1)} %get-tuple-element.83), channel_id=1, source_target_pairs={{0,7},{1,6},{2,5},{3,4},{4,3},{5,2},{6,1},{7,0},{8,15},{9,14},{10,... | collective-permute-start | bytes 202760 | tf_op jit(solution)/shard_map/ppermute | solution.py:531
  27.8 2.8 %collective-permute-start.8 = (bf16[264,128]{1,0:T(8,128)(2,1)S(1)}, bf16[264,128]{1,0:T(8,128)(2,1)S(1)}, u32[]{:S(2)}, u32[]{:S(2)}) collective-permute-start(bf16[264,128]{1,0:T(8,128)(2,1)S(1)} %get-tuple-element.79), channel_id=1, source_target_pairs={{0,3},{1,2},{2,1},{3,0},{4,7},{5,6},{6,5},{7,4},{8,11},{9,10},{10,... | collective-permute-start | bytes 202760 | tf_op jit(solution)/shard_map/ppermute | solution.py:531
  30.6 3.6 %collective-permute-start.9 = (bf16[264,128]{1,0:T(8,128)(2,1)S(1)}, bf16[264,128]{1,0:T(8,128)(2,1)S(1)}, u32[]{:S(2)}, u32[]{:S(2)}) collective-permute-start(bf16[264,128]{1,0:T(8,128)(2,1)S(1)} %get-tuple-element.80), channel_id=1, source_target_pairs={{0,4},{1,5},{2,6},{3,7},{4,0},{5,1},{6,2},{7,3},{8,12},{9,13},{10,... | collective-permute-start | bytes 202760 | tf_op jit(solution)/shard_map/ppermute | solution.py:531
  34.8 3.5 %collective-permute-done.9.refs_10_ = bf16[264,128]{1,0:T(8,128)(2,1)S(1)} collective-permute-done((bf16[264,128]{1,0:T(8,128)(2,1)S(1)}, bf16[264,128]{1,0:T(8,128)(2,1)S(1)}, u32[]{:S(2)}, u32[]{:S(2)}) %collective-permute-start.9) | collective-permute-done | bytes 67616 | tf_op jit(solution)/shard_map/ppermute | solution.py:531
  38.4 6.8 %shard_map.106 = (bf16[64,512]{1,0:T(8,128)(2,1)S(1)}, bf16[64,512]{1,0:T(8,128)(2,1)S(1)}, bf16[64,512]{1,0:T(8,128)(2,1)S(1)}, bf16[64,512]{1,0:T(8,128)(2,1)S...) custom-call(f32[1,512]{1,0:T(1,128)S(1)} %get-tuple-element.58.refs_, ...), custom_call_target="tpu_custom_call" | custom-call | flops 8589934592 | bytes 4194304 | tf_op jit(solution)/shard_map/pallas_call | solution.py:665
  45.7 2.0 %collective-permute-start.3 = (f32[16,256]{1,0:T(8,128)S(1)}, f32[16,256]{1,0:T(8,128)S(1)}, u32[]{:S(2)}, u32[]{:S(2)}) collective-permute-start(f32[16,256]{1,0:T(8,128)S(1)} %get-tuple-element.68.refs_2_), channel_id=1, source_target_pairs={{0,16},{8,24},{16,0},{24,8},{1,17},{9,25},{17,1},{25,9},{2,18},{10... | collective-permute-start | bytes 49160 | tf_op jit(solution)/shard_map/ppermute | solution.py:531
  47.7 1.5 %collective-permute-start.4 = (f32[16,256]{1,0:T(8,128)S(1)}, f32[16,256]{1,0:T(8,128)S(1)}, u32[]{:S(2)}, u32[]{:S(2)}) collective-permute-start(f32[16,256]{1,0:T(8,128)S(1)} %get-tuple-element.68.refs_2_), channel_id=1, source_target_pairs={{0,8},{8,0},{16,24},{24,16},{1,9},{9,1},{17,25},{25,17},{2,10},{10... | collective-permute-start | bytes 49160 | tf_op jit(solution)/shard_map/ppermute | solution.py:531
  49.2 0.7 shard_map.102.refs_1_.refs_2_
  50.6 1.0 %collective-permute-done.4.refs_4_ = f32[16,256]{1,0:T(8,128)S(1)} collective-permute-done((f32[16,256]{1,0:T(8,128)S(1)}, f32[16,256]{1,0:T(8,128)S(1)}, u32[]{:S(2)}, u32[]{:S(2)}) %collective-permute-start.4) | collective-permute-done | bytes 16416 | tf_op jit(solution)/shard_map/ppermute | solution.py:531
  51.5 0.8 collective-permute-start.16
  52.3 1.5 %collective-permute-done.5.refs_5_ = f32[16,256]{1,0:T(8,128)S(1)} collective-permute-done((f32[16,256]{1,0:T(8,128)S(1)}, f32[16,256]{1,0:T(8,128)S(1)}, u32[]{:S(2)}, u32[]{:S(2)}) %collective-permute-start.5) | collective-permute-done | bytes 16416 | tf_op jit(solution)/shard_map/ppermute | solution.py:531
  54.1 2.1 %collective-permute-start.18 = (bf16[64,512]{1,0:T(8,128)(2,1)S(1)}, bf16[64,512]{1,0:T(8,128)(2,1)S(1)}, u32[]{:S(2)}, u32[]{:S(2)}) collective-permute-start(bf16[64,512]{1,0:T(8,128)(2,1)S(1)} %get-tuple-element.90), channel_id=1, source_target_pairs={{0,6},{1,7},{2,4},{3,5},{4,2},{5,3},{6,0},{7,1},{8,14},{9,15},{10,... | collective-permute-start | bytes 196616 | tf_op jit(solution)/shard_map/ppermute | solution.py:531
  56.1 1.9 %collective-permute-start.19 = (bf16[64,512]{1,0:T(8,128)(2,1)S(1)}, bf16[64,512]{1,0:T(8,128)(2,1)S(1)}, u32[]{:S(2)}, u32[]{:S(2)}) collective-permute-start(bf16[64,512]{1,0:T(8,128)(2,1)S(1)} %get-tuple-element.91), channel_id=1, source_target_pairs={{0,7},{1,6},{2,5},{3,4},{4,3},{5,2},{6,1},{7,0},{8,15},{9,14},{10,... | collective-permute-start | bytes 196616 | tf_op jit(solution)/shard_map/ppermute | solution.py:531
  58.0 2.9 %shard_map.105.refs_10_.refs_0_ = bf16[16,256,1024]{2,1,0:T(8,128)(2,1)S(1)} custom-call(bf16[256,512]{1,0:T(8,128)(2,1)S(1)} %get-tuple-element.55.refs_9_.refs_0_.refs_3_, bf16[1024,512]{1,0:T(8,128)(2,1)S(1)} %shard_map.102.refs_1_.refs_2_, f32[16,256]{1,0:T(8,128)S(1)} %get-tuple-element.68.refs_2_, f32[16,256]{1,0:T(8,128)S(1)} %collective-permute-done.3.refs_3_, ...), custom_call_target="tpu_custom_call" | custom-call | flops 4294967296 | bytes 10485760 | tf_op jit(solution)/shard_map/pallas_call | solution.py:658
  60.9 2.5 %collective-permute-done.17.refs_8_ = bf16[64,512]{1,0:T(8,128)(2,1)S(1)} collective-permute-done((bf16[64,512]{1,0:T(8,128)(2,1)S(1)}, bf16[64,512]{1,0:T(8,128)(2,1)S(1)}, u32[]{:S(2)}, u32[]{:S(2)}) %collective-permute-start.17) | collective-permute-done | bytes 65568 | tf_op jit(solution)/shard_map/ppermute | solution.py:531
  63.5 1.0 %shard_map.107 = (bf16[256,512]{1,0:T(8,128)(2,1)S(1)}, bf16[272,512]{1,0:T(8,128)(2,1)S(1)}) custom-call(s32[1,256]{1,0:T(1,128)S(1)} %get-tuple-element.57.refs_4_.refs_0_, bf16[256,512]{1,0:T(8,128)(2,1)S(1)} %get-tuple-element.75.refs_1_, bf16[512,512]{1,0:T(8,128)(2,1)S(1)} %copy-done.6, bf16[64,512]{1,0:T(8,128)(2,1)S(1)} %get-tuple-element.84.refs_3_, ...), custom_call_target="tpu_custom_call" | custom-call | flops 536870912 | bytes 2097152 | tf_op jit(solution)/shard_map/pallas_call | solution.py:687
  65.2 1.5 %collective-permute-start.21 = (bf16[272,512]{1,0:T(8,128)(2,1)S(1)}, bf16[272,512]{1,0:T(8,128)(2,1)S(1)}, u32[]{:S(2)}, u32[]{:S(2)}) collective-permute-start(bf16[272,512]{1,0:T(8,128)(2,1)S(1)} %get-tuple-element.92.refs_11_), channel_id=1, source_target_pairs={{0,8},{8,0},{16,24},{24,16},{1,9},{9,1},{17,25},{25,17},{2,10},{10... | collective-permute-start | bytes 835592 | tf_op jit(solution)/shard_map/ppermute | solution.py:531
  66.7 1.3 %collective-permute-start.22 = (bf16[272,512]{1,0:T(8,128)(2,1)S(1)}, bf16[272,512]{1,0:T(8,128)(2,1)S(1)}, u32[]{:S(2)}, u32[]{:S(2)}) collective-permute-start(bf16[272,512]{1,0:T(8,128)(2,1)S(1)} %get-tuple-element.92.refs_11_), channel_id=1, source_target_pairs={{0,24},{8,16},{16,8},{24,0},{1,25},{9,17},{17,9},{25,1},{2,26},{10... | collective-permute-start | bytes 835592 | tf_op jit(solution)/shard_map/ppermute | solution.py:531
  68.0 7.6 %shard_map.108 = (bf16[256,512]{1,0:T(8,128)(2,1)S(1)}, f32[256,512]{1,0:T(8,128)S(1)}, f32[256,512]{1,0:T(8,128)S(1)}) custom-call(bf16[16,256,256]{2,1,0:T(8,128)(2,1)S(1)} %get-tuple-element.69.refs_0_, bf16[16,256,256]{2,1,0:T(8,128)(2,1)S(1)} %get-tuple-element.70.refs_1_, bf16[16,256,512]{2,1,0:T(8,128)(2,1)S(1)} %get-tuple-element.71.refs_2_, ...), custom_call_target="tpu_custom_call" | custom-call | flops 8589934592 | bytes 10485760 | tf_op jit(solution)/shard_map/pallas_call | solution.py:695
  75.6 2.8 %shard_map.109 = (f32[256,512]{1,0:T(8,128)S(1)}, f32[256,512]{1,0:T(8,128)S(1)}) custom-call(bf16[16,256,1024]{2,1,0:T(8,128)(2,1)S(1)} %shard_map.105.refs_10_.refs_0_, bf16[256,512]{1,0:T(8,128)(2,1)S(1)} %get-tuple-element.64.refs_11_.refs_6_.refs_1_, bf16[1024,512]{1,0:T(8,128)(2,1)S(1)} %shard_map.102.refs_1_.refs_2_, ...), custom_call_target="tpu_custom_call" | custom-call | flops 2147483648 | bytes 4194304 | tf_op jit(solution)/shard_map/pallas_call | solution.py:703
  78.4 1.9 %collective-permute-done.22.refs_11_ = bf16[272,512]{1,0:T(8,128)(2,1)S(1)} collective-permute-done((bf16[272,512]{1,0:T(8,128)(2,1)S(1)}, bf16[272,512]{1,0:T(8,128)(2,1)S(1)}, u32[]{:S(2)}, u32[]{:S(2)}) %collective-permute-start.22) | collective-permute-done | bytes 278560 | tf_op jit(solution)/shard_map/ppermute | solution.py:531
  80.3 5.6 %shard_map.110 = bf16[256,512]{1,0:T(8,128)(2,1)} custom-call(bf16[16,256,1024]{2,1,0:T(8,128)(2,1)S(1)} %shard_map.105.refs_10_.refs_0_, bf16[256,512]{1,0:T(8,128)(2,1)S(1)} %get-tuple-element.64.refs_11_.refs_6_.refs_1_, bf16[1024,512]{1,0:T(8,128)(2,1)S(1)} %shard_map.102.refs_1_.refs_2_, bf16[256,512]{1,0:T(8,128)(2,1)S(1)} %get-tuple-element.93.refs_3_, ...), custom_call_target="tpu_custom_call" | custom-call | flops 8589934592 | bytes 14680064 | tf_op jit(solution)/shard_map/pallas_call | solution.py:710
  (51 shorter events, 4.7 us)
Async XLA Ops:
  0.0 11.5 %collective-permute-start = (bf16[256,512]{1,0:T(8,128)(2,1)}, bf16[256,512]{1,0:T(8,128)(2,1)S(1)}, u32[]{:S(2)}, u32[]{:S(2)}) collective-permute-start(bf16[256,512]{1,0:T(8,128)(2,1)} %bitcast.14), channel_id=1, source_target_pairs={{0,16},{8,24},{16,0},{24,8},{1,17},{9,25},{17,1},{25,9},{2,18},{10... | collective-permute-start | bytes 786440 | tf_op jit(solution)/shard_map/ppermute | solution.py:531
  3.0 11.3 %collective-permute-start.1 = (bf16[256,512]{1,0:T(8,128)(2,1)}, bf16[256,512]{1,0:T(8,128)(2,1)S(1)}, u32[]{:S(2)}, u32[]{:S(2)}) collective-permute-start(bf16[256,512]{1,0:T(8,128)(2,1)} %bitcast.15), channel_id=1, source_target_pairs={{0,8},{8,0},{16,24},{24,16},{1,9},{9,1},{17,25},{25,17},{2,10},{10... | collective-permute-start | bytes 786440 | tf_op jit(solution)/shard_map/ppermute | solution.py:531
  4.5 11.8 %collective-permute-start.2 = (bf16[256,512]{1,0:T(8,128)(2,1)}, bf16[256,512]{1,0:T(8,128)(2,1)S(1)}, u32[]{:S(2)}, u32[]{:S(2)}) collective-permute-start(bf16[256,512]{1,0:T(8,128)(2,1)} %bitcast.16), channel_id=1, source_target_pairs={{0,24},{8,16},{16,8},{24,0},{1,25},{9,17},{17,9},{25,1},{2,26},{10... | collective-permute-start | bytes 786440 | tf_op jit(solution)/shard_map/ppermute | solution.py:531
  8.6 2.9 %copy-start.1 = (bf16[512,1536]{1,0:T(8,128)(2,1)S(1)}, bf16[512,1536]{1,0:T(8,128)(2,1)}, u32[]{:S(2)}) copy-start(bf16[512,1536]{1,0:T(8,128)(2,1)} %refs_8_.1) | copy-start | bytes 4718596
  11.5 4.8 %copy-start.6 = (bf16[512,512]{1,0:T(8,128)(2,1)S(1)}, bf16[512,512]{1,0:T(8,128)(2,1)}, u32[]{:S(2)}) copy-start(bf16[512,512]{1,0:T(8,128)(2,1)} %refs_2_.7) | copy-start | bytes 1572868
  16.3 22.0 %copy-start.4 = (bf16[512,1536]{1,0:T(8,128)(2,1)S(1)}, bf16[512,1536]{1,0:T(8,128)(2,1)}, u32[]{:S(2)}) copy-start(bf16[512,1536]{1,0:T(8,128)(2,1)} %refs_3_.3) | copy-start | bytes 4718596
  16.3 22.0 %copy-start.5 = (bf16[512,512]{1,0:T(8,128)(2,1)S(1)}, bf16[512,512]{1,0:T(8,128)(2,1)}, u32[]{:S(2)}) copy-start(bf16[512,512]{1,0:T(8,128)(2,1)} %refs_4_.1) | copy-start | bytes 1572868
  16.3 22.0 %copy-start.7 = (bf16[1,1,256,512]{3,2,1,0:T(8,128)(2,1)S(1)}, bf16[1,1,256,512]{3,2,1,0:T(8,128)(2,1)}, u32[]{:S(2)}) copy-start(bf16[1,1,256,512]{3,2,1,0:T(8,128)(2,1)} %param.19) | copy-start | bytes 786436
  16.3 22.0 %copy-start.10 = (f32[512]{0:T(512)S(1)}, f32[512]{0:T(512)}, u32[]{:S(2)}) copy-start(f32[512]{0:T(512)} %param.15) | copy-start | bytes 6148
  16.3 22.0 %copy-start.12 = (s32[1,1,256]{2,1,0:T(1,128)S(1)}, s32[1,1,256]{2,1,0:T(1,128)}, u32[]{:S(2)}) copy-start(s32[1,1,256]{2,1,0:T(1,128)} %param.18) | copy-start | bytes 3076
  21.7 6.1 %collective-permute-start.10 = (bf16[264,128]{1,0:T(8,128)(2,1)S(1)}, bf16[264,128]{1,0:T(8,128)(2,1)S(1)}, u32[]{:S(2)}, u32[]{:S(2)}) collective-permute-start(bf16[264,128]{1,0:T(8,128)(2,1)S(1)} %get-tuple-element.81), channel_id=1, source_target_pairs={{0,5},{1,4},{2,7},{3,6},{4,1},{5,0},{6,3},{7,2},{8,13},{9,12},{10,... | collective-permute-start | bytes 202760 | tf_op jit(solution)/shard_map/ppermute | solution.py:531
  22.8 7.7 %collective-permute-start.11 = (bf16[264,128]{1,0:T(8,128)(2,1)S(1)}, bf16[264,128]{1,0:T(8,128)(2,1)S(1)}, u32[]{:S(2)}, u32[]{:S(2)}) collective-permute-start(bf16[264,128]{1,0:T(8,128)(2,1)S(1)} %get-tuple-element.82), channel_id=1, source_target_pairs={{0,6},{1,7},{2,4},{3,5},{4,2},{5,3},{6,0},{7,1},{8,14},{9,15},{10,... | collective-permute-start | bytes 202760 | tf_op jit(solution)/shard_map/ppermute | solution.py:531
  25.6 8.5 %collective-permute-start.12 = (bf16[264,128]{1,0:T(8,128)(2,1)S(1)}, bf16[264,128]{1,0:T(8,128)(2,1)S(1)}, u32[]{:S(2)}, u32[]{:S(2)}) collective-permute-start(bf16[264,128]{1,0:T(8,128)(2,1)S(1)} %get-tuple-element.83), channel_id=1, source_target_pairs={{0,7},{1,6},{2,5},{3,4},{4,3},{5,2},{6,1},{7,0},{8,15},{9,14},{10,... | collective-permute-start | bytes 202760 | tf_op jit(solution)/shard_map/ppermute | solution.py:531
  27.8 6.3 %collective-permute-start.6 = (bf16[264,128]{1,0:T(8,128)(2,1)S(1)}, bf16[264,128]{1,0:T(8,128)(2,1)S(1)}, u32[]{:S(2)}, u32[]{:S(2)}) collective-permute-start(bf16[264,128]{1,0:T(8,128)(2,1)S(1)} %get-tuple-element.77), channel_id=1, source_target_pairs={{0,1},{1,0},{2,3},{3,2},{4,5},{5,4},{6,7},{7,6},{8,9},{9,8},{10,11... | collective-permute-start | bytes 202760 | tf_op jit(solution)/shard_map/ppermute | solution.py:531
  27.8 6.3 %collective-permute-start.7 = (bf16[264,128]{1,0:T(8,128)(2,1)S(1)}, bf16[264,128]{1,0:T(8,128)(2,1)S(1)}, u32[]{:S(2)}, u32[]{:S(2)}) collective-permute-start(bf16[264,128]{1,0:T(8,128)(2,1)S(1)} %get-tuple-element.78), channel_id=1, source_target_pairs={{0,2},{1,3},{2,0},{3,1},{4,6},{5,7},{6,4},{7,5},{8,10},{9,11},{10,... | collective-permute-start | bytes 202760 | tf_op jit(solution)/shard_map/ppermute | solution.py:531
  27.8 7.0 %collective-permute-start.8 = (bf16[264,128]{1,0:T(8,128)(2,1)S(1)}, bf16[264,128]{1,0:T(8,128)(2,1)S(1)}, u32[]{:S(2)}, u32[]{:S(2)}) collective-permute-start(bf16[264,128]{1,0:T(8,128)(2,1)S(1)} %get-tuple-element.79), channel_id=1, source_target_pairs={{0,3},{1,2},{2,1},{3,0},{4,7},{5,6},{6,5},{7,4},{8,11},{9,10},{10,... | collective-permute-start | bytes 202760 | tf_op jit(solution)/shard_map/ppermute | solution.py:531
  30.6 7.8 %collective-permute-start.9 = (bf16[264,128]{1,0:T(8,128)(2,1)S(1)}, bf16[264,128]{1,0:T(8,128)(2,1)S(1)}, u32[]{:S(2)}, u32[]{:S(2)}) collective-permute-start(bf16[264,128]{1,0:T(8,128)(2,1)S(1)} %get-tuple-element.80), channel_id=1, source_target_pairs={{0,4},{1,5},{2,6},{3,7},{4,0},{5,1},{6,2},{7,3},{8,12},{9,13},{10,... | collective-permute-start | bytes 202760 | tf_op jit(solution)/shard_map/ppermute | solution.py:531
  38.4 10.8 %copy-start.3 = (f32[512]{0:T(512)S(1)}, f32[512]{0:T(512)}, u32[]{:S(2)}) copy-start(f32[512]{0:T(512)} %param.11) | copy-start | bytes 6148
  45.2 8.9 %collective-permute-start.13 = (bf16[64,512]{1,0:T(8,128)(2,1)S(1)}, bf16[64,512]{1,0:T(8,128)(2,1)S(1)}, u32[]{:S(2)}, u32[]{:S(2)}) collective-permute-start(bf16[64,512]{1,0:T(8,128)(2,1)S(1)} %get-tuple-element.85), channel_id=1, source_target_pairs={{0,1},{1,0},{2,3},{3,2},{4,5},{5,4},{6,7},{7,6},{8,9},{9,8},{10,11... | collective-permute-start | bytes 196616 | tf_op jit(solution)/shard_map/ppermute | solution.py:531
  45.4 10.7 %collective-permute-start.14 = (bf16[64,512]{1,0:T(8,128)(2,1)S(1)}, bf16[64,512]{1,0:T(8,128)(2,1)S(1)}, u32[]{:S(2)}, u32[]{:S(2)}) collective-permute-start(bf16[64,512]{1,0:T(8,128)(2,1)S(1)} %get-tuple-element.86), channel_id=1, source_target_pairs={{0,2},{1,3},{2,0},{3,1},{4,6},{5,7},{6,4},{7,5},{8,10},{9,11},{10,... | collective-permute-start | bytes 196616 | tf_op jit(solution)/shard_map/ppermute | solution.py:531
  45.7 4.2 %collective-permute-start.3 = (f32[16,256]{1,0:T(8,128)S(1)}, f32[16,256]{1,0:T(8,128)S(1)}, u32[]{:S(2)}, u32[]{:S(2)}) collective-permute-start(f32[16,256]{1,0:T(8,128)S(1)} %get-tuple-element.68.refs_2_), channel_id=1, source_target_pairs={{0,16},{8,24},{16,0},{24,8},{1,17},{9,25},{17,1},{25,9},{2,18},{10... | collective-permute-start | bytes 49160 | tf_op jit(solution)/shard_map/ppermute | solution.py:531
  47.7 3.8 %collective-permute-start.4 = (f32[16,256]{1,0:T(8,128)S(1)}, f32[16,256]{1,0:T(8,128)S(1)}, u32[]{:S(2)}, u32[]{:S(2)}) collective-permute-start(f32[16,256]{1,0:T(8,128)S(1)} %get-tuple-element.68.refs_2_), channel_id=1, source_target_pairs={{0,8},{8,0},{16,24},{24,16},{1,9},{9,1},{17,25},{25,17},{2,10},{10... | collective-permute-start | bytes 49160 | tf_op jit(solution)/shard_map/ppermute | solution.py:531
  49.2 4.6 %collective-permute-start.5 = (f32[16,256]{1,0:T(8,128)S(1)}, f32[16,256]{1,0:T(8,128)S(1)}, u32[]{:S(2)}, u32[]{:S(2)}) collective-permute-start(f32[16,256]{1,0:T(8,128)S(1)} %get-tuple-element.68.refs_2_), channel_id=1, source_target_pairs={{0,24},{8,16},{16,8},{24,0},{1,25},{9,17},{17,9},{25,1},{2,26},{10... | collective-permute-start | bytes 49160 | tf_op jit(solution)/shard_map/ppermute | solution.py:531
  49.9 11.0 %collective-permute-start.15 = (bf16[64,512]{1,0:T(8,128)(2,1)S(1)}, bf16[64,512]{1,0:T(8,128)(2,1)S(1)}, u32[]{:S(2)}, u32[]{:S(2)}) collective-permute-start(bf16[64,512]{1,0:T(8,128)(2,1)S(1)} %get-tuple-element.87), channel_id=1, source_target_pairs={{0,3},{1,2},{2,1},{3,0},{4,7},{5,6},{6,5},{7,4},{8,11},{9,10},{10,... | collective-permute-start | bytes 196616 | tf_op jit(solution)/shard_map/ppermute | solution.py:531
  51.5 9.4 %collective-permute-start.16 = (bf16[64,512]{1,0:T(8,128)(2,1)S(1)}, bf16[64,512]{1,0:T(8,128)(2,1)S(1)}, u32[]{:S(2)}, u32[]{:S(2)}) collective-permute-start(bf16[64,512]{1,0:T(8,128)(2,1)S(1)} %get-tuple-element.88), channel_id=1, source_target_pairs={{0,4},{1,5},{2,6},{3,7},{4,0},{5,1},{6,2},{7,3},{8,12},{9,13},{10,... | collective-permute-start | bytes 196616 | tf_op jit(solution)/shard_map/ppermute | solution.py:531
  53.8 9.7 %collective-permute-start.17 = (bf16[64,512]{1,0:T(8,128)(2,1)S(1)}, bf16[64,512]{1,0:T(8,128)(2,1)S(1)}, u32[]{:S(2)}, u32[]{:S(2)}) collective-permute-start(bf16[64,512]{1,0:T(8,128)(2,1)S(1)} %get-tuple-element.89), channel_id=1, source_target_pairs={{0,5},{1,4},{2,7},{3,6},{4,1},{5,0},{6,3},{7,2},{8,13},{9,12},{10,... | collective-permute-start | bytes 196616 | tf_op jit(solution)/shard_map/ppermute | solution.py:531
  54.1 9.4 %collective-permute-start.18 = (bf16[64,512]{1,0:T(8,128)(2,1)S(1)}, bf16[64,512]{1,0:T(8,128)(2,1)S(1)}, u32[]{:S(2)}, u32[]{:S(2)}) collective-permute-start(bf16[64,512]{1,0:T(8,128)(2,1)S(1)} %get-tuple-element.90), channel_id=1, source_target_pairs={{0,6},{1,7},{2,4},{3,5},{4,2},{5,3},{6,0},{7,1},{8,14},{9,15},{10,... | collective-permute-start | bytes 196616 | tf_op jit(solution)/shard_map/ppermute | solution.py:531
  56.1 7.3 %collective-permute-start.19 = (bf16[64,512]{1,0:T(8,128)(2,1)S(1)}, bf16[64,512]{1,0:T(8,128)(2,1)S(1)}, u32[]{:S(2)}, u32[]{:S(2)}) collective-permute-start(bf16[64,512]{1,0:T(8,128)(2,1)S(1)} %get-tuple-element.91), channel_id=1, source_target_pairs={{0,7},{1,6},{2,5},{3,4},{4,3},{5,2},{6,1},{7,0},{8,15},{9,14},{10,... | collective-permute-start | bytes 196616 | tf_op jit(solution)/shard_map/ppermute | solution.py:531
  64.5 11.1 %collective-permute-start.20 = (bf16[272,512]{1,0:T(8,128)(2,1)S(1)}, bf16[272,512]{1,0:T(8,128)(2,1)S(1)}, u32[]{:S(2)}, u32[]{:S(2)}) collective-permute-start(bf16[272,512]{1,0:T(8,128)(2,1)S(1)} %get-tuple-element.92.refs_11_), channel_id=1, source_target_pairs={{0,16},{8,24},{16,0},{24,8},{1,17},{9,25},{17,1},{25,9},{2,18},{10... | collective-permute-start | bytes 835592 | tf_op jit(solution)/shard_map/ppermute | solution.py:531
  65.2 13.2 %collective-permute-start.21 = (bf16[272,512]{1,0:T(8,128)(2,1)S(1)}, bf16[272,512]{1,0:T(8,128)(2,1)S(1)}, u32[]{:S(2)}, u32[]{:S(2)}) collective-permute-start(bf16[272,512]{1,0:T(8,128)(2,1)S(1)} %get-tuple-element.92.refs_11_), channel_id=1, source_target_pairs={{0,8},{8,0},{16,24},{24,16},{1,9},{9,1},{17,25},{25,17},{2,10},{10... | collective-permute-start | bytes 835592 | tf_op jit(solution)/shard_map/ppermute | solution.py:531
  66.7 13.6 %collective-permute-start.22 = (bf16[272,512]{1,0:T(8,128)(2,1)S(1)}, bf16[272,512]{1,0:T(8,128)(2,1)S(1)}, u32[]{:S(2)}, u32[]{:S(2)}) collective-permute-start(bf16[272,512]{1,0:T(8,128)(2,1)S(1)} %get-tuple-element.92.refs_11_), channel_id=1, source_target_pairs={{0,24},{8,16},{16,8},{24,0},{1,25},{9,17},{17,9},{25,1},{2,26},{10... | collective-permute-start | bytes 835592 | tf_op jit(solution)/shard_map/ppermute | solution.py:531
  75.6 4.8 %copy-start.9 = (bf16[1,1,256,512]{3,2,1,0:T(8,128)(2,1)S(1)}, bf16[1,1,256,512]{3,2,1,0:T(8,128)(2,1)}, u32[]{:S(2)}) copy-start(bf16[1,1,256,512]{3,2,1,0:T(8,128)(2,1)} %param.10) | copy-start | bytes 786436
  (4 other events, 3.7 us)
where the time goes:
time: 86.5 us; the launch traced here: 86 us
  Pallas kernels  38.6 us (45%)
  starting transfers between devices  30.1 us (35%)
  waiting for transfers between devices  13.2 us (15%)
  local copies, waits for them, and re-layouts  3.76 us (4%)
    ppermute x23, starting transfers between devices, by_xor(): return lax.ppermute(array, axis, [(i, i ^ step) for i in range(size)])  30.1 us
    ppermute x23, waiting for transfers between devices, by_xor(): return lax.ppermute(array, axis, [(i, i ^ step) for i in range(size)])  13.2 us
    pallas_call x1, Pallas kernels, shards(): vmem_call(functools.partial(query_grad_body, len(all_keys), depth), (rows...  7.57 us
    pallas_call x1, Pallas kernels, shards(): vmem_call(functools.partial(second_body, chunks, depth), (chunk_bf16,) *...  6.79 us
    pallas_call x1, Pallas kernels, shards(): vmem_call(functools.partial(key_grad_body, early, peers, depth), rows_bf1...  5.6 us
    pallas_call x1, Pallas kernels, shards(): vmem_call(functools.partial(forward_body, early, peers, chunks, capacity,...  5.31 us
    unnamed x26, local copies, waits for them, and re-layouts  3.76 us
    pallas_call x1, Pallas kernels, shards(): vmem_call(functools.partial(weights_flipped_body, peers, depth), shape(BF...  2.89 us
  transfers between devices with their start and end apart: 23, of which 7 were waited for; matrix products, arithmetic and copies ran while one was open for 0% of the time, Pallas kernels for 23%

commit v1 on v0

--- a/solution.py
+++ b/solution.py
@@ -55,7 +55,15 @@
 
 
 def tile_at(t):
+    if isinstance(t, int):
+        return slice(t * LANES, (t + 1) * LANES)
     return pl.ds(pl.multiple_of(t * LANES, LANES), LANES)
+
+
+def tile_loop(tiles, step, carry):
+    for t in range(tiles):
+        carry = step(t, carry)
+    return carry
 
 
 def vmem_call(body, outs, scratch=(), flops=0, moved=0, **more):
@@ -149,7 +157,7 @@
         )
         return carry
 
-    lax.fori_loop(0, width // LANES, tile_step, 0)
+    tile_loop(width // LANES, tile_step, 0)
 
 
 def middle_body(depth, *refs):
@@ -167,7 +175,7 @@
         sums_ref[:, at] = sums + sums_in_ref[:, at]
         return carry
 
-    lax.fori_loop(0, width // LANES, tile_step, 0)
+    tile_loop(width // LANES, tile_step, 0)
 
 
 def forward_body(early, peers, chunks, capacity, depth, *refs):
@@ -204,7 +212,7 @@
         finish_tile(t, at, mixed, sums, 0.0)
         return jnp.where((sums >= LOW) & (sums <= HIGH), bad, 1.0)
 
-    bad = lax.fori_loop(0, width // LANES, fast_step, jnp.zeros((count, LANES), F32))
+    bad = tile_loop(width // LANES, fast_step, jnp.zeros((count, LANES), F32))
 
     @pl.when(jnp.max(bad) > 0.0)
     def _():
@@ -319,7 +327,7 @@
         packed_grad[:, v_at] = dv.astype(BF16)
         return carry
 
-    lax.fori_loop(0, width // LANES, tile_step, 0)
+    tile_loop(width // LANES, tile_step, 0)
     normed_grad = dot_nt(packed_grad[...], w_ref[...]).astype(BF16)
     total = grad_ref[...].astype(F32) + norm_pull(hilbert, gain_ref[...], normed_grad).astype(F32)
     back = lax.broadcasted_iota(jnp.int32, (slots, count), 1).astype(F32) == column(landing)
@@ -366,7 +374,7 @@
             out_ref[h] = jnp.exp2(scores * scale - line).astype(BF16)
         return carry
 
-    lax.fori_loop(0, k_ref.shape[1] // LANES, tile_step, 0)
+    tile_loop(k_ref.shape[1] // LANES, tile_step, 0)
 
 
 def home_body(chunks, depth, *refs):
@@ -456,7 +464,7 @@
         )
         return carry
 
-    lax.fori_loop(0, width // LANES, tile_step, 0)
+    tile_loop(width // LANES, tile_step, 0)
 
 
 def key_middle_body(index, depth, *refs):
@@ -483,7 +491,7 @@
         dv_ref[:, at] = dv + dv_in_ref[:, at]
         return carry
 
-    lax.fori_loop(0, width // LANES, tile_step, 0)
+    tile_loop(width // LANES, tile_step, 0)
 
 
 def key_grad_body(early, peers, depth, *refs):
@@ -516,7 +524,7 @@
         packed_grad[:, tile_at(t + 2 * (width // LANES))] = (dv + dv_ref[:, at]).astype(BF16)
         return carry
 
-    lax.fori_loop(0, width // LANES, tile_step, 0)
+    tile_loop(width // LANES, tile_step, 0)
     normed_grad = dot_nt(packed_grad[...], w_ref[...]).astype(BF16)
     path = norm_pull(x_ref[...], gain_ref[...], normed_grad)
     out_ref[...] = (moved_ref[...].astype(F32) + path.astype(F32)).astype(BF16)
@@ -596,13 +604,13 @@
         moved=4 << 20,
     )(x_then, gain_one, qkv_one)
     early_keys, early_values, early_weights = [k], [v], [own_weights]
-    if peers > 1:
+    for other in others[: peers - 1]:
         k_next, v_next, weights_next, sum_mixed, sums = vmem_call(
             functools.partial(middle_body, depth),
             (rows_bf16,) * 2 + (square,) + (rows_f32,) * 2,
             flops=2 << 30,
             moved=4 << 20,
-        )(others[0], gain_one, qkv_one, q, sum_mixed, sums)
+        )(other, gain_one, qkv_one, q, sum_mixed, sums)
         early_keys.append(k_next)
         early_values.append(v_next)
         early_weights.append(weights_next)

time: 86.5 us -> 81 us (0.936)
  Pallas kernels: 38.6 us -> 34.1 us
  waiting for transfers between devices: 13.2 us -> 12.3 us
    pallas_call x1, Pallas kernels: 5.31 us -> 2.83 us  [shards(): vmem_call(functools.partial(forward_body, early, peers, chunks, capacity,...]
    pallas_call x1, Pallas kernels: 5.6 us -> 3.61 us  [shards(): vmem_call(functools.partial(key_grad_body, early, peers, depth), rows_bf1...]
    pallas_call x1 -> x2, Pallas kernels: 2.78 us -> 4.56 us  [shards(): vmem_call(functools.partial(key_middle_body, index, depth), (rows_f32, ro...]
    pallas_call x1 -> x2, Pallas kernels: 2.72 us -> 3.68 us  [shards(): vmem_call(functools.partial(middle_body, depth), (rows_bf16,) * 2 + (squa...]
    pallas_call x1, Pallas kernels: 6.79 us -> 5.86 us  [shards(): vmem_call(functools.partial(second_body, chunks, depth), (chunk_bf16,) *...]
    ppermute x23, waiting for transfers between devices: 13.2 us -> 12.3 us  [by_xor(): return lax.ppermute(array, axis, [(i, i ^ step) for i in range(size)])]
    pallas_call x1, Pallas kernels: 2.87 us -> 1.98 us  [shards(): vmem_call(functools.partial(prep_body, depth), (rows_bf16,) * 3 + (square...]
  transfers between devices with their start and end apart: 23 -> 23, of which waited for: 7 -> 8; matrix products, arithmetic and copies ran while one was open for 0% -> 0% of each run, Pallas kernels for 23% -> 26%
where the time goes in v1:
time: 81 us; the launch traced here: 80.5 us
  Pallas kernels  34.1 us (42%)
  starting transfers between devices  30.1 us (37%)
  waiting for transfers between devices  12.3 us (15%)
  local copies, waits for them, and re-layouts  3.76 us (5%)
    ppermute x23, starting transfers between devices, by_xor(): return lax.ppermute(array, axis, [(i, i ^ step) for i in range(size)])  30.1 us
    ppermute x23, waiting for transfers between devices, by_xor(): return lax.ppermute(array, axis, [(i, i ^ step) for i in range(size)])  12.3 us
    pallas_call x1, Pallas kernels, shards(): vmem_call(functools.partial(query_grad_body, len(all_keys), depth), (rows...  7.15 us
    pallas_call x1, Pallas kernels, shards(): vmem_call(functools.partial(second_body, chunks, depth), (chunk_bf16,) *...  5.86 us
    pallas_call x2, Pallas kernels, shards(): vmem_call(functools.partial(key_middle_body, index, depth), (rows_f32, ro...  4.56 us
    unnamed x26, local copies, waits for them, and re-layouts  3.76 us
    pallas_call x2, Pallas kernels, shards(): vmem_call(functools.partial(middle_body, depth), (rows_bf16,) * 2 + (squa...  3.68 us
    pallas_call x1, Pallas kernels, shards(): vmem_call(functools.partial(key_grad_body, early, peers, depth), rows_bf1...  3.61 us
  transfers between devices with their start and end apart: 23, of which 8 were waited for; matrix products, arithmetic and copies ran while one was open for 0% of the time, Pallas kernels for 26%

profile of v1, /device:TPU:0, one launch (start us, length us, event | category | flops | bytes accessed | tf_op | source)
XLA Modules:
  0.0 80.5 jit_solution(15682039181434073475)
XLA Ops:
  0.0 3.0 %collective-permute-start = (bf16[256,512]{1,0:T(8,128)(2,1)}, bf16[256,512]{1,0:T(8,128)(2,1)S(1)}, u32[]{:S(2)}, u32[]{:S(2)}) collective-permute-start(bf16[256,512]{1,0:T(8,128)(2,1)} %bitcast.15), channel_id=1, source_target_pairs={{0,16},{8,24},{16,0},{24,8},{1,17},{9,25},{17,1},{25,9},{2,18},{10... | collective-permute-start | bytes 786440 | tf_op jit(solution)/shard_map/ppermute | solution.py:539
  3.0 1.5 %collective-permute-start.1 = (bf16[256,512]{1,0:T(8,128)(2,1)}, bf16[256,512]{1,0:T(8,128)(2,1)S(1)}, u32[]{:S(2)}, u32[]{:S(2)}) collective-permute-start(bf16[256,512]{1,0:T(8,128)(2,1)} %bitcast.16), channel_id=1, source_target_pairs={{0,8},{8,0},{16,24},{24,16},{1,9},{9,1},{17,25},{25,17},{2,10},{10... | collective-permute-start | bytes 786440 | tf_op jit(solution)/shard_map/ppermute | solution.py:539
  5.6 1.4 %copy-done = bf16[512,1536]{1,0:T(8,128)(2,1)S(1)} copy-done((bf16[512,1536]{1,0:T(8,128)(2,1)S(1)}, bf16[512,1536]{1,0:T(8,128)(2,1)}, u32[]{:S(2)}) %copy-start) | copy-done | bytes 1572888
  7.7 0.9 %copy-done.8 = bf16[1,1,256,512]{3,2,1,0:T(8,128)(2,1)S(1)} copy-done((bf16[1,1,256,512]{3,2,1,0:T(8,128)(2,1)S(1)}, bf16[1,1,256,512]{3,2,1,0:T(8,128)(2,1)}, u32[]{:S(2)}) %copy-start.8) | copy-done | bytes 262168
  8.6 2.0 %shard_map.101 = (bf16[256,512]{1,0:T(8,128)(2,1)S(1)}, bf16[256,512]{1,0:T(8,128)(2,1)S(1)}, bf16[256,512]{1,0:T(8,128)(2,1)S(1)}, bf16[16,256,256]{2,1,0:T(8,1...) custom-call(bf16[256,512]{1,0:T(8,128)(2,1)S(1)} %bitcast.18, f32[1,512]{1,0:T(1,128)S(1)} %bitcast.8, ...), custom_call_target="tpu_custom_call" | custom-call | flops 2147483648 | bytes 4194304 | tf_op jit(solution)/shard_map/pallas_call | solution.py:600
  10.6 1.8 %shard_map.103 = (bf16[256,512]{1,0:T(8,128)(2,1)S(1)}, bf16[256,512]{1,0:T(8,128)(2,1)S(1)}, bf16[16,256,256]{2,1,0:T(8,128)(2,1)S(1)}, f32[256,512]{1,0:T(8,128)S(1)}, f32[256,512]{1,0:T(8,128)S(1)}) custom-call(bf16[256,512]{1,0:T(8,128)(2,1)S(1)} %collective-permute-done.refs_3_.refs_0_, f32[1,512]{1,0:T(1,128)S(1)} %bitcast.9, ...), custom_call_target="tpu_custom_call" | custom-call | flops 2147483648 | bytes 4194304 | tf_op jit(solution)/shard_map/pallas_call | solution.py:608
  12.5 1.8 %shard_map.104 = (bf16[256,512]{1,0:T(8,128)(2,1)S(1)}, bf16[256,512]{1,0:T(8,128)(2,1)S(1)}, bf16[16,256,256]{2,1,0:T(8,128)(2,1)S(1)}, f32[256,512]{1,0:T(8,128)S(1)}, f32[256,512]{1,0:T(8,128)S(1)}) custom-call(bf16[256,512]{1,0:T(8,128)(2,1)S(1)} %collective-permute-done.1.refs_4_.refs_0_, f32[1,512]{1,0:T(1,128)S(1)} %bitcast.10, ...), custom_call_target="tpu_custom_call" | custom-call | flops 2147483648 | bytes 4194304 | tf_op jit(solution)/shard_map/pallas_call | solution.py:608
  14.3 2.0 %collective-permute-done.2.refs_5_.refs_15_ = bf16[256,512]{1,0:T(8,128)(2,1)S(1)} collective-permute-done((bf16[256,512]{1,0:T(8,128)(2,1)}, bf16[256,512]{1,0:T(8,128)(2,1)S(1)}, u32[]{:S(2)}, u32[]{:S(2)}) %collective-permute-start.2) | collective-permute-done | bytes 262176 | tf_op jit(solution)/shard_map/ppermute | solution.py:539
  16.4 2.8 %shard_map.105 = (bf16[256,512]{1,0:T(8,128)(2,1)S(1)}, bf16[256,512]{1,0:T(8,128)(2,1)S(1)}, bf16[16,256,256]{2,1,0:T(8,128)(2,1)S(1)}, bf16[256,512]{1,0:T(8,1...) custom-call(bf16[256,512]{1,0:T(8,128)(2,1)S(1)} %bitcast.19, ...), custom_call_target="tpu_custom_call", output_to_operand_aliasing={{6}: (16, {}), {7}: (17, {}), {8}: (18, {})} | custom-call | flops 8589934592 | bytes 8388608 | tf_op jit(solution)/shard_map/pallas_call | solution.py:623
  19.2 1.2 %collective-permute-start.10 = (bf16[264,128]{1,0:T(8,128)(2,1)S(1)}, bf16[264,128]{1,0:T(8,128)(2,1)S(1)}, u32[]{:S(2)}, u32[]{:S(2)}) collective-permute-start(bf16[264,128]{1,0:T(8,128)(2,1)S(1)} %get-tuple-element.95), channel_id=1, source_target_pairs={{0,5},{1,4},{2,7},{3,6},{4,1},{5,0},{6,3},{7,2},{8,13},{9,12},{10,... | collective-permute-start | bytes 202760 | tf_op jit(solution)/shard_map/ppermute | solution.py:539
  20.3 2.8 %collective-permute-start.11 = (bf16[264,128]{1,0:T(8,128)(2,1)S(1)}, bf16[264,128]{1,0:T(8,128)(2,1)S(1)}, u32[]{:S(2)}, u32[]{:S(2)}) collective-permute-start(bf16[264,128]{1,0:T(8,128)(2,1)S(1)} %get-tuple-element.96), channel_id=1, source_target_pairs={{0,6},{1,7},{2,4},{3,5},{4,2},{5,3},{6,0},{7,1},{8,14},{9,15},{10,... | collective-permute-start | bytes 202760 | tf_op jit(solution)/shard_map/ppermute | solution.py:539
  23.1 2.2 %collective-permute-start.12 = (bf16[264,128]{1,0:T(8,128)(2,1)S(1)}, bf16[264,128]{1,0:T(8,128)(2,1)S(1)}, u32[]{:S(2)}, u32[]{:S(2)}) collective-permute-start(bf16[264,128]{1,0:T(8,128)(2,1)S(1)} %get-tuple-element.97), channel_id=1, source_target_pairs={{0,7},{1,6},{2,5},{3,4},{4,3},{5,2},{6,1},{7,0},{8,15},{9,14},{10,... | collective-permute-start | bytes 202760 | tf_op jit(solution)/shard_map/ppermute | solution.py:539
  25.3 2.8 %collective-permute-start.8 = (bf16[264,128]{1,0:T(8,128)(2,1)S(1)}, bf16[264,128]{1,0:T(8,128)(2,1)S(1)}, u32[]{:S(2)}, u32[]{:S(2)}) collective-permute-start(bf16[264,128]{1,0:T(8,128)(2,1)S(1)} %get-tuple-element.93), channel_id=1, source_target_pairs={{0,3},{1,2},{2,1},{3,0},{4,7},{5,6},{6,5},{7,4},{8,11},{9,10},{10,... | collective-permute-start | bytes 202760 | tf_op jit(solution)/shard_map/ppermute | solution.py:539
  28.1 3.6 %collective-permute-start.9 = (bf16[264,128]{1,0:T(8,128)(2,1)S(1)}, bf16[264,128]{1,0:T(8,128)(2,1)S(1)}, u32[]{:S(2)}, u32[]{:S(2)}) collective-permute-start(bf16[264,128]{1,0:T(8,128)(2,1)S(1)} %get-tuple-element.94), channel_id=1, source_target_pairs={{0,4},{1,5},{2,6},{3,7},{4,0},{5,1},{6,2},{7,3},{8,12},{9,13},{10,... | collective-permute-start | bytes 202760 | tf_op jit(solution)/shard_map/ppermute | solution.py:539
  32.3 3.5 %collective-permute-done.9.refs_10_ = bf16[264,128]{1,0:T(8,128)(2,1)S(1)} collective-permute-done((bf16[264,128]{1,0:T(8,128)(2,1)S(1)}, bf16[264,128]{1,0:T(8,128)(2,1)S(1)}, u32[]{:S(2)}, u32[]{:S(2)}) %collective-permute-start.9) | collective-permute-done | bytes 67616 | tf_op jit(solution)/shard_map/ppermute | solution.py:539
  35.9 5.9 %shard_map.107 = (bf16[64,512]{1,0:T(8,128)(2,1)S(1)}, bf16[64,512]{1,0:T(8,128)(2,1)S(1)}, bf16[64,512]{1,0:T(8,128)(2,1)S(1)}, bf16[64,512]{1,0:T(8,128)(2,1)S...) custom-call(f32[1,512]{1,0:T(1,128)S(1)} %get-tuple-element.66.refs_, ...), custom_call_target="tpu_custom_call" | custom-call | flops 8589934592 | bytes 4194304 | tf_op jit(solution)/shard_map/pallas_call | solution.py:673
  42.3 1.9 %collective-permute-start.3 = (f32[16,256]{1,0:T(8,128)S(1)}, f32[16,256]{1,0:T(8,128)S(1)}, u32[]{:S(2)}, u32[]{:S(2)}) collective-permute-start(f32[16,256]{1,0:T(8,128)S(1)} %get-tuple-element.81.refs_2_), channel_id=1, source_target_pairs={{0,16},{8,24},{16,0},{24,8},{1,17},{9,25},{17,1},{25,9},{2,18},{10... | collective-permute-start | bytes 49160 | tf_op jit(solution)/shard_map/ppermute | solution.py:539
  44.2 1.5 %collective-permute-start.4 = (f32[16,256]{1,0:T(8,128)S(1)}, f32[16,256]{1,0:T(8,128)S(1)}, u32[]{:S(2)}, u32[]{:S(2)}) collective-permute-start(f32[16,256]{1,0:T(8,128)S(1)} %get-tuple-element.81.refs_2_), channel_id=1, source_target_pairs={{0,8},{8,0},{16,24},{24,16},{1,9},{9,1},{17,25},{25,17},{2,10},{10... | collective-permute-start | bytes 49160 | tf_op jit(solution)/shard_map/ppermute | solution.py:539
  47.1 0.9 %collective-permute-done.4.refs_4_ = f32[16,256]{1,0:T(8,128)S(1)} collective-permute-done((f32[16,256]{1,0:T(8,128)S(1)}, f32[16,256]{1,0:T(8,128)S(1)}, u32[]{:S(2)}, u32[]{:S(2)}) %collective-permute-start.4) | collective-permute-done | bytes 16416 | tf_op jit(solution)/shard_map/ppermute | solution.py:539
  48.1 0.8 %collective-permute-start.16 = (bf16[64,512]{1,0:T(8,128)(2,1)S(1)}, bf16[64,512]{1,0:T(8,128)(2,1)S(1)}, u32[]{:S(2)}, u32[]{:S(2)}) collective-permute-start(bf16[64,512]{1,0:T(8,128)(2,1)S(1)} %get-tuple-element.102), channel_id=1, source_target_pairs={{0,4},{1,5},{2,6},{3,7},{4,0},{5,1},{6,2},{7,3},{8,12},{9,13},{10,... | collective-permute-start | bytes 196616 | tf_op jit(solution)/shard_map/ppermute | solution.py:539
  48.9 1.5 %collective-permute-done.5.refs_5_ = f32[16,256]{1,0:T(8,128)S(1)} collective-permute-done((f32[16,256]{1,0:T(8,128)S(1)}, f32[16,256]{1,0:T(8,128)S(1)}, u32[]{:S(2)}, u32[]{:S(2)}) %collective-permute-start.5) | collective-permute-done | bytes 16416 | tf_op jit(solution)/shard_map/ppermute | solution.py:539
  50.6 2.1 %collective-permute-start.18 = (bf16[64,512]{1,0:T(8,128)(2,1)S(1)}, bf16[64,512]{1,0:T(8,128)(2,1)S(1)}, u32[]{:S(2)}, u32[]{:S(2)}) collective-permute-start(bf16[64,512]{1,0:T(8,128)(2,1)S(1)} %get-tuple-element.104), channel_id=1, source_target_pairs={{0,6},{1,7},{2,4},{3,5},{4,2},{5,3},{6,0},{7,1},{8,14},{9,15},{10,... | collective-permute-start | bytes 196616 | tf_op jit(solution)/shard_map/ppermute | solution.py:539
  52.7 1.9 %collective-permute-start.19 = (bf16[64,512]{1,0:T(8,128)(2,1)S(1)}, bf16[64,512]{1,0:T(8,128)(2,1)S(1)}, u32[]{:S(2)}, u32[]{:S(2)}) collective-permute-start(bf16[64,512]{1,0:T(8,128)(2,1)S(1)} %get-tuple-element.105), channel_id=1, source_target_pairs={{0,7},{1,6},{2,5},{3,4},{4,3},{5,2},{6,1},{7,0},{8,15},{9,14},{10,... | collective-permute-start | bytes 196616 | tf_op jit(solution)/shard_map/ppermute | solution.py:539
  54.6 2.3 %shard_map.106.refs_13_.refs_0_ = bf16[16,256,1024]{2,1,0:T(8,128)(2,1)S(1)} custom-call(bf16[256,512]{1,0:T(8,128)(2,1)S(1)} %get-tuple-element.63.refs_9_.refs_0_.refs_4_, bf16[1024,512]{1,0:T(8,128)(2,1)S(1)} %shard_map.102.refs_1_.refs_2_, f32[16,256]{1,0:T(8,128)S(1)} %get-tuple-element.81.refs_2_, f32[16,256]{1,0:T(8,128)S(1)} %collective-permute-done.3.refs_3_, ...), custom_call_target="tpu_custom_call" | custom-call | flops 4294967296 | bytes 10485760 | tf_op jit(solution)/shard_map/pallas_call | solution.py:666
  57.5 2.6 %collective-permute-done.17.refs_8_ = bf16[64,512]{1,0:T(8,128)(2,1)S(1)} collective-permute-done((bf16[64,512]{1,0:T(8,128)(2,1)S(1)}, bf16[64,512]{1,0:T(8,128)(2,1)S(1)}, u32[]{:S(2)}, u32[]{:S(2)}) %collective-permute-start.17) | collective-permute-done | bytes 65568 | tf_op jit(solution)/shard_map/ppermute | solution.py:539
  60.0 1.0 %shard_map.108 = (bf16[256,512]{1,0:T(8,128)(2,1)S(1)}, bf16[272,512]{1,0:T(8,128)(2,1)S(1)}) custom-call(s32[1,256]{1,0:T(1,128)S(1)} %get-tuple-element.65.refs_4_.refs_0_, bf16[256,512]{1,0:T(8,128)(2,1)S(1)} %get-tuple-element.89.refs_1_, bf16[512,512]{1,0:T(8,128)(2,1)S(1)} %copy-done.6, bf16[64,512]{1,0:T(8,128)(2,1)S(1)} %get-tuple-element.98.refs_3_, ...), custom_call_target="tpu_custom_call" | custom-call | flops 536870912 | bytes 2097152 | tf_op jit(solution)/shard_map/pallas_call | solution.py:695
  61.7 1.5 %collective-permute-start.21 = (bf16[272,512]{1,0:T(8,128)(2,1)S(1)}, bf16[272,512]{1,0:T(8,128)(2,1)S(1)}, u32[]{:S(2)}, u32[]{:S(2)}) collective-permute-start(bf16[272,512]{1,0:T(8,128)(2,1)S(1)} %get-tuple-element.106.refs_14_), channel_id=1, source_target_pairs={{0,8},{8,0},{16,24},{24,16},{1,9},{9,1},{17,25},{25,17},{2,10},{10... | collective-permute-start | bytes 835592 | tf_op jit(solution)/shard_map/ppermute | solution.py:539
  63.2 1.3 %collective-permute-start.22 = (bf16[272,512]{1,0:T(8,128)(2,1)S(1)}, bf16[272,512]{1,0:T(8,128)(2,1)S(1)}, u32[]{:S(2)}, u32[]{:S(2)}) collective-permute-start(bf16[272,512]{1,0:T(8,128)(2,1)S(1)} %get-tuple-element.106.refs_14_), channel_id=1, source_target_pairs={{0,24},{8,16},{16,8},{24,0},{1,25},{9,17},{17,9},{25,1},{2,26},{10... | collective-permute-start | bytes 835592 | tf_op jit(solution)/shard_map/ppermute | solution.py:539
  64.6 7.2 %shard_map.109 = (bf16[256,512]{1,0:T(8,128)(2,1)S(1)}, f32[256,512]{1,0:T(8,128)S(1)}, f32[256,512]{1,0:T(8,128)S(1)}) custom-call(bf16[16,256,256]{2,1,0:T(8,128)(2,1)S(1)} %get-tuple-element.82.refs_0_, bf16[16,256,256]{2,1,0:T(8,128)(2,1)S(1)} %get-tuple-element.83.refs_1_, bf16[16,256,256]{2,1,0:T(8,128)(2,1)S(1)} %get-tuple-element.84.refs_2_, ...), custom_call_target="tpu_custom_call" | custom-call | flops 8589934592 | bytes 10485760 | tf_op jit(solution)/shard_map/pallas_call | solution.py:703
  71.7 2.3 %shard_map.110 = (f32[256,512]{1,0:T(8,128)S(1)}, f32[256,512]{1,0:T(8,128)S(1)}) custom-call(bf16[16,256,1024]{2,1,0:T(8,128)(2,1)S(1)} %shard_map.106.refs_13_.refs_0_, bf16[256,512]{1,0:T(8,128)(2,1)S(1)} %get-tuple-element.75.refs_12_.refs_8_.refs_1_, bf16[1024,512]{1,0:T(8,128)(2,1)S(1)} %shard_map.102.refs_1_.refs_2_, ...), custom_call_target="tpu_custom_call" | custom-call | flops 2147483648 | bytes 4194304 | tf_op jit(solution)/shard_map/pallas_call | solution.py:711
  74.0 2.3 %shard_map.111 = (f32[256,512]{1,0:T(8,128)S(1)}, f32[256,512]{1,0:T(8,128)S(1)}) custom-call(bf16[16,256,1024]{2,1,0:T(8,128)(2,1)S(1)} %shard_map.106.refs_13_.refs_0_, bf16[256,512]{1,0:T(8,128)(2,1)S(1)} %get-tuple-element.75.refs_12_.refs_8_.refs_1_, bf16[1024,512]{1,0:T(8,128)(2,1)S(1)} %shard_map.102.refs_1_.refs_2_, ...), custom_call_target="tpu_custom_call" | custom-call | flops 2147483648 | bytes 4194304 | tf_op jit(solution)/shard_map/pallas_call | solution.py:711
  76.9 3.6 %shard_map.112 = bf16[256,512]{1,0:T(8,128)(2,1)} custom-call(bf16[16,256,1024]{2,1,0:T(8,128)(2,1)S(1)} %shard_map.106.refs_13_.refs_0_, bf16[256,512]{1,0:T(8,128)(2,1)S(1)} %get-tuple-element.75.refs_12_.refs_8_.refs_1_, bf16[1024,512]{1,0:T(8,128)(2,1)S(1)} %shard_map.102.refs_1_.refs_2_, bf16[256,512]{1,0:T(8,128)(2,1)S(1)} %get-tuple-element.107.refs_3_, ...), custom_call_target="tpu_custom_call" | custom-call | flops 8589934592 | bytes 14680064 | tf_op jit(solution)/shard_map/pallas_call | solution.py:718
  (53 shorter events, 6.5 us)
Async XLA Ops:
  0.0 10.6 %collective-permute-start = (bf16[256,512]{1,0:T(8,128)(2,1)}, bf16[256,512]{1,0:T(8,128)(2,1)S(1)}, u32[]{:S(2)}, u32[]{:S(2)}) collective-permute-start(bf16[256,512]{1,0:T(8,128)(2,1)} %bitcast.15), channel_id=1, source_target_pairs={{0,16},{8,24},{16,0},{24,8},{1,17},{9,25},{17,1},{25,9},{2,18},{10... | collective-permute-start | bytes 786440 | tf_op jit(solution)/shard_map/ppermute | solution.py:539
  3.0 9.5 %collective-permute-start.1 = (bf16[256,512]{1,0:T(8,128)(2,1)}, bf16[256,512]{1,0:T(8,128)(2,1)S(1)}, u32[]{:S(2)}, u32[]{:S(2)}) collective-permute-start(bf16[256,512]{1,0:T(8,128)(2,1)} %bitcast.16), channel_id=1, source_target_pairs={{0,8},{8,0},{16,24},{24,16},{1,9},{9,1},{17,25},{25,17},{2,10},{10... | collective-permute-start | bytes 786440 | tf_op jit(solution)/shard_map/ppermute | solution.py:539
  4.5 11.8 %collective-permute-start.2 = (bf16[256,512]{1,0:T(8,128)(2,1)}, bf16[256,512]{1,0:T(8,128)(2,1)S(1)}, u32[]{:S(2)}, u32[]{:S(2)}) collective-permute-start(bf16[256,512]{1,0:T(8,128)(2,1)} %bitcast.17), channel_id=1, source_target_pairs={{0,24},{8,16},{16,8},{24,0},{1,25},{9,17},{17,9},{25,1},{2,26},{10... | collective-permute-start | bytes 786440 | tf_op jit(solution)/shard_map/ppermute | solution.py:539
  8.6 2.0 %copy-start.1 = (bf16[512,1536]{1,0:T(8,128)(2,1)S(1)}, bf16[512,1536]{1,0:T(8,128)(2,1)}, u32[]{:S(2)}) copy-start(bf16[512,1536]{1,0:T(8,128)(2,1)} %refs_8_.1) | copy-start | bytes 4718596
  12.5 3.8 %copy-start.6 = (bf16[512,512]{1,0:T(8,128)(2,1)S(1)}, bf16[512,512]{1,0:T(8,128)(2,1)}, u32[]{:S(2)}) copy-start(bf16[512,512]{1,0:T(8,128)(2,1)} %refs_2_.9) | copy-start | bytes 1572868
  16.3 19.5 %copy-start.4 = (bf16[512,1536]{1,0:T(8,128)(2,1)S(1)}, bf16[512,1536]{1,0:T(8,128)(2,1)}, u32[]{:S(2)}) copy-start(bf16[512,1536]{1,0:T(8,128)(2,1)} %refs_3_.3) | copy-start | bytes 4718596
  16.3 19.5 %copy-start.5 = (bf16[512,512]{1,0:T(8,128)(2,1)S(1)}, bf16[512,512]{1,0:T(8,128)(2,1)}, u32[]{:S(2)}) copy-start(bf16[512,512]{1,0:T(8,128)(2,1)} %refs_4_.1) | copy-start | bytes 1572868
  16.3 19.5 %copy-start.7 = (bf16[1,1,256,512]{3,2,1,0:T(8,128)(2,1)S(1)}, bf16[1,1,256,512]{3,2,1,0:T(8,128)(2,1)}, u32[]{:S(2)}) copy-start(bf16[1,1,256,512]{3,2,1,0:T(8,128)(2,1)} %param.19) | copy-start | bytes 786436
  16.3 19.5 %copy-start.10 = (f32[512]{0:T(512)S(1)}, f32[512]{0:T(512)}, u32[]{:S(2)}) copy-start(f32[512]{0:T(512)} %param.15) | copy-start | bytes 6148
  16.3 19.5 %copy-start.12 = (s32[1,1,256]{2,1,0:T(1,128)S(1)}, s32[1,1,256]{2,1,0:T(1,128)}, u32[]{:S(2)}) copy-start(s32[1,1,256]{2,1,0:T(1,128)} %param.18) | copy-start | bytes 3076
  19.2 6.1 %collective-permute-start.10 = (bf16[264,128]{1,0:T(8,128)(2,1)S(1)}, bf16[264,128]{1,0:T(8,128)(2,1)S(1)}, u32[]{:S(2)}, u32[]{:S(2)}) collective-permute-start(bf16[264,128]{1,0:T(8,128)(2,1)S(1)} %get-tuple-element.95), channel_id=1, source_target_pairs={{0,5},{1,4},{2,7},{3,6},{4,1},{5,0},{6,3},{7,2},{8,13},{9,12},{10,... | collective-permute-start | bytes 202760 | tf_op jit(solution)/shard_map/ppermute | solution.py:539
  20.3 7.7 %collective-permute-start.11 = (bf16[264,128]{1,0:T(8,128)(2,1)S(1)}, bf16[264,128]{1,0:T(8,128)(2,1)S(1)}, u32[]{:S(2)}, u32[]{:S(2)}) collective-permute-start(bf16[264,128]{1,0:T(8,128)(2,1)S(1)} %get-tuple-element.96), channel_id=1, source_target_pairs={{0,6},{1,7},{2,4},{3,5},{4,2},{5,3},{6,0},{7,1},{8,14},{9,15},{10,... | collective-permute-start | bytes 202760 | tf_op jit(solution)/shard_map/ppermute | solution.py:539
  23.1 8.5 %collective-permute-start.12 = (bf16[264,128]{1,0:T(8,128)(2,1)S(1)}, bf16[264,128]{1,0:T(8,128)(2,1)S(1)}, u32[]{:S(2)}, u32[]{:S(2)}) collective-permute-start(bf16[264,128]{1,0:T(8,128)(2,1)S(1)} %get-tuple-element.97), channel_id=1, source_target_pairs={{0,7},{1,6},{2,5},{3,4},{4,3},{5,2},{6,1},{7,0},{8,15},{9,14},{10,... | collective-permute-start | bytes 202760 | tf_op jit(solution)/shard_map/ppermute | solution.py:539
  25.3 6.3 %collective-permute-start.6 = (bf16[264,128]{1,0:T(8,128)(2,1)S(1)}, bf16[264,128]{1,0:T(8,128)(2,1)S(1)}, u32[]{:S(2)}, u32[]{:S(2)}) collective-permute-start(bf16[264,128]{1,0:T(8,128)(2,1)S(1)} %get-tuple-element.91), channel_id=1, source_target_pairs={{0,1},{1,0},{2,3},{3,2},{4,5},{5,4},{6,7},{7,6},{8,9},{9,8},{10,11... | collective-permute-start | bytes 202760 | tf_op jit(solution)/shard_map/ppermute | solution.py:539
  25.3 6.3 %collective-permute-start.7 = (bf16[264,128]{1,0:T(8,128)(2,1)S(1)}, bf16[264,128]{1,0:T(8,128)(2,1)S(1)}, u32[]{:S(2)}, u32[]{:S(2)}) collective-permute-start(bf16[264,128]{1,0:T(8,128)(2,1)S(1)} %get-tuple-element.92), channel_id=1, source_target_pairs={{0,2},{1,3},{2,0},{3,1},{4,6},{5,7},{6,4},{7,5},{8,10},{9,11},{10,... | collective-permute-start | bytes 202760 | tf_op jit(solution)/shard_map/ppermute | solution.py:539
  25.3 7.0 %collective-permute-start.8 = (bf16[264,128]{1,0:T(8,128)(2,1)S(1)}, bf16[264,128]{1,0:T(8,128)(2,1)S(1)}, u32[]{:S(2)}, u32[]{:S(2)}) collective-permute-start(bf16[264,128]{1,0:T(8,128)(2,1)S(1)} %get-tuple-element.93), channel_id=1, source_target_pairs={{0,3},{1,2},{2,1},{3,0},{4,7},{5,6},{6,5},{7,4},{8,11},{9,10},{10,... | collective-permute-start | bytes 202760 | tf_op jit(solution)/shard_map/ppermute | solution.py:539
  28.1 7.8 %collective-permute-start.9 = (bf16[264,128]{1,0:T(8,128)(2,1)S(1)}, bf16[264,128]{1,0:T(8,128)(2,1)S(1)}, u32[]{:S(2)}, u32[]{:S(2)}) collective-permute-start(bf16[264,128]{1,0:T(8,128)(2,1)S(1)} %get-tuple-element.94), channel_id=1, source_target_pairs={{0,4},{1,5},{2,6},{3,7},{4,0},{5,1},{6,2},{7,3},{8,12},{9,13},{10,... | collective-permute-start | bytes 202760 | tf_op jit(solution)/shard_map/ppermute | solution.py:539
  35.9 9.9 %copy-start.3 = (f32[512]{0:T(512)S(1)}, f32[512]{0:T(512)}, u32[]{:S(2)}) copy-start(f32[512]{0:T(512)} %param.11) | copy-start | bytes 6148
  41.8 8.9 %collective-permute-start.13 = (bf16[64,512]{1,0:T(8,128)(2,1)S(1)}, bf16[64,512]{1,0:T(8,128)(2,1)S(1)}, u32[]{:S(2)}, u32[]{:S(2)}) collective-permute-start(bf16[64,512]{1,0:T(8,128)(2,1)S(1)} %get-tuple-element.99), channel_id=1, source_target_pairs={{0,1},{1,0},{2,3},{3,2},{4,5},{5,4},{6,7},{7,6},{8,9},{9,8},{10,11... | collective-permute-start | bytes 196616 | tf_op jit(solution)/shard_map/ppermute | solution.py:539
  42.0 10.7 %collective-permute-start.14 = (bf16[64,512]{1,0:T(8,128)(2,1)S(1)}, bf16[64,512]{1,0:T(8,128)(2,1)S(1)}, u32[]{:S(2)}, u32[]{:S(2)}) collective-permute-start(bf16[64,512]{1,0:T(8,128)(2,1)S(1)} %get-tuple-element.100), channel_id=1, source_target_pairs={{0,2},{1,3},{2,0},{3,1},{4,6},{5,7},{6,4},{7,5},{8,10},{9,11},{10,... | collective-permute-start | bytes 196616 | tf_op jit(solution)/shard_map/ppermute | solution.py:539
  42.3 4.2 %collective-permute-start.3 = (f32[16,256]{1,0:T(8,128)S(1)}, f32[16,256]{1,0:T(8,128)S(1)}, u32[]{:S(2)}, u32[]{:S(2)}) collective-permute-start(f32[16,256]{1,0:T(8,128)S(1)} %get-tuple-element.81.refs_2_), channel_id=1, source_target_pairs={{0,16},{8,24},{16,0},{24,8},{1,17},{9,25},{17,1},{25,9},{2,18},{10... | collective-permute-start | bytes 49160 | tf_op jit(solution)/shard_map/ppermute | solution.py:539
  44.2 3.8 %collective-permute-start.4 = (f32[16,256]{1,0:T(8,128)S(1)}, f32[16,256]{1,0:T(8,128)S(1)}, u32[]{:S(2)}, u32[]{:S(2)}) collective-permute-start(f32[16,256]{1,0:T(8,128)S(1)} %get-tuple-element.81.refs_2_), channel_id=1, source_target_pairs={{0,8},{8,0},{16,24},{24,16},{1,9},{9,1},{17,25},{25,17},{2,10},{10... | collective-permute-start | bytes 49160 | tf_op jit(solution)/shard_map/ppermute | solution.py:539
  45.7 4.6 %collective-permute-start.5 = (f32[16,256]{1,0:T(8,128)S(1)}, f32[16,256]{1,0:T(8,128)S(1)}, u32[]{:S(2)}, u32[]{:S(2)}) collective-permute-start(f32[16,256]{1,0:T(8,128)S(1)} %get-tuple-element.81.refs_2_), channel_id=1, source_target_pairs={{0,24},{8,16},{16,8},{24,0},{1,25},{9,17},{17,9},{25,1},{2,26},{10... | collective-permute-start | bytes 49160 | tf_op jit(solution)/shard_map/ppermute | solution.py:539
  46.5 10.4 %collective-permute-start.15 = (bf16[64,512]{1,0:T(8,128)(2,1)S(1)}, bf16[64,512]{1,0:T(8,128)(2,1)S(1)}, u32[]{:S(2)}, u32[]{:S(2)}) collective-permute-start(bf16[64,512]{1,0:T(8,128)(2,1)S(1)} %get-tuple-element.101), channel_id=1, source_target_pairs={{0,3},{1,2},{2,1},{3,0},{4,7},{5,6},{6,5},{7,4},{8,11},{9,10},{10,... | collective-permute-start | bytes 196616 | tf_op jit(solution)/shard_map/ppermute | solution.py:539
  48.1 9.4 %collective-permute-start.16 = (bf16[64,512]{1,0:T(8,128)(2,1)S(1)}, bf16[64,512]{1,0:T(8,128)(2,1)S(1)}, u32[]{:S(2)}, u32[]{:S(2)}) collective-permute-start(bf16[64,512]{1,0:T(8,128)(2,1)S(1)} %get-tuple-element.102), channel_id=1, source_target_pairs={{0,4},{1,5},{2,6},{3,7},{4,0},{5,1},{6,2},{7,3},{8,12},{9,13},{10,... | collective-permute-start | bytes 196616 | tf_op jit(solution)/shard_map/ppermute | solution.py:539
  50.4 9.7 %collective-permute-start.17 = (bf16[64,512]{1,0:T(8,128)(2,1)S(1)}, bf16[64,512]{1,0:T(8,128)(2,1)S(1)}, u32[]{:S(2)}, u32[]{:S(2)}) collective-permute-start(bf16[64,512]{1,0:T(8,128)(2,1)S(1)} %get-tuple-element.103), channel_id=1, source_target_pairs={{0,5},{1,4},{2,7},{3,6},{4,1},{5,0},{6,3},{7,2},{8,13},{9,12},{10,... | collective-permute-start | bytes 196616 | tf_op jit(solution)/shard_map/ppermute | solution.py:539
  50.6 9.4 %collective-permute-start.18 = (bf16[64,512]{1,0:T(8,128)(2,1)S(1)}, bf16[64,512]{1,0:T(8,128)(2,1)S(1)}, u32[]{:S(2)}, u32[]{:S(2)}) collective-permute-start(bf16[64,512]{1,0:T(8,128)(2,1)S(1)} %get-tuple-element.104), channel_id=1, source_target_pairs={{0,6},{1,7},{2,4},{3,5},{4,2},{5,3},{6,0},{7,1},{8,14},{9,15},{10,... | collective-permute-start | bytes 196616 | tf_op jit(solution)/shard_map/ppermute | solution.py:539
  52.7 7.4 %collective-permute-start.19 = (bf16[64,512]{1,0:T(8,128)(2,1)S(1)}, bf16[64,512]{1,0:T(8,128)(2,1)S(1)}, u32[]{:S(2)}, u32[]{:S(2)}) collective-permute-start(bf16[64,512]{1,0:T(8,128)(2,1)S(1)} %get-tuple-element.105), channel_id=1, source_target_pairs={{0,7},{1,6},{2,5},{3,4},{4,3},{5,2},{6,1},{7,0},{8,15},{9,14},{10,... | collective-permute-start | bytes 196616 | tf_op jit(solution)/shard_map/ppermute | solution.py:539
  61.0 10.7 %collective-permute-start.20 = (bf16[272,512]{1,0:T(8,128)(2,1)S(1)}, bf16[272,512]{1,0:T(8,128)(2,1)S(1)}, u32[]{:S(2)}, u32[]{:S(2)}) collective-permute-start(bf16[272,512]{1,0:T(8,128)(2,1)S(1)} %get-tuple-element.106.refs_14_), channel_id=1, source_target_pairs={{0,16},{8,24},{16,0},{24,8},{1,17},{9,25},{17,1},{25,9},{2,18},{10... | collective-permute-start | bytes 835592 | tf_op jit(solution)/shard_map/ppermute | solution.py:539
  61.7 12.3 %collective-permute-start.21 = (bf16[272,512]{1,0:T(8,128)(2,1)S(1)}, bf16[272,512]{1,0:T(8,128)(2,1)S(1)}, u32[]{:S(2)}, u32[]{:S(2)}) collective-permute-start(bf16[272,512]{1,0:T(8,128)(2,1)S(1)} %get-tuple-element.106.refs_14_), channel_id=1, source_target_pairs={{0,8},{8,0},{16,24},{24,16},{1,9},{9,1},{17,25},{25,17},{2,10},{10... | collective-permute-start | bytes 835592 | tf_op jit(solution)/shard_map/ppermute | solution.py:539
  63.2 13.7 %collective-permute-start.22 = (bf16[272,512]{1,0:T(8,128)(2,1)S(1)}, bf16[272,512]{1,0:T(8,128)(2,1)S(1)}, u32[]{:S(2)}, u32[]{:S(2)}) collective-permute-start(bf16[272,512]{1,0:T(8,128)(2,1)S(1)} %get-tuple-element.106.refs_14_), channel_id=1, source_target_pairs={{0,24},{8,16},{16,8},{24,0},{1,25},{9,17},{17,9},{25,1},{2,26},{10... | collective-permute-start | bytes 835592 | tf_op jit(solution)/shard_map/ppermute | solution.py:539
  74.0 2.9 %copy-start.9 = (bf16[1,1,256,512]{3,2,1,0:T(8,128)(2,1)S(1)}, bf16[1,1,256,512]{3,2,1,0:T(8,128)(2,1)}, u32[]{:S(2)}) copy-start(bf16[1,1,256,512]{3,2,1,0:T(8,128)(2,1)} %param.10) | copy-start | bytes 786436
  (4 other events, 3.7 us)

commit v2 on v1

--- a/solution.py
+++ b/solution.py
@@ -31,19 +31,21 @@
     return lax.dot_general(left, right, (((0,), (0,)), ((), ())), preferred_element_type=F32)
 
 
-def norm_rows(rows, gain):
-    wide = rows.astype(F32)
-    power = jnp.mean(wide * wide, axis=-1, keepdims=True)
-    return (wide * lax.rsqrt(power + EPS) * gain).astype(BF16)
-
-
-def norm_pull(rows, gain, cotangent):
+def norm_parts(rows):
     wide = rows.astype(F32)
     power = jnp.mean(wide * wide, axis=-1, keepdims=True)
     inverse = lax.rsqrt(power + EPS)
-    scaled = cotangent.astype(F32) * gain
-    along = jnp.mean(scaled * wide, axis=-1, keepdims=True)
-    return (inverse * scaled - wide * (inverse * inverse * inverse * along)).astype(BF16)
+    return wide * inverse, inverse
+
+
+def norm_rows(rows, gain):
+    return (norm_parts(rows)[0] * gain).astype(BF16)
+
+
+def norm_pull(unit, slope, cotangent):
+    scaled = cotangent.astype(F32) * slope
+    along = jnp.mean(scaled * unit, axis=-1, keepdims=True)
+    return (scaled - unit * along).astype(BF16)
 
 
 def head_mask(rows, index, depth):
@@ -120,7 +122,7 @@
     return mixed, sums
 
 
-def route_body(chunks, capacity, me_ref, target_ref, slot_ref, at_ref):
+def route_body(chunks, capacity, me_ref, target_ref, put_ref, take_ref, at_ref):
     count = target_ref.shape[1]
     slots = 2 * count
     target = target_ref[...]
@@ -133,19 +135,23 @@
     )
     ranking = jnp.sum(jnp.where(same & earlier, 1.0, 0.0), axis=0, keepdims=True).astype(jnp.int32)
     lane = owner if chunks == 1 else lax.bitwise_xor(owner, jnp.full_like(owner, me_ref[0]))
-    slot_ref[...] = lane * capacity + ranking
-    hit = column(lane * capacity + ranking) == (
-        lax.broadcasted_iota(jnp.int32, (count, slots), 1).astype(F32)
-    )
+    slot = lane * capacity + ranking
+    put = lax.broadcasted_iota(jnp.int32, (slots, count), 0) == slot
+    put_ref[...] = put.astype(F32).astype(BF16)
+    hit = column(slot) == lax.broadcasted_iota(jnp.int32, (count, slots), 1).astype(F32)
+    take_ref[...] = hit.astype(F32).astype(BF16)
     at = jnp.sum(jnp.where(hit, column(offset) - count, 0.0), axis=0, keepdims=True) + count
     at_ref[...] = at.astype(at_ref.dtype)
 
 
 def prep_body(depth, *refs):
     x_ref, gain_ref, w_ref = refs[:3]
-    q_ref, k_ref, v_ref, weights_ref, mixed_ref, sums_ref = refs[3:]
+    q_ref, k_ref, v_ref, weights_ref, mixed_ref, sums_ref, unit_ref, slope_ref = refs[3:]
     width = x_ref.shape[1]
-    normed = norm_rows(x_ref[...], gain_ref[...])
+    unit, inverse = norm_parts(x_ref[...])
+    unit_ref[...] = unit
+    slope_ref[...] = inverse * gain_ref[...]
+    normed = (unit * gain_ref[...]).astype(BF16)
     q_ref[...] = dot_nn(normed, w_ref[:, :width]).astype(BF16)
     k_ref[...] = dot_nn(normed, w_ref[:, width : 2 * width]).astype(BF16)
     v_ref[...] = dot_nn(normed, w_ref[:, 2 * width :]).astype(BF16)
@@ -179,7 +185,7 @@
 
 
 def forward_body(early, peers, chunks, capacity, depth, *refs):
-    x_ref, gain_ref, w_ref, out_w_ref, slot_ref, at_ref, q_ref, mixed_in_ref, sums_in_ref = refs[:9]
+    x_ref, gain_ref, w_ref, out_w_ref, put_ref, at_ref, q_ref, mixed_in_ref, sums_in_ref = refs[:9]
     refs = refs[9:]
     early_keys, early_values, refs = refs[:early], refs[early : 2 * early], refs[2 * early :]
     others, refs = refs[: peers + 1 - early], refs[peers + 1 - early + early :]
@@ -249,8 +255,7 @@
 
     moved = (x_ref[...].astype(F32) + dot_nn(mixed_ref[...], out_w_ref[...])).astype(BF16)
     slots = 2 * count
-    picked = (lax.broadcasted_iota(jnp.int32, (slots, count), 0) == slot_ref[...]).astype(F32)
-    leaving = dot_nn(picked.astype(BF16), moved).astype(BF16)
+    leaving = dot_nn(put_ref[...], moved).astype(BF16)
     if chunks == 1:
         sends[0][...] = leaving
     else:
@@ -265,16 +270,19 @@
             send[send.shape[0] - tail :] = jnp.concatenate([line[:, part], padding], axis=1)
 
 
+def second_early_body(seg_ref, out_w_ref, grad_ref, mixed_grad_ref, bias_ref):
+    mixed_grad_ref[...] = dot_nt(grad_ref[...], out_w_ref[...]).astype(BF16)
+    bias_ref[...] = jnp.where(column(seg_ref[...]) == seg_ref[...].astype(F32), 0.0, MASKED)
+
+
 def second_body(chunks, depth, *refs):
-    land_ref, seg_ref, gain_ref, w_ref, out_w_ref, grad_ref = refs[:6]
+    land_ref, gain_ref, w_ref, grad_ref, mixed_grad, bias = refs[:6]
     arrived = refs[6 : 6 + chunks]
     sends = refs[6 + chunks : 6 + 2 * chunks]
-    packed, packed_grad, mixed_grad, bias = refs[6 + 2 * chunks :]
+    packed, packed_grad = refs[6 + 2 * chunks :]
     count, width = grad_ref.shape
     slots = 2 * count
     size = slots // chunks
-    mixed_grad[...] = dot_nt(grad_ref[...], out_w_ref[...]).astype(BF16)
-    bias[...] = jnp.where(column(seg_ref[...]) == seg_ref[...].astype(F32), 0.0, MASKED)
     if chunks == 1:
         landing = land_ref[...].astype(F32)
         rows = arrived[0][...]
@@ -289,32 +297,39 @@
     place = lax.broadcasted_iota(jnp.int32, (count, slots), 0).astype(F32) == landing
     place = place.astype(F32)
     hilbert = dot_nn(place.astype(BF16), rows).astype(BF16)
-    normed = norm_rows(hilbert, gain_ref[...])
-    packed[...] = dot_nn(normed, w_ref[...]).astype(BF16)
+    unit, inverse = norm_parts(hilbert)
+    packed[...] = dot_nn((unit * gain_ref[...]).astype(BF16), w_ref[...]).astype(BF16)
     scale = depth ** (-0.5)
 
-    def tile_step(t, carry):
-        at = tile_at(t)
-        k_at = tile_at(t + width // LANES)
-        v_at = tile_at(t + 2 * (width // LANES))
-        q_tile = packed[:, at]
-        k_tile = packed[:, k_at]
-        v_tile = packed[:, v_at]
-        g_tile = mixed_grad[:, at]
-        k_flipped = flip_tile(k_tile)
-        heads = LANES // depth
-        masks = [head_mask(count, j, depth) for j in range(heads)]
-        stacked = (heads, count, count)
+    tiles = width // LANES
+    heads = LANES // depth
+    masks = [head_mask(count, j, depth) for j in range(heads)]
+    stacked = (heads, count, count)
+
+    def products(t):
+        k_tile = packed[:, tile_at(t + tiles)]
+        v_tile = packed[:, tile_at(t + 2 * tiles)]
         k_heads = jnp.concatenate([only(mask, k_tile) for mask in masks], axis=0)
         v_heads = jnp.concatenate([only(mask, v_tile) for mask in masks], axis=0)
-        scores = dot_nt(k_heads, q_tile).reshape(stacked) * (scale * LOG2E) + bias[...][None]
-        weight_grad = dot_nt(v_heads, g_tile).reshape(stacked)
+        scores = dot_nt(k_heads, packed[:, tile_at(t)])
+        return scores, dot_nt(v_heads, mixed_grad[:, tile_at(t)])
+
+    def softmax(scores, weight_grad):
+        scores = scores.reshape(stacked) * (scale * LOG2E) + bias[...][None]
+        weight_grad = weight_grad.reshape(stacked)
         shifted = jnp.exp2(scores - jnp.max(scores, axis=1, keepdims=True))
-        weights = shifted * (1.0 / jnp.sum(shifted, axis=1, keepdims=True))
-        carried = jnp.sum(weights * weight_grad, axis=1, keepdims=True)
+        inverse = 1.0 / jnp.sum(shifted, axis=1, keepdims=True)
+        carried = jnp.sum(shifted * weight_grad, axis=1, keepdims=True) * inverse
+        weights = shifted * inverse
         score_grad = (weights * (weight_grad - carried)).astype(BF16)
-        dk_heads = dot_nn(score_grad.reshape(heads * count, count), q_tile)
-        dv_heads = dot_nn(weights.astype(BF16).reshape(heads * count, count), g_tile)
+        return weights.astype(BF16), score_grad
+
+    def gradients(t, weights, score_grad):
+        at = tile_at(t)
+        k_at, v_at = tile_at(t + tiles), tile_at(t + 2 * tiles)
+        k_flipped = flip_tile(packed[:, k_at])
+        dk_heads = dot_nn(score_grad.reshape(heads * count, count), packed[:, at])
+        dv_heads = dot_nn(weights.reshape(heads * count, count), mixed_grad[:, at])
         dk, dv, dq = dk_heads[:count], dv_heads[:count], []
         for j in range(heads):
             part = slice(j * count, (j + 1) * count)
@@ -325,11 +340,14 @@
         packed_grad[:, at] = (dq * scale).astype(BF16)
         packed_grad[:, k_at] = (dk * scale).astype(BF16)
         packed_grad[:, v_at] = dv.astype(BF16)
-        return carry
-
-    tile_loop(width // LANES, tile_step, 0)
+
+    ahead = products(0)
+    for t in range(tiles):
+        now, ahead = ahead, products(t + 1) if t + 1 < tiles else None
+        gradients(t, *softmax(*now))
     normed_grad = dot_nt(packed_grad[...], w_ref[...]).astype(BF16)
-    total = grad_ref[...].astype(F32) + norm_pull(hilbert, gain_ref[...], normed_grad).astype(F32)
+    path = norm_pull(unit, inverse * gain_ref[...], normed_grad)
+    total = grad_ref[...].astype(F32) + path.astype(F32)
     back = lax.broadcasted_iota(jnp.int32, (slots, count), 1).astype(F32) == column(landing)
     returning = dot_nn(back.astype(F32).astype(BF16), total.astype(BF16)).astype(BF16)
     for m, send in enumerate(sends):
@@ -378,14 +396,12 @@
 
 
 def home_body(chunks, depth, *refs):
-    slot_ref, mixed_ref, out_w_ref = refs[:3]
+    take_ref, mixed_ref, out_w_ref = refs[:3]
     home = refs[3 : 3 + chunks]
     moved_ref, grad_ref = refs[3 + chunks :]
     count, width = moved_ref.shape
-    slots = 2 * count
-    take = lax.broadcasted_iota(jnp.int32, (count, slots), 1).astype(F32) == column(slot_ref[...])
-    take = take.astype(F32).astype(BF16)
-    moved = dot_nn(take, jnp.concatenate([piece[...] for piece in home], axis=0)).astype(BF16)
+    rows = jnp.concatenate([piece[...] for piece in home], axis=0)
+    moved = dot_nn(take_ref[...], rows).astype(BF16)
     moved_ref[...] = moved
     grad = dot_nt(moved, out_w_ref[...]).astype(BF16)
     grad_ref[:count] = grad
@@ -429,9 +445,9 @@
     weights_refs, refs = refs[:parts], refs[parts:]
     keys_refs, refs = refs[:parts], refs[parts:]
     values_refs, refs = refs[:parts], refs[parts:]
-    inverse_ref, flipped_ref, grad_ref, q_ref = refs[:4]
-    out_ref, dk_ref, dv_ref, lines, wide = refs[4:]
-    count, width = out_ref.shape
+    inverse_ref, flipped_ref, grad_ref, q_ref, w_ref = refs[:5]
+    normed_ref, dk_ref, dv_ref, dq_all, lines, wide = refs[5:]
+    count, width = q_ref.shape
     heads = LANES // depth
     high, low = halves(grad_ref[count:])
     lines[...] = high.astype(F32) + low.astype(F32)
@@ -451,7 +467,7 @@
             weights = jnp.concatenate([ref[t * heads + j] for ref in weights_refs], axis=1)
             score_grad = (weights.astype(F32) * (weight_grad - delta)).astype(BF16)
             dq = jnp.where(mask, dot_nn(score_grad, keys), dq)
-        out_ref[:, at] = (dq * (inverse_ref[:, at] * depth ** (-0.5))).astype(BF16)
+        dq_all[:, at] = (dq * (inverse_ref[:, at] * depth ** (-0.5))).astype(BF16)
         dk_ref[:, at], dv_ref[:, at] = key_tile(
             depth,
             t,
@@ -465,6 +481,7 @@
         return carry
 
     tile_loop(width // LANES, tile_step, 0)
+    normed_ref[...] = dot_nt(dq_all[...], w_ref[:, :width])
 
 
 def key_middle_body(index, depth, *refs):
@@ -495,12 +512,11 @@
 
 
 def key_grad_body(early, peers, depth, *refs):
-    flipped_ref, v_ref, queries_ref, dq_ref, dk_ref, dv_ref = refs[:6]
-    x_ref, gain_ref, w_ref, moved_ref = refs[6:10]
+    flipped_ref, v_ref, queries_ref, normed_ref, dk_ref, dv_ref = refs[:6]
+    unit_ref, slope_ref, w_ref, moved_ref = refs[6:10]
     others = refs[10 : 11 + peers - early]
     out_ref, packed_grad, grads, lines = refs[11 + peers - early :]
-    count, width = x_ref.shape
-    packed_grad[:, :width] = dq_ref[...]
+    count, width = unit_ref.shape
     for i, other in enumerate(others):
         rows = slice(i * count, (i + 1) * count)
         grads[rows] = other[:count]
@@ -520,13 +536,13 @@
             lines,
         )
         dk = (dk + dk_ref[:, at]) * depth ** (-0.5)
-        packed_grad[:, tile_at(t + width // LANES)] = dk.astype(BF16)
-        packed_grad[:, tile_at(t + 2 * (width // LANES))] = (dv + dv_ref[:, at]).astype(BF16)
+        packed_grad[:, at] = dk.astype(BF16)
+        packed_grad[:, tile_at(t + width // LANES)] = (dv + dv_ref[:, at]).astype(BF16)
         return carry
 
     tile_loop(width // LANES, tile_step, 0)
-    normed_grad = dot_nt(packed_grad[...], w_ref[...]).astype(BF16)
-    path = norm_pull(x_ref[...], gain_ref[...], normed_grad)
+    normed_grad = normed_ref[...] + dot_nt(packed_grad[...], w_ref[:, width:])
+    path = norm_pull(unit_ref[...], slope_ref[...], normed_grad.astype(BF16))
     out_ref[...] = (moved_ref[...].astype(F32) + path.astype(F32)).astype(BF16)
 
 
@@ -575,14 +591,15 @@
         return jax.ShapeDtypeStruct(dims, kind)
 
     me = lax.axis_index("curve").astype(jnp.int32).reshape(1)
-    slot, leaving_at = vmem_call(
+    put, take, leaving_at = vmem_call(
         functools.partial(route_body, chunks, capacity),
-        (shape(jnp.int32, 1, count), shape(jnp.int32 if chunks == 1 else F32, 1, slots)),
-        flops=1 << 20,
-        moved=1 << 12,
+        (shape(BF16, slots, count), shape(BF16, count, slots))
+        + (shape(jnp.int32 if chunks == 1 else F32, 1, slots),),
+        flops=8 << 30,
+        moved=16 << 20,
         in_specs=[SMEM_SPEC, VMEM_SPEC],
     )(me, hilbert_pos.reshape(1, count))
-    x_then, slot, leaving_at = lax.optimization_barrier((x, slot, leaving_at))
+    x_then, put, take, leaving_at = lax.optimization_barrier((x, put, take, leaving_at))
     landing = leaving_at
     if chunks == 1:
         landing = lax.all_to_all(
@@ -597,9 +614,9 @@
     lines_f32 = shape(F32, HEADS, count)
     square = shape(BF16, HEADS, count, count)
     dma = pltpu.SemaphoreType.DMA
-    q, k, v, own_weights, sum_mixed, sums = vmem_call(
+    q, k, v, own_weights, sum_mixed, sums, unit, slope = vmem_call(
         functools.partial(prep_body, depth),
-        (rows_bf16,) * 3 + (square,) + (rows_f32,) * 2,
+        (rows_bf16,) * 3 + (square,) + (rows_f32,) * 4,
         flops=2 << 30,
         moved=4 << 20,
     )(x_then, gain_one, qkv_one)
@@ -640,7 +657,7 @@
         gain_one,
         qkv_one,
         out_one,
-        slot,
+        put,
         leaving_at,
         q,
         sum_mixed,
@@ -656,6 +673,7 @@
     arrived = exchange(results[6 + early :], "curve")
     lse_all = [lse] + [by_xor(lse, "patch", m) for m in steps]
 
+    out_grad_then, inverse = lax.optimization_barrier((out_grad, inverse))
     queries_all = vmem_call(
         functools.partial(queries_body, peers),
         all_bf16,
@@ -670,24 +688,22 @@
         moved=10 << 20,
     )(k, queries_all, *lse_all)
 
+    second_mixed, bias = vmem_call(
+        second_early_body, (rows_bf16, shape(F32, count, count)), flops=1 << 29, moved=1 << 20
+    )(segments.reshape(1, count), out_two, out_grad_then.reshape(count, width))
     returning = vmem_call(
         functools.partial(second_body, chunks, depth),
         (chunk_bf16,) * chunks,
-        [
-            pltpu.VMEM((count, 3 * width), BF16),
-            pltpu.VMEM((count, 3 * width), BF16),
-            pltpu.VMEM((count, width), BF16),
-            pltpu.VMEM((count, count), F32),
-        ],
+        [pltpu.VMEM((count, 3 * width), BF16), pltpu.VMEM((count, 3 * width), BF16)],
         flops=8 << 30,
         moved=4 << 20,
     )(
         landing,
-        segments.reshape(1, count),
         gain_two,
         qkv_two,
-        out_two,
-        out_grad.reshape(count, width),
+        out_grad_then.reshape(count, width),
+        second_mixed,
+        bias,
         *arrived,
     )
     home = exchange(returning, "curve")
@@ -697,16 +713,20 @@
         (rows_bf16, shape(BF16, count + HEADS, width)),
         flops=1 << 29,
         moved=2 << 20,
-    )(slot, mixed, out_one, *home)
+    )(take, mixed, out_one, *home)
     grads = [by_xor(grad_own, "patch", m) for m in steps]
 
-    query_grad, key_grad, value_grad = vmem_call(
+    normed_grad, key_grad, value_grad = vmem_call(
         functools.partial(query_grad_body, len(all_keys), depth),
-        (rows_bf16, rows_f32, rows_f32),
-        [pltpu.VMEM((HEADS, count), F32), pltpu.VMEM((count, width), F32)],
+        (rows_f32, rows_f32, rows_f32),
+        [
+            pltpu.VMEM((count, width), BF16),
+            pltpu.VMEM((HEADS, count), F32),
+            pltpu.VMEM((count, width), F32),
+        ],
         flops=8 << 30,
         moved=10 << 20,
-    )(*all_weights, *all_keys, *all_values, inverse, flipped, grad_own, q)
+    )(*all_weights, *all_keys, *all_values, inverse, flipped, grad_own, q, qkv_one)
     for index in range(1, early):
         key_grad, value_grad = vmem_call(
             functools.partial(key_middle_body, index, depth),
@@ -719,7 +739,7 @@
         functools.partial(key_grad_body, early, peers, depth),
         rows_bf16,
         [
-            pltpu.VMEM((count, 3 * width), BF16),
+            pltpu.VMEM((count, 2 * width), BF16),
             pltpu.VMEM((late * count, width), BF16),
             pltpu.VMEM((HEADS, late * count), F32),
         ],
@@ -729,11 +749,11 @@
         flipped,
         v,
         queries_all,
-        query_grad,
+        normed_grad,
         key_grad,
         value_grad,
-        x,
-        gain_one,
+        unit,
+        slope,
         qkv_one,
         moved_grad,
         *grads[early - 1 :],

time: 81 us -> 80.2 us (level)
  local copies, waits for them, and re-layouts: 3.76 us -> 1.61 us
  waiting for transfers between devices: 12.3 us -> 14.1 us
    unnamed x26 -> x20, local copies, waits for them, and re-layouts: 3.76 us -> 1.61 us
    ppermute x23, waiting for transfers between devices: 12.3 us -> 14.1 us  [by_xor(): return lax.ppermute(array, axis, [(i, i ^ step) for i in range(size)])]
  transfers between devices with their start and end apart: 23 -> 23, of which waited for: 8 -> 10; matrix products, arithmetic and copies ran while one was open for 0% -> 0% of each run, Pallas kernels for 26% -> 27%
where the time goes in v2:
time: 80.2 us; the launch traced here: 79.7 us
  Pallas kernels  33.7 us (42%)
  starting transfers between devices  30.1 us (38%)
  waiting for transfers between devices  14.1 us (18%)
  local copies, waits for them, and re-layouts  1.61 us (2%)
    ppermute x23, starting transfers between devices, by_xor(): return lax.ppermute(array, axis, [(i, i ^ step) for i in range(size)])  30.1 us
    ppermute x23, waiting for transfers between devices, by_xor(): return lax.ppermute(array, axis, [(i, i ^ step) for i in range(size)])  14.1 us
    pallas_call x1, Pallas kernels, shards(): vmem_call(functools.partial(query_grad_body, len(all_keys), depth), (rows...  7.2 us
    pallas_call x1, Pallas kernels, shards(): vmem_call(functools.partial(second_body, chunks, depth), (chunk_bf16,) *...  5.58 us
    pallas_call x2, Pallas kernels, shards(): vmem_call(functools.partial(key_middle_body, index, depth), (rows_f32, ro...  4.56 us
    pallas_call x2, Pallas kernels, shards(): vmem_call(functools.partial(middle_body, depth), (rows_bf16,) * 2 + (squa...  3.57 us
    pallas_call x1, Pallas kernels, shards(): vmem_call(functools.partial(key_grad_body, early, peers, depth), rows_bf1...  3.42 us
    pallas_call x1, Pallas kernels, shards(): vmem_call(functools.partial(forward_body, early, peers, chunks, capacity,...  2.78 us
  transfers between devices with their start and end apart: 23, of which 10 were waited for; matrix products, arithmetic and copies ran while one was open for 0% of the time, Pallas kernels for 27%

profile of v2, /device:TPU:0, one launch (start us, length us, event | category | flops | bytes accessed | tf_op | source)
XLA Modules:
  0.0 79.7 jit_solution(3488405157065762919)
XLA Ops:
  0.0 3.0 %collective-permute-start = (bf16[256,512]{1,0:T(8,128)(2,1)}, bf16[256,512]{1,0:T(8,128)(2,1)S(1)}, u32[]{:S(2)}, u32[]{:S(2)}) collective-permute-start(bf16[256,512]{1,0:T(8,128)(2,1)} %bitcast.13), channel_id=1, source_target_pairs={{0,16},{8,24},{16,0},{24,8},{1,17},{9,25},{17,1},{25,9},{2,18},{10... | collective-permute-start | bytes 786440 | tf_op jit(solution)/shard_map/ppermute | solution.py:555
  3.0 1.5 %collective-permute-start.1 = (bf16[256,512]{1,0:T(8,128)(2,1)}, bf16[256,512]{1,0:T(8,128)(2,1)S(1)}, u32[]{:S(2)}, u32[]{:S(2)}) collective-permute-start(bf16[256,512]{1,0:T(8,128)(2,1)} %bitcast.14), channel_id=1, source_target_pairs={{0,8},{8,0},{16,24},{24,16},{1,9},{9,1},{17,25},{25,17},{2,10},{10... | collective-permute-start | bytes 786440 | tf_op jit(solution)/shard_map/ppermute | solution.py:555
  5.7 0.9 %copy-done = bf16[512,1536]{1,0:T(8,128)(2,1)S(1)} copy-done((bf16[512,1536]{1,0:T(8,128)(2,1)S(1)}, bf16[512,1536]{1,0:T(8,128)(2,1)}, u32[]{:S(2)}) %copy-start) | copy-done | bytes 1572888
  6.6 1.9 %shard_map.101 = (bf16[256,512]{1,0:T(8,128)(2,1)S(1)}, bf16[256,512]{1,0:T(8,128)(2,1)S(1)}, bf16[256,512]{1,0:T(8,128)(2,1)S(1)}, bf16[16,256,256]{2,1,0:T(8,1...) custom-call(bf16[256,512]{1,0:T(8,128)(2,1)S(1)} %bitcast.16, ...), custom_call_target="tpu_custom_call" | custom-call | flops 2147483648 | bytes 4194304 | tf_op jit(solution)/shard_map/pallas_call | solution.py:617
  8.6 1.0 %collective-permute-done.refs_3_.refs_0_ = bf16[256,512]{1,0:T(8,128)(2,1)S(1)} collective-permute-done((bf16[256,512]{1,0:T(8,128)(2,1)}, bf16[256,512]{1,0:T(8,128)(2,1)S(1)}, u32[]{:S(2)}, u32[]{:S(2)}) %collective-permute-start) | collective-permute-done | bytes 262176 | tf_op jit(solution)/shard_map/ppermute | solution.py:555
  9.5 1.8 %shard_map.103 = (bf16[256,512]{1,0:T(8,128)(2,1)S(1)}, bf16[256,512]{1,0:T(8,128)(2,1)S(1)}, bf16[16,256,256]{2,1,0:T(8,128)(2,1)S(1)}, f32[256,512]{1,0:T(8,128)S(1)}, f32[256,512]{1,0:T(8,128)S(1)}) custom-call(bf16[256,512]{1,0:T(8,128)(2,1)S(1)} %collective-permute-done.refs_3_.refs_0_, f32[1,512]{1,0:T(1,128)S(1)} %bitcast.9, ...), custom_call_target="tpu_custom_call" | custom-call | flops 2147483648 | bytes 4194304 | tf_op jit(solution)/shard_map/pallas_call | solution.py:625
  11.3 1.1 %collective-permute-done.1.refs_4_.refs_0_ = bf16[256,512]{1,0:T(8,128)(2,1)S(1)} collective-permute-done((bf16[256,512]{1,0:T(8,128)(2,1)}, bf16[256,512]{1,0:T(8,128)(2,1)S(1)}, u32[]{:S(2)}, u32[]{:S(2)}) %collective-permute-start.1) | collective-permute-done | bytes 262176 | tf_op jit(solution)/shard_map/ppermute | solution.py:555
  12.4 1.8 %shard_map.104 = (bf16[256,512]{1,0:T(8,128)(2,1)S(1)}, bf16[256,512]{1,0:T(8,128)(2,1)S(1)}, bf16[16,256,256]{2,1,0:T(8,128)(2,1)S(1)}, f32[256,512]{1,0:T(8,128)S(1)}, f32[256,512]{1,0:T(8,128)S(1)}) custom-call(bf16[256,512]{1,0:T(8,128)(2,1)S(1)} %collective-permute-done.1.refs_4_.refs_0_, f32[1,512]{1,0:T(1,128)S(1)} %bitcast.10, ...), custom_call_target="tpu_custom_call" | custom-call | flops 2147483648 | bytes 4194304 | tf_op jit(solution)/shard_map/pallas_call | solution.py:625
  14.2 2.1 %collective-permute-done.2.refs_5_.refs_15_ = bf16[256,512]{1,0:T(8,128)(2,1)S(1)} collective-permute-done((bf16[256,512]{1,0:T(8,128)(2,1)}, bf16[256,512]{1,0:T(8,128)(2,1)S(1)}, u32[]{:S(2)}, u32[]{:S(2)}) %collective-permute-start.2) | collective-permute-done | bytes 262176 | tf_op jit(solution)/shard_map/ppermute | solution.py:555
  16.4 2.8 %shard_map.105 = (bf16[256,512]{1,0:T(8,128)(2,1)S(1)}, bf16[256,512]{1,0:T(8,128)(2,1)S(1)}, bf16[16,256,256]{2,1,0:T(8,128)(2,1)S(1)}, bf16[256,512]{1,0:T(8,1...) custom-call(bf16[256,512]{1,0:T(8,128)(2,1)S(1)} %bitcast.17, ...), custom_call_target="tpu_custom_call", output_to_operand_aliasing={{6}: (16, {}), {7}: (17, {}), {8}: (18, {})} | custom-call | flops 8589934592 | bytes 8388608 | tf_op jit(solution)/shard_map/pallas_call | solution.py:640
  19.1 1.2 %collective-permute-start.10 = (bf16[264,128]{1,0:T(8,128)(2,1)S(1)}, bf16[264,128]{1,0:T(8,128)(2,1)S(1)}, u32[]{:S(2)}, u32[]{:S(2)}) collective-permute-start(bf16[264,128]{1,0:T(8,128)(2,1)S(1)} %get-tuple-element.109), channel_id=1, source_target_pairs={{0,5},{1,4},{2,7},{3,6},{4,1},{5,0},{6,3},{7,2},{8,13},{9,12},{10,... | collective-permute-start | bytes 202760 | tf_op jit(solution)/shard_map/ppermute | solution.py:555
  20.3 2.8 %collective-permute-start.11 = (bf16[264,128]{1,0:T(8,128)(2,1)S(1)}, bf16[264,128]{1,0:T(8,128)(2,1)S(1)}, u32[]{:S(2)}, u32[]{:S(2)}) collective-permute-start(bf16[264,128]{1,0:T(8,128)(2,1)S(1)} %get-tuple-element.110), channel_id=1, source_target_pairs={{0,6},{1,7},{2,4},{3,5},{4,2},{5,3},{6,0},{7,1},{8,14},{9,15},{10,... | collective-permute-start | bytes 202760 | tf_op jit(solution)/shard_map/ppermute | solution.py:555
  23.1 2.2 %collective-permute-start.12 = (bf16[264,128]{1,0:T(8,128)(2,1)S(1)}, bf16[264,128]{1,0:T(8,128)(2,1)S(1)}, u32[]{:S(2)}, u32[]{:S(2)}) collective-permute-start(bf16[264,128]{1,0:T(8,128)(2,1)S(1)} %get-tuple-element.111), channel_id=1, source_target_pairs={{0,7},{1,6},{2,5},{3,4},{4,3},{5,2},{6,1},{7,0},{8,15},{9,14},{10,... | collective-permute-start | bytes 202760 | tf_op jit(solution)/shard_map/ppermute | solution.py:555
  25.3 2.8 %collective-permute-start.8 = (bf16[264,128]{1,0:T(8,128)(2,1)S(1)}, bf16[264,128]{1,0:T(8,128)(2,1)S(1)}, u32[]{:S(2)}, u32[]{:S(2)}) collective-permute-start(bf16[264,128]{1,0:T(8,128)(2,1)S(1)} %get-tuple-element.107), channel_id=1, source_target_pairs={{0,3},{1,2},{2,1},{3,0},{4,7},{5,6},{6,5},{7,4},{8,11},{9,10},{10,... | collective-permute-start | bytes 202760 | tf_op jit(solution)/shard_map/ppermute | solution.py:555
  28.1 3.6 %collective-permute-start.9 = (bf16[264,128]{1,0:T(8,128)(2,1)S(1)}, bf16[264,128]{1,0:T(8,128)(2,1)S(1)}, u32[]{:S(2)}, u32[]{:S(2)}) collective-permute-start(bf16[264,128]{1,0:T(8,128)(2,1)S(1)} %get-tuple-element.108), channel_id=1, source_target_pairs={{0,4},{1,5},{2,6},{3,7},{4,0},{5,1},{6,2},{7,3},{8,12},{9,13},{10,... | collective-permute-start | bytes 202760 | tf_op jit(solution)/shard_map/ppermute | solution.py:555
  32.3 3.5 %collective-permute-done.9.refs_10_ = bf16[264,128]{1,0:T(8,128)(2,1)S(1)} collective-permute-done((bf16[264,128]{1,0:T(8,128)(2,1)S(1)}, bf16[264,128]{1,0:T(8,128)(2,1)S(1)}, u32[]{:S(2)}, u32[]{:S(2)}) %collective-permute-start.9) | collective-permute-done | bytes 67616 | tf_op jit(solution)/shard_map/ppermute | solution.py:555
  35.9 5.6 %shard_map.108 = (bf16[64,512]{1,0:T(8,128)(2,1)S(1)}, bf16[64,512]{1,0:T(8,128)(2,1)S(1)}, bf16[64,512]{1,0:T(8,128)(2,1)S(1)}, bf16[64,512]{1,0:T(8,128)(2,1)S...) custom-call(f32[1,512]{1,0:T(1,128)S(1)} %get-tuple-element.75.refs_, ...), custom_call_target="tpu_custom_call" | custom-call | flops 8589934592 | bytes 4194304 | tf_op jit(solution)/shard_map/pallas_call | solution.py:694
  41.9 1.9 %collective-permute-start.3 = (f32[16,256]{1,0:T(8,128)S(1)}, f32[16,256]{1,0:T(8,128)S(1)}, u32[]{:S(2)}, u32[]{:S(2)}) collective-permute-start(f32[16,256]{1,0:T(8,128)S(1)} %get-tuple-element.90.refs_2_), channel_id=1, source_target_pairs={{0,16},{8,24},{16,0},{24,8},{1,17},{9,25},{17,1},{25,9},{2,18},{10... | collective-permute-start | bytes 49160 | tf_op jit(solution)/shard_map/ppermute | solution.py:555
  43.9 1.5 %collective-permute-start.4 = (f32[16,256]{1,0:T(8,128)S(1)}, f32[16,256]{1,0:T(8,128)S(1)}, u32[]{:S(2)}, u32[]{:S(2)}) collective-permute-start(f32[16,256]{1,0:T(8,128)S(1)} %get-tuple-element.90.refs_2_), channel_id=1, source_target_pairs={{0,8},{8,0},{16,24},{24,16},{1,9},{9,1},{17,25},{25,17},{2,10},{10... | collective-permute-start | bytes 49160 | tf_op jit(solution)/shard_map/ppermute | solution.py:555
  46.8 1.0 %collective-permute-done.4.refs_4_ = f32[16,256]{1,0:T(8,128)S(1)} collective-permute-done((f32[16,256]{1,0:T(8,128)S(1)}, f32[16,256]{1,0:T(8,128)S(1)}, u32[]{:S(2)}, u32[]{:S(2)}) %collective-permute-start.4) | collective-permute-done | bytes 16416 | tf_op jit(solution)/shard_map/ppermute | solution.py:555
  47.8 0.8 %collective-permute-start.16 = (bf16[64,512]{1,0:T(8,128)(2,1)S(1)}, bf16[64,512]{1,0:T(8,128)(2,1)S(1)}, u32[]{:S(2)}, u32[]{:S(2)}) collective-permute-start(bf16[64,512]{1,0:T(8,128)(2,1)S(1)} %get-tuple-element.116), channel_id=1, source_target_pairs={{0,4},{1,5},{2,6},{3,7},{4,0},{5,1},{6,2},{7,3},{8,12},{9,13},{10,... | collective-permute-start | bytes 196616 | tf_op jit(solution)/shard_map/ppermute | solution.py:555
  48.6 1.5 %collective-permute-done.5.refs_5_ = f32[16,256]{1,0:T(8,128)S(1)} collective-permute-done((f32[16,256]{1,0:T(8,128)S(1)}, f32[16,256]{1,0:T(8,128)S(1)}, u32[]{:S(2)}, u32[]{:S(2)}) %collective-permute-start.5) | collective-permute-done | bytes 16416 | tf_op jit(solution)/shard_map/ppermute | solution.py:555
  50.3 2.1 %collective-permute-start.18 = (bf16[64,512]{1,0:T(8,128)(2,1)S(1)}, bf16[64,512]{1,0:T(8,128)(2,1)S(1)}, u32[]{:S(2)}, u32[]{:S(2)}) collective-permute-start(bf16[64,512]{1,0:T(8,128)(2,1)S(1)} %get-tuple-element.118), channel_id=1, source_target_pairs={{0,6},{1,7},{2,4},{3,5},{4,2},{5,3},{6,0},{7,1},{8,14},{9,15},{10,... | collective-permute-start | bytes 196616 | tf_op jit(solution)/shard_map/ppermute | solution.py:555
  52.3 1.9 %collective-permute-start.19 = (bf16[64,512]{1,0:T(8,128)(2,1)S(1)}, bf16[64,512]{1,0:T(8,128)(2,1)S(1)}, u32[]{:S(2)}, u32[]{:S(2)}) collective-permute-start(bf16[64,512]{1,0:T(8,128)(2,1)S(1)} %get-tuple-element.119), channel_id=1, source_target_pairs={{0,7},{1,6},{2,5},{3,4},{4,3},{5,2},{6,1},{7,0},{8,15},{9,14},{10,... | collective-permute-start | bytes 196616 | tf_op jit(solution)/shard_map/ppermute | solution.py:555
  54.2 2.3 %shard_map.106.refs_13_.refs_0_ = bf16[16,256,1024]{2,1,0:T(8,128)(2,1)S(1)} custom-call(bf16[256,512]{1,0:T(8,128)(2,1)S(1)} %get-tuple-element.72.refs_9_.refs_0_.refs_4_, bf16[1024,512]{1,0:T(8,128)(2,1)S(1)} %shard_map.102.refs_1_.refs_2_, f32[16,256]{1,0:T(8,128)S(1)} %get-tuple-element.90.refs_2_, f32[16,256]{1,0:T(8,128)S(1)} %collective-permute-done.3.refs_3_, ...), custom_call_target="tpu_custom_call" | custom-call | flops 4294967296 | bytes 10485760 | tf_op jit(solution)/shard_map/pallas_call | solution.py:684
  57.1 2.5 %collective-permute-done.17.refs_8_ = bf16[64,512]{1,0:T(8,128)(2,1)S(1)} collective-permute-done((bf16[64,512]{1,0:T(8,128)(2,1)S(1)}, bf16[64,512]{1,0:T(8,128)(2,1)S(1)}, u32[]{:S(2)}, u32[]{:S(2)}) %collective-permute-start.17) | collective-permute-done | bytes 65568 | tf_op jit(solution)/shard_map/ppermute | solution.py:555
  61.2 1.5 %collective-permute-start.21 = (bf16[272,512]{1,0:T(8,128)(2,1)S(1)}, bf16[272,512]{1,0:T(8,128)(2,1)S(1)}, u32[]{:S(2)}, u32[]{:S(2)}) collective-permute-start(bf16[272,512]{1,0:T(8,128)(2,1)S(1)} %get-tuple-element.120.refs_14_), channel_id=1, source_target_pairs={{0,8},{8,0},{16,24},{24,16},{1,9},{9,1},{17,25},{25,17},{2,10},{10... | collective-permute-start | bytes 835592 | tf_op jit(solution)/shard_map/ppermute | solution.py:555
  62.6 1.3 %collective-permute-start.22 = (bf16[272,512]{1,0:T(8,128)(2,1)S(1)}, bf16[272,512]{1,0:T(8,128)(2,1)S(1)}, u32[]{:S(2)}, u32[]{:S(2)}) collective-permute-start(bf16[272,512]{1,0:T(8,128)(2,1)S(1)} %get-tuple-element.120.refs_14_), channel_id=1, source_target_pairs={{0,24},{8,16},{16,8},{24,0},{1,25},{9,17},{17,9},{25,1},{2,26},{10... | collective-permute-start | bytes 835592 | tf_op jit(solution)/shard_map/ppermute | solution.py:555
  64.0 7.2 %shard_map.110 = (f32[256,512]{1,0:T(8,128)S(1)}, f32[256,512]{1,0:T(8,128)S(1)}, f32[256,512]{1,0:T(8,128)S(1)}) custom-call(bf16[16,256,256]{2,1,0:T(8,128)(2,1)S(1)} %get-tuple-element.91.refs_0_, bf16[16,256,256]{2,1,0:T(8,128)(2,1)S(1)} %get-tuple-element.92.refs_1_, bf16[16,256,256]{2,1,0:T(8,128)(2,1)S(1)} %get-tuple-element.93.refs_2_, ...), custom_call_target="tpu_custom_call" | custom-call | flops 8589934592 | bytes 10485760 | tf_op jit(solution)/shard_map/pallas_call | solution.py:719
  71.2 2.3 %shard_map.111 = (f32[256,512]{1,0:T(8,128)S(1)}, f32[256,512]{1,0:T(8,128)S(1)}) custom-call(bf16[16,256,1024]{2,1,0:T(8,128)(2,1)S(1)} %shard_map.106.refs_13_.refs_0_, bf16[256,512]{1,0:T(8,128)(2,1)S(1)} %get-tuple-element.84.refs_12_.refs_8_.refs_1_, bf16[1024,512]{1,0:T(8,128)(2,1)S(1)} %shard_map.102.refs_1_.refs_2_, ...), custom_call_target="tpu_custom_call" | custom-call | flops 2147483648 | bytes 4194304 | tf_op jit(solution)/shard_map/pallas_call | solution.py:731
  73.5 2.3 %shard_map.112 = (f32[256,512]{1,0:T(8,128)S(1)}, f32[256,512]{1,0:T(8,128)S(1)}) custom-call(bf16[16,256,1024]{2,1,0:T(8,128)(2,1)S(1)} %shard_map.106.refs_13_.refs_0_, bf16[256,512]{1,0:T(8,128)(2,1)S(1)} %get-tuple-element.84.refs_12_.refs_8_.refs_1_, bf16[1024,512]{1,0:T(8,128)(2,1)S(1)} %shard_map.102.refs_1_.refs_2_, ...), custom_call_target="tpu_custom_call" | custom-call | flops 2147483648 | bytes 4194304 | tf_op jit(solution)/shard_map/pallas_call | solution.py:731
  76.3 3.4 %shard_map.113 = bf16[256,512]{1,0:T(8,128)(2,1)} custom-call(bf16[16,256,1024]{2,1,0:T(8,128)(2,1)S(1)} %shard_map.106.refs_13_.refs_0_, bf16[256,512]{1,0:T(8,128)(2,1)S(1)} %get-tuple-element.84.refs_12_.refs_8_.refs_1_, bf16[1024,512]{1,0:T(8,128)(2,1)S(1)} %shard_map.102.refs_1_.refs_2_, f32[256,512]{1,0:T(8,128)S(1)} %get-tuple-element.121.refs_3_, ...), custom_call_target="tpu_custom_call" | custom-call | flops 8589934592 | bytes 14680064 | tf_op jit(solution)/shard_map/pallas_call | solution.py:738
  (48 shorter events, 6.6 us)
Async XLA Ops:
  0.0 9.5 %collective-permute-start = (bf16[256,512]{1,0:T(8,128)(2,1)}, bf16[256,512]{1,0:T(8,128)(2,1)S(1)}, u32[]{:S(2)}, u32[]{:S(2)}) collective-permute-start(bf16[256,512]{1,0:T(8,128)(2,1)} %bitcast.13), channel_id=1, source_target_pairs={{0,16},{8,24},{16,0},{24,8},{1,17},{9,25},{17,1},{25,9},{2,18},{10... | collective-permute-start | bytes 786440 | tf_op jit(solution)/shard_map/ppermute | solution.py:555
  3.0 9.4 %collective-permute-start.1 = (bf16[256,512]{1,0:T(8,128)(2,1)}, bf16[256,512]{1,0:T(8,128)(2,1)S(1)}, u32[]{:S(2)}, u32[]{:S(2)}) collective-permute-start(bf16[256,512]{1,0:T(8,128)(2,1)} %bitcast.14), channel_id=1, source_target_pairs={{0,8},{8,0},{16,24},{24,16},{1,9},{9,1},{17,25},{25,17},{2,10},{10... | collective-permute-start | bytes 786440 | tf_op jit(solution)/shard_map/ppermute | solution.py:555
  4.5 11.8 %collective-permute-start.2 = (bf16[256,512]{1,0:T(8,128)(2,1)}, bf16[256,512]{1,0:T(8,128)(2,1)S(1)}, u32[]{:S(2)}, u32[]{:S(2)}) collective-permute-start(bf16[256,512]{1,0:T(8,128)(2,1)} %bitcast.15), channel_id=1, source_target_pairs={{0,24},{8,16},{16,8},{24,0},{1,25},{9,17},{17,9},{25,1},{2,26},{10... | collective-permute-start | bytes 786440 | tf_op jit(solution)/shard_map/ppermute | solution.py:555
  5.2 1.4 %copy-start = (bf16[512,1536]{1,0:T(8,128)(2,1)S(1)}, bf16[512,1536]{1,0:T(8,128)(2,1)}, u32[]{:S(2)}) copy-start(bf16[512,1536]{1,0:T(8,128)(2,1)} %refs_8_.1) | copy-start | bytes 4718596
  5.2 1.4 %copy-start.1 = (f32[512]{0:T(512)S(1)}, f32[512]{0:T(512)}, u32[]{:S(2)}) copy-start(f32[512]{0:T(512)} %param.11) | copy-start | bytes 6148
  5.2 1.4 %copy-start.5 = (bf16[1,1,256,512]{3,2,1,0:T(8,128)(2,1)S(1)}, bf16[1,1,256,512]{3,2,1,0:T(8,128)(2,1)}, u32[]{:S(2)}) copy-start(bf16[1,1,256,512]{3,2,1,0:T(8,128)(2,1)} %param.10) | copy-start | bytes 786436
  12.4 3.9 %copy-start.4 = (bf16[512,512]{1,0:T(8,128)(2,1)S(1)}, bf16[512,512]{1,0:T(8,128)(2,1)}, u32[]{:S(2)}) copy-start(bf16[512,512]{1,0:T(8,128)(2,1)} %refs_2_.11) | copy-start | bytes 1572868
  16.3 15.3 %copy-start.3 = (bf16[512,512]{1,0:T(8,128)(2,1)S(1)}, bf16[512,512]{1,0:T(8,128)(2,1)}, u32[]{:S(2)}) copy-start(bf16[512,512]{1,0:T(8,128)(2,1)} %out_w_ref.1) | copy-start | bytes 1572868
  16.3 15.3 %copy-start.6 = (bf16[1,1,256,512]{3,2,1,0:T(8,128)(2,1)S(1)}, bf16[1,1,256,512]{3,2,1,0:T(8,128)(2,1)}, u32[]{:S(2)}) copy-start(bf16[1,1,256,512]{3,2,1,0:T(8,128)(2,1)} %param.19) | copy-start | bytes 786436
  16.3 15.3 %copy-start.9 = (s32[1,1,256]{2,1,0:T(1,128)S(1)}, s32[1,1,256]{2,1,0:T(1,128)}, u32[]{:S(2)}) copy-start(s32[1,1,256]{2,1,0:T(1,128)} %param.18) | copy-start | bytes 3076
  16.3 19.5 %copy-start.2 = (bf16[512,1536]{1,0:T(8,128)(2,1)S(1)}, bf16[512,1536]{1,0:T(8,128)(2,1)}, u32[]{:S(2)}) copy-start(bf16[512,1536]{1,0:T(8,128)(2,1)} %refs_2_.10) | copy-start | bytes 4718596
  16.3 19.5 %copy-start.7 = (f32[512]{0:T(512)S(1)}, f32[512]{0:T(512)}, u32[]{:S(2)}) copy-start(f32[512]{0:T(512)} %param.15) | copy-start | bytes 6148
  19.1 6.2 %collective-permute-start.10 = (bf16[264,128]{1,0:T(8,128)(2,1)S(1)}, bf16[264,128]{1,0:T(8,128)(2,1)S(1)}, u32[]{:S(2)}, u32[]{:S(2)}) collective-permute-start(bf16[264,128]{1,0:T(8,128)(2,1)S(1)} %get-tuple-element.109), channel_id=1, source_target_pairs={{0,5},{1,4},{2,7},{3,6},{4,1},{5,0},{6,3},{7,2},{8,13},{9,12},{10,... | collective-permute-start | bytes 202760 | tf_op jit(solution)/shard_map/ppermute | solution.py:555
  20.3 7.7 %collective-permute-start.11 = (bf16[264,128]{1,0:T(8,128)(2,1)S(1)}, bf16[264,128]{1,0:T(8,128)(2,1)S(1)}, u32[]{:S(2)}, u32[]{:S(2)}) collective-permute-start(bf16[264,128]{1,0:T(8,128)(2,1)S(1)} %get-tuple-element.110), channel_id=1, source_target_pairs={{0,6},{1,7},{2,4},{3,5},{4,2},{5,3},{6,0},{7,1},{8,14},{9,15},{10,... | collective-permute-start | bytes 202760 | tf_op jit(solution)/shard_map/ppermute | solution.py:555
  23.1 8.9 %collective-permute-start.12 = (bf16[264,128]{1,0:T(8,128)(2,1)S(1)}, bf16[264,128]{1,0:T(8,128)(2,1)S(1)}, u32[]{:S(2)}, u32[]{:S(2)}) collective-permute-start(bf16[264,128]{1,0:T(8,128)(2,1)S(1)} %get-tuple-element.111), channel_id=1, source_target_pairs={{0,7},{1,6},{2,5},{3,4},{4,3},{5,2},{6,1},{7,0},{8,15},{9,14},{10,... | collective-permute-start | bytes 202760 | tf_op jit(solution)/shard_map/ppermute | solution.py:555
  25.3 6.7 %collective-permute-start.6 = (bf16[264,128]{1,0:T(8,128)(2,1)S(1)}, bf16[264,128]{1,0:T(8,128)(2,1)S(1)}, u32[]{:S(2)}, u32[]{:S(2)}) collective-permute-start(bf16[264,128]{1,0:T(8,128)(2,1)S(1)} %get-tuple-element.105), channel_id=1, source_target_pairs={{0,1},{1,0},{2,3},{3,2},{4,5},{5,4},{6,7},{7,6},{8,9},{9,8},{10,11... | collective-permute-start | bytes 202760 | tf_op jit(solution)/shard_map/ppermute | solution.py:555
  25.3 6.7 %collective-permute-start.7 = (bf16[264,128]{1,0:T(8,128)(2,1)S(1)}, bf16[264,128]{1,0:T(8,128)(2,1)S(1)}, u32[]{:S(2)}, u32[]{:S(2)}) collective-permute-start(bf16[264,128]{1,0:T(8,128)(2,1)S(1)} %get-tuple-element.106), channel_id=1, source_target_pairs={{0,2},{1,3},{2,0},{3,1},{4,6},{5,7},{6,4},{7,5},{8,10},{9,11},{10,... | collective-permute-start | bytes 202760 | tf_op jit(solution)/shard_map/ppermute | solution.py:555
  25.3 7.0 %collective-permute-start.8 = (bf16[264,128]{1,0:T(8,128)(2,1)S(1)}, bf16[264,128]{1,0:T(8,128)(2,1)S(1)}, u32[]{:S(2)}, u32[]{:S(2)}) collective-permute-start(bf16[264,128]{1,0:T(8,128)(2,1)S(1)} %get-tuple-element.107), channel_id=1, source_target_pairs={{0,3},{1,2},{2,1},{3,0},{4,7},{5,6},{6,5},{7,4},{8,11},{9,10},{10,... | collective-permute-start | bytes 202760 | tf_op jit(solution)/shard_map/ppermute | solution.py:555
  28.1 7.8 %collective-permute-start.9 = (bf16[264,128]{1,0:T(8,128)(2,1)S(1)}, bf16[264,128]{1,0:T(8,128)(2,1)S(1)}, u32[]{:S(2)}, u32[]{:S(2)}) collective-permute-start(bf16[264,128]{1,0:T(8,128)(2,1)S(1)} %get-tuple-element.108), channel_id=1, source_target_pairs={{0,4},{1,5},{2,6},{3,7},{4,0},{5,1},{6,2},{7,3},{8,12},{9,13},{10,... | collective-permute-start | bytes 202760 | tf_op jit(solution)/shard_map/ppermute | solution.py:555
  41.4 8.8 %collective-permute-start.13 = (bf16[64,512]{1,0:T(8,128)(2,1)S(1)}, bf16[64,512]{1,0:T(8,128)(2,1)S(1)}, u32[]{:S(2)}, u32[]{:S(2)}) collective-permute-start(bf16[64,512]{1,0:T(8,128)(2,1)S(1)} %get-tuple-element.113), channel_id=1, source_target_pairs={{0,1},{1,0},{2,3},{3,2},{4,5},{5,4},{6,7},{7,6},{8,9},{9,8},{10,11... | collective-permute-start | bytes 196616 | tf_op jit(solution)/shard_map/ppermute | solution.py:555
  41.6 10.7 %collective-permute-start.14 = (bf16[64,512]{1,0:T(8,128)(2,1)S(1)}, bf16[64,512]{1,0:T(8,128)(2,1)S(1)}, u32[]{:S(2)}, u32[]{:S(2)}) collective-permute-start(bf16[64,512]{1,0:T(8,128)(2,1)S(1)} %get-tuple-element.114), channel_id=1, source_target_pairs={{0,2},{1,3},{2,0},{3,1},{4,6},{5,7},{6,4},{7,5},{8,10},{9,11},{10,... | collective-permute-start | bytes 196616 | tf_op jit(solution)/shard_map/ppermute | solution.py:555
  41.9 4.2 %collective-permute-start.3 = (f32[16,256]{1,0:T(8,128)S(1)}, f32[16,256]{1,0:T(8,128)S(1)}, u32[]{:S(2)}, u32[]{:S(2)}) collective-permute-start(f32[16,256]{1,0:T(8,128)S(1)} %get-tuple-element.90.refs_2_), channel_id=1, source_target_pairs={{0,16},{8,24},{16,0},{24,8},{1,17},{9,25},{17,1},{25,9},{2,18},{10... | collective-permute-start | bytes 49160 | tf_op jit(solution)/shard_map/ppermute | solution.py:555
  43.9 3.9 %collective-permute-start.4 = (f32[16,256]{1,0:T(8,128)S(1)}, f32[16,256]{1,0:T(8,128)S(1)}, u32[]{:S(2)}, u32[]{:S(2)}) collective-permute-start(f32[16,256]{1,0:T(8,128)S(1)} %get-tuple-element.90.refs_2_), channel_id=1, source_target_pairs={{0,8},{8,0},{16,24},{24,16},{1,9},{9,1},{17,25},{25,17},{2,10},{10... | collective-permute-start | bytes 49160 | tf_op jit(solution)/shard_map/ppermute | solution.py:555
  45.4 4.6 %collective-permute-start.5 = (f32[16,256]{1,0:T(8,128)S(1)}, f32[16,256]{1,0:T(8,128)S(1)}, u32[]{:S(2)}, u32[]{:S(2)}) collective-permute-start(f32[16,256]{1,0:T(8,128)S(1)} %get-tuple-element.90.refs_2_), channel_id=1, source_target_pairs={{0,24},{8,16},{16,8},{24,0},{1,25},{9,17},{17,9},{25,1},{2,26},{10... | collective-permute-start | bytes 49160 | tf_op jit(solution)/shard_map/ppermute | solution.py:555
  46.1 10.5 %collective-permute-start.15 = (bf16[64,512]{1,0:T(8,128)(2,1)S(1)}, bf16[64,512]{1,0:T(8,128)(2,1)S(1)}, u32[]{:S(2)}, u32[]{:S(2)}) collective-permute-start(bf16[64,512]{1,0:T(8,128)(2,1)S(1)} %get-tuple-element.115), channel_id=1, source_target_pairs={{0,3},{1,2},{2,1},{3,0},{4,7},{5,6},{6,5},{7,4},{8,11},{9,10},{10,... | collective-permute-start | bytes 196616 | tf_op jit(solution)/shard_map/ppermute | solution.py:555
  47.8 9.4 %collective-permute-start.16 = (bf16[64,512]{1,0:T(8,128)(2,1)S(1)}, bf16[64,512]{1,0:T(8,128)(2,1)S(1)}, u32[]{:S(2)}, u32[]{:S(2)}) collective-permute-start(bf16[64,512]{1,0:T(8,128)(2,1)S(1)} %get-tuple-element.116), channel_id=1, source_target_pairs={{0,4},{1,5},{2,6},{3,7},{4,0},{5,1},{6,2},{7,3},{8,12},{9,13},{10,... | collective-permute-start | bytes 196616 | tf_op jit(solution)/shard_map/ppermute | solution.py:555
  50.0 9.6 %collective-permute-start.17 = (bf16[64,512]{1,0:T(8,128)(2,1)S(1)}, bf16[64,512]{1,0:T(8,128)(2,1)S(1)}, u32[]{:S(2)}, u32[]{:S(2)}) collective-permute-start(bf16[64,512]{1,0:T(8,128)(2,1)S(1)} %get-tuple-element.117), channel_id=1, source_target_pairs={{0,5},{1,4},{2,7},{3,6},{4,1},{5,0},{6,3},{7,2},{8,13},{9,12},{10,... | collective-permute-start | bytes 196616 | tf_op jit(solution)/shard_map/ppermute | solution.py:555
  50.3 9.4 %collective-permute-start.18 = (bf16[64,512]{1,0:T(8,128)(2,1)S(1)}, bf16[64,512]{1,0:T(8,128)(2,1)S(1)}, u32[]{:S(2)}, u32[]{:S(2)}) collective-permute-start(bf16[64,512]{1,0:T(8,128)(2,1)S(1)} %get-tuple-element.118), channel_id=1, source_target_pairs={{0,6},{1,7},{2,4},{3,5},{4,2},{5,3},{6,0},{7,1},{8,14},{9,15},{10,... | collective-permute-start | bytes 196616 | tf_op jit(solution)/shard_map/ppermute | solution.py:555
  52.3 7.3 %collective-permute-start.19 = (bf16[64,512]{1,0:T(8,128)(2,1)S(1)}, bf16[64,512]{1,0:T(8,128)(2,1)S(1)}, u32[]{:S(2)}, u32[]{:S(2)}) collective-permute-start(bf16[64,512]{1,0:T(8,128)(2,1)S(1)} %get-tuple-element.119), channel_id=1, source_target_pairs={{0,7},{1,6},{2,5},{3,4},{4,3},{5,2},{6,1},{7,0},{8,15},{9,14},{10,... | collective-permute-start | bytes 196616 | tf_op jit(solution)/shard_map/ppermute | solution.py:555
  60.4 10.7 %collective-permute-start.20 = (bf16[272,512]{1,0:T(8,128)(2,1)S(1)}, bf16[272,512]{1,0:T(8,128)(2,1)S(1)}, u32[]{:S(2)}, u32[]{:S(2)}) collective-permute-start(bf16[272,512]{1,0:T(8,128)(2,1)S(1)} %get-tuple-element.120.refs_14_), channel_id=1, source_target_pairs={{0,16},{8,24},{16,0},{24,8},{1,17},{9,25},{17,1},{25,9},{2,18},{10... | collective-permute-start | bytes 835592 | tf_op jit(solution)/shard_map/ppermute | solution.py:555
  61.2 12.3 %collective-permute-start.21 = (bf16[272,512]{1,0:T(8,128)(2,1)S(1)}, bf16[272,512]{1,0:T(8,128)(2,1)S(1)}, u32[]{:S(2)}, u32[]{:S(2)}) collective-permute-start(bf16[272,512]{1,0:T(8,128)(2,1)S(1)} %get-tuple-element.120.refs_14_), channel_id=1, source_target_pairs={{0,8},{8,0},{16,24},{24,16},{1,9},{9,1},{17,25},{25,17},{2,10},{10... | collective-permute-start | bytes 835592 | tf_op jit(solution)/shard_map/ppermute | solution.py:555
  62.6 13.7 %collective-permute-start.22 = (bf16[272,512]{1,0:T(8,128)(2,1)S(1)}, bf16[272,512]{1,0:T(8,128)(2,1)S(1)}, u32[]{:S(2)}, u32[]{:S(2)}) collective-permute-start(bf16[272,512]{1,0:T(8,128)(2,1)S(1)} %get-tuple-element.120.refs_14_), channel_id=1, source_target_pairs={{0,24},{8,16},{16,8},{24,0},{1,25},{9,17},{17,9},{25,1},{2,26},{10... | collective-permute-start | bytes 835592 | tf_op jit(solution)/shard_map/ppermute | solution.py:555
  (1 other events, 0.7 us)

commit v3 on v2

--- a/solution.py
+++ b/solution.py
@@ -398,7 +398,7 @@
 def home_body(chunks, depth, *refs):
     take_ref, mixed_ref, out_w_ref = refs[:3]
     home = refs[3 : 3 + chunks]
-    moved_ref, grad_ref = refs[3 + chunks :]
+    moved_ref, grad_ref, delta_ref = refs[3 + chunks :]
     count, width = moved_ref.shape
     rows = jnp.concatenate([piece[...] for piece in home], axis=0)
     moved = dot_nn(take_ref[...], rows).astype(BF16)
@@ -413,10 +413,13 @@
         lax.broadcasted_iota(jnp.int32, (heads, width), 0)
     )
     pick = pick.astype(F32).astype(BF16)
-    rows = dot_nt(pick, high) + dot_nt(pick, low)
-    rows_high = rows.astype(BF16)
-    grad_ref[count:, :count] = rows_high
-    grad_ref[count:, count:] = (rows - rows_high.astype(F32)).astype(BF16)
+    delta = dot_nt(pick, high) + dot_nt(pick, low)
+    delta_ref[...] = delta
+    beside = width // count
+    tail = heads // beside
+    for part in range(beside):
+        lines = delta[part * tail : (part + 1) * tail].astype(BF16)
+        grad_ref[count:, part * count : (part + 1) * count] = lines
 
 
 def key_tile(depth, t, v_tile, weights_ref, columns, queries, grads, deltas_ref):
@@ -436,21 +439,22 @@
     return dk, dv
 
 
-def halves(lines):
-    half = lines.shape[1] // 2
-    return lines[:, :half], lines[:, half:]
+def heads_apart(lines, count):
+    wide = lines.astype(F32)
+    parts = [wide[:, i * count : (i + 1) * count] for i in range(lines.shape[1] // count)]
+    return jnp.concatenate(parts, axis=0)
 
 
 def query_grad_body(parts, depth, *refs):
     weights_refs, refs = refs[:parts], refs[parts:]
     keys_refs, refs = refs[:parts], refs[parts:]
     values_refs, refs = refs[:parts], refs[parts:]
-    inverse_ref, flipped_ref, grad_ref, q_ref, w_ref = refs[:5]
-    normed_ref, dk_ref, dv_ref, dq_all, lines, wide = refs[5:]
+    inverse_ref, flipped_ref, grad_ref, lines, q_ref, w_ref = refs[:6]
+    normed_ref, dk_ref, dv_ref, dq_all, wide = refs[6:]
     count, width = q_ref.shape
     heads = LANES // depth
-    high, low = halves(grad_ref[count:])
-    lines[...] = high.astype(F32) + low.astype(F32)
+    high = lines[...].astype(BF16)
+    low = (lines[...] - high.astype(F32)).astype(BF16)
     wide[...] = spread(high, width) + spread(low, width)
 
     def tile_step(t, carry):
@@ -488,8 +492,7 @@
     flipped_ref, v_ref, queries_ref, dk_in_ref, dv_in_ref, grad_ref = refs[:6]
     dk_ref, dv_ref, lines = refs[6:]
     count, width = v_ref.shape
-    high, low = halves(grad_ref[count:])
-    lines[...] = high.astype(F32) + low.astype(F32)
+    lines[...] = heads_apart(grad_ref[count:], count)
     rows = slice(index * count, (index + 1) * count)
 
     def tile_step(t, carry):
@@ -520,8 +523,7 @@
     for i, other in enumerate(others):
         rows = slice(i * count, (i + 1) * count)
         grads[rows] = other[:count]
-        high, low = halves(other[count:])
-        lines[:, rows] = high.astype(F32) + low.astype(F32)
+        lines[:, rows] = heads_apart(other[count:], count)
 
     def tile_step(t, carry):
         at = tile_at(t)
@@ -708,9 +710,9 @@
     )
     home = exchange(returning, "curve")
 
-    moved_grad, grad_own = vmem_call(
+    moved_grad, grad_own, delta = vmem_call(
         functools.partial(home_body, chunks, depth),
-        (rows_bf16, shape(BF16, count + HEADS, width)),
+        (rows_bf16, shape(BF16, count + HEADS * count // width, width), lines_f32),
         flops=1 << 29,
         moved=2 << 20,
     )(take, mixed, out_one, *home)
@@ -721,12 +723,11 @@
         (rows_f32, rows_f32, rows_f32),
         [
             pltpu.VMEM((count, width), BF16),
-            pltpu.VMEM((HEADS, count), F32),
             pltpu.VMEM((count, width), F32),
         ],
         flops=8 << 30,
         moved=10 << 20,
-    )(*all_weights, *all_keys, *all_values, inverse, flipped, grad_own, q, qkv_one)
+    )(*all_weights, *all_keys, *all_values, inverse, flipped, grad_own, delta, q, qkv_one)
     for index in range(1, early):
         key_grad, value_grad = vmem_call(
             functools.partial(key_middle_body, index, depth),

time: 80.2 us -> 79.9 us (level)
  no operation moved by 1% of the time
where the time goes in v3:
time: 79.9 us; the launch traced here: 79.4 us
  Pallas kernels  33.8 us (42%)
  starting transfers between devices  30.1 us (38%)
  waiting for transfers between devices  13.7 us (17%)
  local copies, waits for them, and re-layouts  1.61 us (2%)
    ppermute x23, starting transfers between devices, by_xor(): return lax.ppermute(array, axis, [(i, i ^ step) for i in range(size)])  30.1 us
    ppermute x23, waiting for transfers between devices, by_xor(): return lax.ppermute(array, axis, [(i, i ^ step) for i in range(size)])  13.7 us
    pallas_call x1, Pallas kernels, shards(): vmem_call(functools.partial(query_grad_body, len(all_keys), depth), (rows...  7.27 us
    pallas_call x1, Pallas kernels, shards(): vmem_call(functools.partial(second_body, chunks, depth), (chunk_bf16,) *...  5.58 us
    pallas_call x2, Pallas kernels, shards(): vmem_call(functools.partial(key_middle_body, index, depth), (rows_f32, ro...  4.55 us
    pallas_call x2, Pallas kernels, shards(): vmem_call(functools.partial(middle_body, depth), (rows_bf16,) * 2 + (squa...  3.57 us
    pallas_call x1, Pallas kernels, shards(): vmem_call(functools.partial(key_grad_body, early, peers, depth), rows_bf1...  3.44 us
    pallas_call x1, Pallas kernels, shards(): vmem_call(functools.partial(forward_body, early, peers, chunks, capacity,...  2.78 us
  transfers between devices with their start and end apart: 23, of which 10 were waited for; matrix products, arithmetic and copies ran while one was open for 0% of the time, Pallas kernels for 27%

profile of v3, /device:TPU:0, one launch (start us, length us, event | category | flops | bytes accessed | tf_op | source)
XLA Modules:
  0.0 79.4 jit_solution(13805566876660369052)
XLA Ops:
  0.0 3.0 %collective-permute-start = (bf16[256,512]{1,0:T(8,128)(2,1)}, bf16[256,512]{1,0:T(8,128)(2,1)S(1)}, u32[]{:S(2)}, u32[]{:S(2)}) collective-permute-start(bf16[256,512]{1,0:T(8,128)(2,1)} %bitcast.13), channel_id=1, source_target_pairs={{0,16},{8,24},{16,0},{24,8},{1,17},{9,25},{17,1},{25,9},{2,18},{10... | collective-permute-start | bytes 786440 | tf_op jit(solution)/shard_map/ppermute | solution.py:557
  3.0 1.5 %collective-permute-start.1 = (bf16[256,512]{1,0:T(8,128)(2,1)}, bf16[256,512]{1,0:T(8,128)(2,1)S(1)}, u32[]{:S(2)}, u32[]{:S(2)}) collective-permute-start(bf16[256,512]{1,0:T(8,128)(2,1)} %bitcast.14), channel_id=1, source_target_pairs={{0,8},{8,0},{16,24},{24,16},{1,9},{9,1},{17,25},{25,17},{2,10},{10... | collective-permute-start | bytes 786440 | tf_op jit(solution)/shard_map/ppermute | solution.py:557
  5.7 0.9 %copy-done = bf16[512,1536]{1,0:T(8,128)(2,1)S(1)} copy-done((bf16[512,1536]{1,0:T(8,128)(2,1)S(1)}, bf16[512,1536]{1,0:T(8,128)(2,1)}, u32[]{:S(2)}) %copy-start) | copy-done | bytes 1572888
  6.6 1.9 %shard_map.101 = (bf16[256,512]{1,0:T(8,128)(2,1)S(1)}, bf16[256,512]{1,0:T(8,128)(2,1)S(1)}, bf16[256,512]{1,0:T(8,128)(2,1)S(1)}, bf16[16,256,256]{2,1,0:T(8,1...) custom-call(bf16[256,512]{1,0:T(8,128)(2,1)S(1)} %bitcast.16, ...), custom_call_target="tpu_custom_call" | custom-call | flops 2147483648 | bytes 4194304 | tf_op jit(solution)/shard_map/pallas_call | solution.py:619
  8.6 1.0 %collective-permute-done.refs_3_.refs_0_ = bf16[256,512]{1,0:T(8,128)(2,1)S(1)} collective-permute-done((bf16[256,512]{1,0:T(8,128)(2,1)}, bf16[256,512]{1,0:T(8,128)(2,1)S(1)}, u32[]{:S(2)}, u32[]{:S(2)}) %collective-permute-start) | collective-permute-done | bytes 262176 | tf_op jit(solution)/shard_map/ppermute | solution.py:557
  9.5 1.8 %shard_map.103 = (bf16[256,512]{1,0:T(8,128)(2,1)S(1)}, bf16[256,512]{1,0:T(8,128)(2,1)S(1)}, bf16[16,256,256]{2,1,0:T(8,128)(2,1)S(1)}, f32[256,512]{1,0:T(8,128)S(1)}, f32[256,512]{1,0:T(8,128)S(1)}) custom-call(bf16[256,512]{1,0:T(8,128)(2,1)S(1)} %collective-permute-done.refs_3_.refs_0_, f32[1,512]{1,0:T(1,128)S(1)} %bitcast.9, ...), custom_call_target="tpu_custom_call" | custom-call | flops 2147483648 | bytes 4194304 | tf_op jit(solution)/shard_map/pallas_call | solution.py:627
  11.3 1.1 %collective-permute-done.1.refs_4_.refs_0_ = bf16[256,512]{1,0:T(8,128)(2,1)S(1)} collective-permute-done((bf16[256,512]{1,0:T(8,128)(2,1)}, bf16[256,512]{1,0:T(8,128)(2,1)S(1)}, u32[]{:S(2)}, u32[]{:S(2)}) %collective-permute-start.1) | collective-permute-done | bytes 262176 | tf_op jit(solution)/shard_map/ppermute | solution.py:557
  12.4 1.8 %shard_map.104 = (bf16[256,512]{1,0:T(8,128)(2,1)S(1)}, bf16[256,512]{1,0:T(8,128)(2,1)S(1)}, bf16[16,256,256]{2,1,0:T(8,128)(2,1)S(1)}, f32[256,512]{1,0:T(8,128)S(1)}, f32[256,512]{1,0:T(8,128)S(1)}) custom-call(bf16[256,512]{1,0:T(8,128)(2,1)S(1)} %collective-permute-done.1.refs_4_.refs_0_, f32[1,512]{1,0:T(1,128)S(1)} %bitcast.10, ...), custom_call_target="tpu_custom_call" | custom-call | flops 2147483648 | bytes 4194304 | tf_op jit(solution)/shard_map/pallas_call | solution.py:627
  14.2 2.1 %collective-permute-done.2.refs_5_.refs_15_ = bf16[256,512]{1,0:T(8,128)(2,1)S(1)} collective-permute-done((bf16[256,512]{1,0:T(8,128)(2,1)}, bf16[256,512]{1,0:T(8,128)(2,1)S(1)}, u32[]{:S(2)}, u32[]{:S(2)}) %collective-permute-start.2) | collective-permute-done | bytes 262176 | tf_op jit(solution)/shard_map/ppermute | solution.py:557
  16.4 2.8 %shard_map.105 = (bf16[256,512]{1,0:T(8,128)(2,1)S(1)}, bf16[256,512]{1,0:T(8,128)(2,1)S(1)}, bf16[16,256,256]{2,1,0:T(8,128)(2,1)S(1)}, bf16[256,512]{1,0:T(8,1...) custom-call(bf16[256,512]{1,0:T(8,128)(2,1)S(1)} %bitcast.17, ...), custom_call_target="tpu_custom_call", output_to_operand_aliasing={{6}: (16, {}), {7}: (17, {}), {8}: (18, {})} | custom-call | flops 8589934592 | bytes 8388608 | tf_op jit(solution)/shard_map/pallas_call | solution.py:642
  19.1 1.2 %collective-permute-start.10 = (bf16[264,128]{1,0:T(8,128)(2,1)S(1)}, bf16[264,128]{1,0:T(8,128)(2,1)S(1)}, u32[]{:S(2)}, u32[]{:S(2)}) collective-permute-start(bf16[264,128]{1,0:T(8,128)(2,1)S(1)} %get-tuple-element.110), channel_id=1, source_target_pairs={{0,5},{1,4},{2,7},{3,6},{4,1},{5,0},{6,3},{7,2},{8,13},{9,12},{10,... | collective-permute-start | bytes 202760 | tf_op jit(solution)/shard_map/ppermute | solution.py:557
  20.3 2.8 %collective-permute-start.11 = (bf16[264,128]{1,0:T(8,128)(2,1)S(1)}, bf16[264,128]{1,0:T(8,128)(2,1)S(1)}, u32[]{:S(2)}, u32[]{:S(2)}) collective-permute-start(bf16[264,128]{1,0:T(8,128)(2,1)S(1)} %get-tuple-element.111), channel_id=1, source_target_pairs={{0,6},{1,7},{2,4},{3,5},{4,2},{5,3},{6,0},{7,1},{8,14},{9,15},{10,... | collective-permute-start | bytes 202760 | tf_op jit(solution)/shard_map/ppermute | solution.py:557
  23.1 2.2 %collective-permute-start.12 = (bf16[264,128]{1,0:T(8,128)(2,1)S(1)}, bf16[264,128]{1,0:T(8,128)(2,1)S(1)}, u32[]{:S(2)}, u32[]{:S(2)}) collective-permute-start(bf16[264,128]{1,0:T(8,128)(2,1)S(1)} %get-tuple-element.112), channel_id=1, source_target_pairs={{0,7},{1,6},{2,5},{3,4},{4,3},{5,2},{6,1},{7,0},{8,15},{9,14},{10,... | collective-permute-start | bytes 202760 | tf_op jit(solution)/shard_map/ppermute | solution.py:557
  25.3 2.8 %collective-permute-start.8 = (bf16[264,128]{1,0:T(8,128)(2,1)S(1)}, bf16[264,128]{1,0:T(8,128)(2,1)S(1)}, u32[]{:S(2)}, u32[]{:S(2)}) collective-permute-start(bf16[264,128]{1,0:T(8,128)(2,1)S(1)} %get-tuple-element.108), channel_id=1, source_target_pairs={{0,3},{1,2},{2,1},{3,0},{4,7},{5,6},{6,5},{7,4},{8,11},{9,10},{10,... | collective-permute-start | bytes 202760 | tf_op jit(solution)/shard_map/ppermute | solution.py:557
  28.1 3.6 %collective-permute-start.9 = (bf16[264,128]{1,0:T(8,128)(2,1)S(1)}, bf16[264,128]{1,0:T(8,128)(2,1)S(1)}, u32[]{:S(2)}, u32[]{:S(2)}) collective-permute-start(bf16[264,128]{1,0:T(8,128)(2,1)S(1)} %get-tuple-element.109), channel_id=1, source_target_pairs={{0,4},{1,5},{2,6},{3,7},{4,0},{5,1},{6,2},{7,3},{8,12},{9,13},{10,... | collective-permute-start | bytes 202760 | tf_op jit(solution)/shard_map/ppermute | solution.py:557
  32.3 3.5 %collective-permute-done.9.refs_10_ = bf16[264,128]{1,0:T(8,128)(2,1)S(1)} collective-permute-done((bf16[264,128]{1,0:T(8,128)(2,1)S(1)}, bf16[264,128]{1,0:T(8,128)(2,1)S(1)}, u32[]{:S(2)}, u32[]{:S(2)}) %collective-permute-start.9) | collective-permute-done | bytes 67616 | tf_op jit(solution)/shard_map/ppermute | solution.py:557
  35.8 5.6 %shard_map.108 = (bf16[64,512]{1,0:T(8,128)(2,1)S(1)}, bf16[64,512]{1,0:T(8,128)(2,1)S(1)}, bf16[64,512]{1,0:T(8,128)(2,1)S(1)}, bf16[64,512]{1,0:T(8,128)(2,1)S...) custom-call(f32[1,512]{1,0:T(1,128)S(1)} %get-tuple-element.76.refs_, ...), custom_call_target="tpu_custom_call" | custom-call | flops 8589934592 | bytes 4194304 | tf_op jit(solution)/shard_map/pallas_call | solution.py:696
  41.9 2.0 %collective-permute-start.3 = (f32[16,256]{1,0:T(8,128)S(1)}, f32[16,256]{1,0:T(8,128)S(1)}, u32[]{:S(2)}, u32[]{:S(2)}) collective-permute-start(f32[16,256]{1,0:T(8,128)S(1)} %get-tuple-element.91.refs_2_), channel_id=1, source_target_pairs={{0,16},{8,24},{16,0},{24,8},{1,17},{9,25},{17,1},{25,9},{2,18},{10... | collective-permute-start | bytes 49160 | tf_op jit(solution)/shard_map/ppermute | solution.py:557
  43.9 1.5 %collective-permute-start.4 = (f32[16,256]{1,0:T(8,128)S(1)}, f32[16,256]{1,0:T(8,128)S(1)}, u32[]{:S(2)}, u32[]{:S(2)}) collective-permute-start(f32[16,256]{1,0:T(8,128)S(1)} %get-tuple-element.91.refs_2_), channel_id=1, source_target_pairs={{0,8},{8,0},{16,24},{24,16},{1,9},{9,1},{17,25},{25,17},{2,10},{10... | collective-permute-start | bytes 49160 | tf_op jit(solution)/shard_map/ppermute | solution.py:557
  46.8 1.0 %collective-permute-done.4.refs_4_ = f32[16,256]{1,0:T(8,128)S(1)} collective-permute-done((f32[16,256]{1,0:T(8,128)S(1)}, f32[16,256]{1,0:T(8,128)S(1)}, u32[]{:S(2)}, u32[]{:S(2)}) %collective-permute-start.4) | collective-permute-done | bytes 16416 | tf_op jit(solution)/shard_map/ppermute | solution.py:557
  48.6 1.5 %collective-permute-done.5.refs_5_ = f32[16,256]{1,0:T(8,128)S(1)} collective-permute-done((f32[16,256]{1,0:T(8,128)S(1)}, f32[16,256]{1,0:T(8,128)S(1)}, u32[]{:S(2)}, u32[]{:S(2)}) %collective-permute-start.5) | collective-permute-done | bytes 16416 | tf_op jit(solution)/shard_map/ppermute | solution.py:557
  50.3 2.1 %collective-permute-start.18 = (bf16[64,512]{1,0:T(8,128)(2,1)S(1)}, bf16[64,512]{1,0:T(8,128)(2,1)S(1)}, u32[]{:S(2)}, u32[]{:S(2)}) collective-permute-start(bf16[64,512]{1,0:T(8,128)(2,1)S(1)} %get-tuple-element.119), channel_id=1, source_target_pairs={{0,6},{1,7},{2,4},{3,5},{4,2},{5,3},{6,0},{7,1},{8,14},{9,15},{10,... | collective-permute-start | bytes 196616 | tf_op jit(solution)/shard_map/ppermute | solution.py:557
  52.3 1.9 %collective-permute-start.19 = (bf16[64,512]{1,0:T(8,128)(2,1)S(1)}, bf16[64,512]{1,0:T(8,128)(2,1)S(1)}, u32[]{:S(2)}, u32[]{:S(2)}) collective-permute-start(bf16[64,512]{1,0:T(8,128)(2,1)S(1)} %get-tuple-element.120), channel_id=1, source_target_pairs={{0,7},{1,6},{2,5},{3,4},{4,3},{5,2},{6,1},{7,0},{8,15},{9,14},{10,... | collective-permute-start | bytes 196616 | tf_op jit(solution)/shard_map/ppermute | solution.py:557
  54.2 2.3 %shard_map.106.refs_13_.refs_0_ = bf16[16,256,1024]{2,1,0:T(8,128)(2,1)S(1)} custom-call(bf16[256,512]{1,0:T(8,128)(2,1)S(1)} %get-tuple-element.73.refs_9_.refs_0_.refs_4_, bf16[1024,512]{1,0:T(8,128)(2,1)S(1)} %shard_map.102.refs_1_.refs_2_, f32[16,256]{1,0:T(8,128)S(1)} %get-tuple-element.91.refs_2_, f32[16,256]{1,0:T(8,128)S(1)} %collective-permute-done.3.refs_3_, ...), custom_call_target="tpu_custom_call" | custom-call | flops 4294967296 | bytes 10485760 | tf_op jit(solution)/shard_map/pallas_call | solution.py:686
  56.6 2.0 %collective-permute-done.16.refs_7_ = bf16[64,512]{1,0:T(8,128)(2,1)S(1)} collective-permute-done((bf16[64,512]{1,0:T(8,128)(2,1)S(1)}, bf16[64,512]{1,0:T(8,128)(2,1)S(1)}, u32[]{:S(2)}, u32[]{:S(2)}) %collective-permute-start.16) | collective-permute-done | bytes 65568 | tf_op jit(solution)/shard_map/ppermute | solution.py:557
  58.5 1.1 %collective-permute-done.17.refs_8_ = bf16[64,512]{1,0:T(8,128)(2,1)S(1)} collective-permute-done((bf16[64,512]{1,0:T(8,128)(2,1)S(1)}, bf16[64,512]{1,0:T(8,128)(2,1)S(1)}, u32[]{:S(2)}, u32[]{:S(2)}) %collective-permute-start.17) | collective-permute-done | bytes 65568 | tf_op jit(solution)/shard_map/ppermute | solution.py:557
  61.2 1.5 %collective-permute-start.21 = (bf16[264,512]{1,0:T(8,128)(2,1)S(1)}, bf16[264,512]{1,0:T(8,128)(2,1)S(1)}, u32[]{:S(2)}, u32[]{:S(2)}) collective-permute-start(bf16[264,512]{1,0:T(8,128)(2,1)S(1)} %get-tuple-element.121.refs_14_), channel_id=1, source_target_pairs={{0,8},{8,0},{16,24},{24,16},{1,9},{9,1},{17,25},{25,17},{2,10},{10... | collective-permute-start | bytes 811016 | tf_op jit(solution)/shard_map/ppermute | solution.py:557
  62.6 1.3 %collective-permute-start.22 = (bf16[264,512]{1,0:T(8,128)(2,1)S(1)}, bf16[264,512]{1,0:T(8,128)(2,1)S(1)}, u32[]{:S(2)}, u32[]{:S(2)}) collective-permute-start(bf16[264,512]{1,0:T(8,128)(2,1)S(1)} %get-tuple-element.121.refs_14_), channel_id=1, source_target_pairs={{0,24},{8,16},{16,8},{24,0},{1,25},{9,17},{17,9},{25,1},{2,26},{10... | collective-permute-start | bytes 811016 | tf_op jit(solution)/shard_map/ppermute | solution.py:557
  64.0 7.3 %shard_map.110 = (f32[256,512]{1,0:T(8,128)S(1)}, f32[256,512]{1,0:T(8,128)S(1)}, f32[256,512]{1,0:T(8,128)S(1)}) custom-call(bf16[16,256,256]{2,1,0:T(8,128)(2,1)S(1)} %get-tuple-element.92.refs_0_, bf16[16,256,256]{2,1,0:T(8,128)(2,1)S(1)} %get-tuple-element.93.refs_1_, bf16[16,256,256]{2,1,0:T(8,128)(2,1)S(1)} %get-tuple-element.94.refs_2_, ...), custom_call_target="tpu_custom_call" | custom-call | flops 8589934592 | bytes 10485760 | tf_op jit(solution)/shard_map/pallas_call | solution.py:721
  71.3 2.3 %shard_map.111 = (f32[256,512]{1,0:T(8,128)S(1)}, f32[256,512]{1,0:T(8,128)S(1)}) custom-call(bf16[16,256,1024]{2,1,0:T(8,128)(2,1)S(1)} %shard_map.106.refs_13_.refs_0_, bf16[256,512]{1,0:T(8,128)(2,1)S(1)} %get-tuple-element.85.refs_12_.refs_8_.refs_1_, bf16[1024,512]{1,0:T(8,128)(2,1)S(1)} %shard_map.102.refs_1_.refs_2_, ...), custom_call_target="tpu_custom_call" | custom-call | flops 2147483648 | bytes 4194304 | tf_op jit(solution)/shard_map/pallas_call | solution.py:732
  73.5 2.3 %shard_map.112 = (f32[256,512]{1,0:T(8,128)S(1)}, f32[256,512]{1,0:T(8,128)S(1)}) custom-call(bf16[16,256,1024]{2,1,0:T(8,128)(2,1)S(1)} %shard_map.106.refs_13_.refs_0_, bf16[256,512]{1,0:T(8,128)(2,1)S(1)} %get-tuple-element.85.refs_12_.refs_8_.refs_1_, bf16[1024,512]{1,0:T(8,128)(2,1)S(1)} %shard_map.102.refs_1_.refs_2_, ...), custom_call_target="tpu_custom_call" | custom-call | flops 2147483648 | bytes 4194304 | tf_op jit(solution)/shard_map/pallas_call | solution.py:732
  76.0 3.4 %shard_map.113 = bf16[256,512]{1,0:T(8,128)(2,1)} custom-call(bf16[16,256,1024]{2,1,0:T(8,128)(2,1)S(1)} %shard_map.106.refs_13_.refs_0_, bf16[256,512]{1,0:T(8,128)(2,1)S(1)} %get-tuple-element.85.refs_12_.refs_8_.refs_1_, bf16[1024,512]{1,0:T(8,128)(2,1)S(1)} %shard_map.102.refs_1_.refs_2_, f32[256,512]{1,0:T(8,128)S(1)} %get-tuple-element.123.refs_3_, ...), custom_call_target="tpu_custom_call" | custom-call | flops 8589934592 | bytes 14680064 | tf_op jit(solution)/shard_map/pallas_call | solution.py:739
  (48 shorter events, 6.5 us)
Async XLA Ops:
  0.0 9.5 %collective-permute-start = (bf16[256,512]{1,0:T(8,128)(2,1)}, bf16[256,512]{1,0:T(8,128)(2,1)S(1)}, u32[]{:S(2)}, u32[]{:S(2)}) collective-permute-start(bf16[256,512]{1,0:T(8,128)(2,1)} %bitcast.13), channel_id=1, source_target_pairs={{0,16},{8,24},{16,0},{24,8},{1,17},{9,25},{17,1},{25,9},{2,18},{10... | collective-permute-start | bytes 786440 | tf_op jit(solution)/shard_map/ppermute | solution.py:557
  3.0 9.4 %collective-permute-start.1 = (bf16[256,512]{1,0:T(8,128)(2,1)}, bf16[256,512]{1,0:T(8,128)(2,1)S(1)}, u32[]{:S(2)}, u32[]{:S(2)}) collective-permute-start(bf16[256,512]{1,0:T(8,128)(2,1)} %bitcast.14), channel_id=1, source_target_pairs={{0,8},{8,0},{16,24},{24,16},{1,9},{9,1},{17,25},{25,17},{2,10},{10... | collective-permute-start | bytes 786440 | tf_op jit(solution)/shard_map/ppermute | solution.py:557
  4.5 11.8 %collective-permute-start.2 = (bf16[256,512]{1,0:T(8,128)(2,1)}, bf16[256,512]{1,0:T(8,128)(2,1)S(1)}, u32[]{:S(2)}, u32[]{:S(2)}) collective-permute-start(bf16[256,512]{1,0:T(8,128)(2,1)} %bitcast.15), channel_id=1, source_target_pairs={{0,24},{8,16},{16,8},{24,0},{1,25},{9,17},{17,9},{25,1},{2,26},{10... | collective-permute-start | bytes 786440 | tf_op jit(solution)/shard_map/ppermute | solution.py:557
  5.2 1.4 %copy-start = (bf16[512,1536]{1,0:T(8,128)(2,1)S(1)}, bf16[512,1536]{1,0:T(8,128)(2,1)}, u32[]{:S(2)}) copy-start(bf16[512,1536]{1,0:T(8,128)(2,1)} %refs_8_.1) | copy-start | bytes 4718596
  5.2 1.4 %copy-start.1 = (f32[512]{0:T(512)S(1)}, f32[512]{0:T(512)}, u32[]{:S(2)}) copy-start(f32[512]{0:T(512)} %param.11) | copy-start | bytes 6148
  5.2 1.4 %copy-start.5 = (bf16[1,1,256,512]{3,2,1,0:T(8,128)(2,1)S(1)}, bf16[1,1,256,512]{3,2,1,0:T(8,128)(2,1)}, u32[]{:S(2)}) copy-start(bf16[1,1,256,512]{3,2,1,0:T(8,128)(2,1)} %param.10) | copy-start | bytes 786436
  12.4 3.9 %copy-start.4 = (bf16[512,512]{1,0:T(8,128)(2,1)S(1)}, bf16[512,512]{1,0:T(8,128)(2,1)}, u32[]{:S(2)}) copy-start(bf16[512,512]{1,0:T(8,128)(2,1)} %refs_2_.11) | copy-start | bytes 1572868
  16.3 15.3 %copy-start.3 = (bf16[512,512]{1,0:T(8,128)(2,1)S(1)}, bf16[512,512]{1,0:T(8,128)(2,1)}, u32[]{:S(2)}) copy-start(bf16[512,512]{1,0:T(8,128)(2,1)} %out_w_ref.1) | copy-start | bytes 1572868
  16.3 15.3 %copy-start.6 = (bf16[1,1,256,512]{3,2,1,0:T(8,128)(2,1)S(1)}, bf16[1,1,256,512]{3,2,1,0:T(8,128)(2,1)}, u32[]{:S(2)}) copy-start(bf16[1,1,256,512]{3,2,1,0:T(8,128)(2,1)} %param.19) | copy-start | bytes 786436
  16.3 15.3 %copy-start.9 = (s32[1,1,256]{2,1,0:T(1,128)S(1)}, s32[1,1,256]{2,1,0:T(1,128)}, u32[]{:S(2)}) copy-start(s32[1,1,256]{2,1,0:T(1,128)} %param.18) | copy-start | bytes 3076
  16.3 19.5 %copy-start.2 = (bf16[512,1536]{1,0:T(8,128)(2,1)S(1)}, bf16[512,1536]{1,0:T(8,128)(2,1)}, u32[]{:S(2)}) copy-start(bf16[512,1536]{1,0:T(8,128)(2,1)} %refs_2_.10) | copy-start | bytes 4718596
  16.3 19.5 %copy-start.7 = (f32[512]{0:T(512)S(1)}, f32[512]{0:T(512)}, u32[]{:S(2)}) copy-start(f32[512]{0:T(512)} %param.15) | copy-start | bytes 6148
  19.1 6.2 %collective-permute-start.10 = (bf16[264,128]{1,0:T(8,128)(2,1)S(1)}, bf16[264,128]{1,0:T(8,128)(2,1)S(1)}, u32[]{:S(2)}, u32[]{:S(2)}) collective-permute-start(bf16[264,128]{1,0:T(8,128)(2,1)S(1)} %get-tuple-element.110), channel_id=1, source_target_pairs={{0,5},{1,4},{2,7},{3,6},{4,1},{5,0},{6,3},{7,2},{8,13},{9,12},{10,... | collective-permute-start | bytes 202760 | tf_op jit(solution)/shard_map/ppermute | solution.py:557
  20.3 7.7 %collective-permute-start.11 = (bf16[264,128]{1,0:T(8,128)(2,1)S(1)}, bf16[264,128]{1,0:T(8,128)(2,1)S(1)}, u32[]{:S(2)}, u32[]{:S(2)}) collective-permute-start(bf16[264,128]{1,0:T(8,128)(2,1)S(1)} %get-tuple-element.111), channel_id=1, source_target_pairs={{0,6},{1,7},{2,4},{3,5},{4,2},{5,3},{6,0},{7,1},{8,14},{9,15},{10,... | collective-permute-start | bytes 202760 | tf_op jit(solution)/shard_map/ppermute | solution.py:557
  23.1 8.9 %collective-permute-start.12 = (bf16[264,128]{1,0:T(8,128)(2,1)S(1)}, bf16[264,128]{1,0:T(8,128)(2,1)S(1)}, u32[]{:S(2)}, u32[]{:S(2)}) collective-permute-start(bf16[264,128]{1,0:T(8,128)(2,1)S(1)} %get-tuple-element.112), channel_id=1, source_target_pairs={{0,7},{1,6},{2,5},{3,4},{4,3},{5,2},{6,1},{7,0},{8,15},{9,14},{10,... | collective-permute-start | bytes 202760 | tf_op jit(solution)/shard_map/ppermute | solution.py:557
  25.3 6.7 %collective-permute-start.6 = (bf16[264,128]{1,0:T(8,128)(2,1)S(1)}, bf16[264,128]{1,0:T(8,128)(2,1)S(1)}, u32[]{:S(2)}, u32[]{:S(2)}) collective-permute-start(bf16[264,128]{1,0:T(8,128)(2,1)S(1)} %get-tuple-element.106), channel_id=1, source_target_pairs={{0,1},{1,0},{2,3},{3,2},{4,5},{5,4},{6,7},{7,6},{8,9},{9,8},{10,11... | collective-permute-start | bytes 202760 | tf_op jit(solution)/shard_map/ppermute | solution.py:557
  25.3 6.7 %collective-permute-start.7 = (bf16[264,128]{1,0:T(8,128)(2,1)S(1)}, bf16[264,128]{1,0:T(8,128)(2,1)S(1)}, u32[]{:S(2)}, u32[]{:S(2)}) collective-permute-start(bf16[264,128]{1,0:T(8,128)(2,1)S(1)} %get-tuple-element.107), channel_id=1, source_target_pairs={{0,2},{1,3},{2,0},{3,1},{4,6},{5,7},{6,4},{7,5},{8,10},{9,11},{10,... | collective-permute-start | bytes 202760 | tf_op jit(solution)/shard_map/ppermute | solution.py:557
  25.3 7.0 %collective-permute-start.8 = (bf16[264,128]{1,0:T(8,128)(2,1)S(1)}, bf16[264,128]{1,0:T(8,128)(2,1)S(1)}, u32[]{:S(2)}, u32[]{:S(2)}) collective-permute-start(bf16[264,128]{1,0:T(8,128)(2,1)S(1)} %get-tuple-element.108), channel_id=1, source_target_pairs={{0,3},{1,2},{2,1},{3,0},{4,7},{5,6},{6,5},{7,4},{8,11},{9,10},{10,... | collective-permute-start | bytes 202760 | tf_op jit(solution)/shard_map/ppermute | solution.py:557
  28.1 7.8 %collective-permute-start.9 = (bf16[264,128]{1,0:T(8,128)(2,1)S(1)}, bf16[264,128]{1,0:T(8,128)(2,1)S(1)}, u32[]{:S(2)}, u32[]{:S(2)}) collective-permute-start(bf16[264,128]{1,0:T(8,128)(2,1)S(1)} %get-tuple-element.109), channel_id=1, source_target_pairs={{0,4},{1,5},{2,6},{3,7},{4,0},{5,1},{6,2},{7,3},{8,12},{9,13},{10,... | collective-permute-start | bytes 202760 | tf_op jit(solution)/shard_map/ppermute | solution.py:557
  41.4 8.8 %collective-permute-start.13 = (bf16[64,512]{1,0:T(8,128)(2,1)S(1)}, bf16[64,512]{1,0:T(8,128)(2,1)S(1)}, u32[]{:S(2)}, u32[]{:S(2)}) collective-permute-start(bf16[64,512]{1,0:T(8,128)(2,1)S(1)} %get-tuple-element.114), channel_id=1, source_target_pairs={{0,1},{1,0},{2,3},{3,2},{4,5},{5,4},{6,7},{7,6},{8,9},{9,8},{10,11... | collective-permute-start | bytes 196616 | tf_op jit(solution)/shard_map/ppermute | solution.py:557
  41.6 10.7 %collective-permute-start.14 = (bf16[64,512]{1,0:T(8,128)(2,1)S(1)}, bf16[64,512]{1,0:T(8,128)(2,1)S(1)}, u32[]{:S(2)}, u32[]{:S(2)}) collective-permute-start(bf16[64,512]{1,0:T(8,128)(2,1)S(1)} %get-tuple-element.115), channel_id=1, source_target_pairs={{0,2},{1,3},{2,0},{3,1},{4,6},{5,7},{6,4},{7,5},{8,10},{9,11},{10,... | collective-permute-start | bytes 196616 | tf_op jit(solution)/shard_map/ppermute | solution.py:557
  41.9 4.2 %collective-permute-start.3 = (f32[16,256]{1,0:T(8,128)S(1)}, f32[16,256]{1,0:T(8,128)S(1)}, u32[]{:S(2)}, u32[]{:S(2)}) collective-permute-start(f32[16,256]{1,0:T(8,128)S(1)} %get-tuple-element.91.refs_2_), channel_id=1, source_target_pairs={{0,16},{8,24},{16,0},{24,8},{1,17},{9,25},{17,1},{25,9},{2,18},{10... | collective-permute-start | bytes 49160 | tf_op jit(solution)/shard_map/ppermute | solution.py:557
  43.9 3.9 %collective-permute-start.4 = (f32[16,256]{1,0:T(8,128)S(1)}, f32[16,256]{1,0:T(8,128)S(1)}, u32[]{:S(2)}, u32[]{:S(2)}) collective-permute-start(f32[16,256]{1,0:T(8,128)S(1)} %get-tuple-element.91.refs_2_), channel_id=1, source_target_pairs={{0,8},{8,0},{16,24},{24,16},{1,9},{9,1},{17,25},{25,17},{2,10},{10... | collective-permute-start | bytes 49160 | tf_op jit(solution)/shard_map/ppermute | solution.py:557
  45.4 4.6 %collective-permute-start.5 = (f32[16,256]{1,0:T(8,128)S(1)}, f32[16,256]{1,0:T(8,128)S(1)}, u32[]{:S(2)}, u32[]{:S(2)}) collective-permute-start(f32[16,256]{1,0:T(8,128)S(1)} %get-tuple-element.91.refs_2_), channel_id=1, source_target_pairs={{0,24},{8,16},{16,8},{24,0},{1,25},{9,17},{17,9},{25,1},{2,26},{10... | collective-permute-start | bytes 49160 | tf_op jit(solution)/shard_map/ppermute | solution.py:557
  46.1 10.4 %collective-permute-start.15 = (bf16[64,512]{1,0:T(8,128)(2,1)S(1)}, bf16[64,512]{1,0:T(8,128)(2,1)S(1)}, u32[]{:S(2)}, u32[]{:S(2)}) collective-permute-start(bf16[64,512]{1,0:T(8,128)(2,1)S(1)} %get-tuple-element.116), channel_id=1, source_target_pairs={{0,3},{1,2},{2,1},{3,0},{4,7},{5,6},{6,5},{7,4},{8,11},{9,10},{10,... | collective-permute-start | bytes 196616 | tf_op jit(solution)/shard_map/ppermute | solution.py:557
  47.8 10.8 %collective-permute-start.16 = (bf16[64,512]{1,0:T(8,128)(2,1)S(1)}, bf16[64,512]{1,0:T(8,128)(2,1)S(1)}, u32[]{:S(2)}, u32[]{:S(2)}) collective-permute-start(bf16[64,512]{1,0:T(8,128)(2,1)S(1)} %get-tuple-element.117), channel_id=1, source_target_pairs={{0,4},{1,5},{2,6},{3,7},{4,0},{5,1},{6,2},{7,3},{8,12},{9,13},{10,... | collective-permute-start | bytes 196616 | tf_op jit(solution)/shard_map/ppermute | solution.py:557
  50.0 9.6 %collective-permute-start.17 = (bf16[64,512]{1,0:T(8,128)(2,1)S(1)}, bf16[64,512]{1,0:T(8,128)(2,1)S(1)}, u32[]{:S(2)}, u32[]{:S(2)}) collective-permute-start(bf16[64,512]{1,0:T(8,128)(2,1)S(1)} %get-tuple-element.118), channel_id=1, source_target_pairs={{0,5},{1,4},{2,7},{3,6},{4,1},{5,0},{6,3},{7,2},{8,13},{9,12},{10,... | collective-permute-start | bytes 196616 | tf_op jit(solution)/shard_map/ppermute | solution.py:557
  50.3 9.4 %collective-permute-start.18 = (bf16[64,512]{1,0:T(8,128)(2,1)S(1)}, bf16[64,512]{1,0:T(8,128)(2,1)S(1)}, u32[]{:S(2)}, u32[]{:S(2)}) collective-permute-start(bf16[64,512]{1,0:T(8,128)(2,1)S(1)} %get-tuple-element.119), channel_id=1, source_target_pairs={{0,6},{1,7},{2,4},{3,5},{4,2},{5,3},{6,0},{7,1},{8,14},{9,15},{10,... | collective-permute-start | bytes 196616 | tf_op jit(solution)/shard_map/ppermute | solution.py:557
  52.3 7.3 %collective-permute-start.19 = (bf16[64,512]{1,0:T(8,128)(2,1)S(1)}, bf16[64,512]{1,0:T(8,128)(2,1)S(1)}, u32[]{:S(2)}, u32[]{:S(2)}) collective-permute-start(bf16[64,512]{1,0:T(8,128)(2,1)S(1)} %get-tuple-element.120), channel_id=1, source_target_pairs={{0,7},{1,6},{2,5},{3,4},{4,3},{5,2},{6,1},{7,0},{8,15},{9,14},{10,... | collective-permute-start | bytes 196616 | tf_op jit(solution)/shard_map/ppermute | solution.py:557
  60.4 10.8 %collective-permute-start.20 = (bf16[264,512]{1,0:T(8,128)(2,1)S(1)}, bf16[264,512]{1,0:T(8,128)(2,1)S(1)}, u32[]{:S(2)}, u32[]{:S(2)}) collective-permute-start(bf16[264,512]{1,0:T(8,128)(2,1)S(1)} %get-tuple-element.121.refs_14_), channel_id=1, source_target_pairs={{0,16},{8,24},{16,0},{24,8},{1,17},{9,25},{17,1},{25,9},{2,18},{10... | collective-permute-start | bytes 811016 | tf_op jit(solution)/shard_map/ppermute | solution.py:557
  61.2 12.4 %collective-permute-start.21 = (bf16[264,512]{1,0:T(8,128)(2,1)S(1)}, bf16[264,512]{1,0:T(8,128)(2,1)S(1)}, u32[]{:S(2)}, u32[]{:S(2)}) collective-permute-start(bf16[264,512]{1,0:T(8,128)(2,1)S(1)} %get-tuple-element.121.refs_14_), channel_id=1, source_target_pairs={{0,8},{8,0},{16,24},{24,16},{1,9},{9,1},{17,25},{25,17},{2,10},{10... | collective-permute-start | bytes 811016 | tf_op jit(solution)/shard_map/ppermute | solution.py:557
  62.6 13.3 %collective-permute-start.22 = (bf16[264,512]{1,0:T(8,128)(2,1)S(1)}, bf16[264,512]{1,0:T(8,128)(2,1)S(1)}, u32[]{:S(2)}, u32[]{:S(2)}) collective-permute-start(bf16[264,512]{1,0:T(8,128)(2,1)S(1)} %get-tuple-element.121.refs_14_), channel_id=1, source_target_pairs={{0,24},{8,16},{16,8},{24,0},{1,25},{9,17},{17,9},{25,1},{2,26},{10... | collective-permute-start | bytes 811016 | tf_op jit(solution)/shard_map/ppermute | solution.py:557
  (1 other events, 0.7 us)

commit v4 on v3

--- a/solution.py
+++ b/solution.py
@@ -191,7 +191,7 @@
     others, refs = refs[: peers + 1 - early], refs[peers + 1 - early + early :]
     keys_ref, values_ref, weights_ref, mixed_ref, inverse_ref, lse_ref = refs[:6]
     early_weights, refs = refs[6 : 6 + early], refs[6 + early :]
-    sends, (safe, out_sems) = refs[:chunks], refs[chunks:]
+    sends, (mixed_low, safe, out_sems) = refs[:chunks], refs[chunks:]
     count, width = x_ref.shape
     heads = LANES // depth
     for index, other in enumerate(others):
@@ -202,7 +202,8 @@
 
     def finish_tile(t, at, mixed, sums, tops):
         inverse = 1.0 / sums
-        mixed_ref[:, at] = (mixed * inverse).astype(BF16)
+        mixed_ref[:, at] = mixed * inverse
+        mixed_low[:, at] = (mixed * inverse).astype(BF16)
         inverse_ref[:, at] = inverse
         flipped = flip_tile(tops + jnp.log(sums) * LOG2E)
         for j in range(heads):
@@ -253,7 +254,7 @@
         for copy in start_all(pairs, out_sems):
             copy.wait()
 
-    moved = (x_ref[...].astype(F32) + dot_nn(mixed_ref[...], out_w_ref[...])).astype(BF16)
+    moved = (x_ref[...].astype(F32) + dot_nn(mixed_low[...], out_w_ref[...])).astype(BF16)
     slots = 2 * count
     leaving = dot_nn(put_ref[...], moved).astype(BF16)
     if chunks == 1:
@@ -405,7 +406,7 @@
     moved_ref[...] = moved
     grad = dot_nt(moved, out_w_ref[...]).astype(BF16)
     grad_ref[:count] = grad
-    product = grad.astype(F32) * mixed_ref[...].astype(F32)
+    product = grad.astype(F32) * mixed_ref[...]
     high = product.astype(BF16)
     low = (product - high.astype(F32)).astype(BF16)
     heads = width // depth
@@ -417,9 +418,14 @@
     delta_ref[...] = delta
     beside = width // count
     tail = heads // beside
-    for part in range(beside):
-        lines = delta[part * tail : (part + 1) * tail].astype(BF16)
-        grad_ref[count:, part * count : (part + 1) * count] = lines
+    rest = delta
+    for term in range(2):
+        rounded = rest.astype(BF16)
+        rest -= rounded.astype(F32)
+        rows = slice(count + term * tail, count + (term + 1) * tail)
+        for part in range(beside):
+            lines = rounded[part * tail : (part + 1) * tail]
+            grad_ref[rows, part * count : (part + 1) * count] = lines
 
 
 def key_tile(depth, t, v_tile, weights_ref, columns, queries, grads, deltas_ref):
@@ -441,6 +447,7 @@
 
 def heads_apart(lines, count):
     wide = lines.astype(F32)
+    wide = wide[: wide.shape[0] // 2] + wide[wide.shape[0] // 2 :]
     parts = [wide[:, i * count : (i + 1) * count] for i in range(lines.shape[1] // count)]
     return jnp.concatenate(parts, axis=0)
 
@@ -642,10 +649,11 @@
     results = vmem_call(
         functools.partial(forward_body, early, peers, chunks, capacity, depth),
         (late_bf16, late_bf16, shape(BF16, HEADS, count, late * count))
-        + (rows_bf16, rows_f32, lines_f32)
+        + (rows_f32, rows_f32, lines_f32)
         + (square,) * early
         + (sent,) * chunks,
         [
+            pltpu.VMEM((count, width), BF16),
             pltpu.VMEM((early,) + square.shape, BF16),
             dma((early,)),
         ],
@@ -712,7 +720,7 @@
 
     moved_grad, grad_own, delta = vmem_call(
         functools.partial(home_body, chunks, depth),
-        (rows_bf16, shape(BF16, count + HEADS * count // width, width), lines_f32),
+        (rows_bf16, shape(BF16, count + 2 * HEADS * count // width, width), lines_f32),
         flops=1 << 29,
         moved=2 << 20,
     )(take, mixed, out_one, *home)

time: 79.9 us -> 80.2 us (level)
  no operation moved by 1% of the time
where the time goes in v4:
time: 80.2 us; the launch traced here: 79.7 us
  Pallas kernels  33.7 us (42%)
  starting transfers between devices  30.1 us (38%)
  waiting for transfers between devices  14 us (17%)
  local copies, waits for them, and re-layouts  1.61 us (2%)
    ppermute x23, starting transfers between devices, by_xor(): return lax.ppermute(array, axis, [(i, i ^ step) for i in range(size)])  30.1 us
    ppermute x23, waiting for transfers between devices, by_xor(): return lax.ppermute(array, axis, [(i, i ^ step) for i in range(size)])  14 us
    pallas_call x1, Pallas kernels, shards(): vmem_call(functools.partial(query_grad_body, len(all_keys), depth), (rows...  7.22 us
    pallas_call x1, Pallas kernels, shards(): vmem_call(functools.partial(second_body, chunks, depth), (chunk_bf16,) *...  5.58 us
    pallas_call x2, Pallas kernels, shards(): vmem_call(functools.partial(key_middle_body, index, depth), (rows_f32, ro...  4.56 us
    pallas_call x2, Pallas kernels, shards(): vmem_call(functools.partial(middle_body, depth), (rows_bf16,) * 2 + (squa...  3.58 us
    pallas_call x1, Pallas kernels, shards(): vmem_call(functools.partial(key_grad_body, early, peers, depth), rows_bf1...  3.43 us
    pallas_call x1, Pallas kernels, shards(): vmem_call(functools.partial(forward_body, early, peers, chunks, capacity,...  2.77 us
  transfers between devices with their start and end apart: 23, of which 10 were waited for; matrix products, arithmetic and copies ran while one was open for 0% of the time, Pallas kernels for 27%

profile of v4, /device:TPU:0, one launch (start us, length us, event | category | flops | bytes accessed | tf_op | source)
XLA Modules:
  0.0 79.7 jit_solution(218285249859647303)
XLA Ops:
  0.0 3.0 %collective-permute-start = (bf16[256,512]{1,0:T(8,128)(2,1)}, bf16[256,512]{1,0:T(8,128)(2,1)S(1)}, u32[]{:S(2)}, u32[]{:S(2)}) collective-permute-start(bf16[256,512]{1,0:T(8,128)(2,1)} %bitcast.13), channel_id=1, source_target_pairs={{0,16},{8,24},{16,0},{24,8},{1,17},{9,25},{17,1},{25,9},{2,18},{10... | collective-permute-start | bytes 786440 | tf_op jit(solution)/shard_map/ppermute | solution.py:564
  3.0 1.5 %collective-permute-start.1 = (bf16[256,512]{1,0:T(8,128)(2,1)}, bf16[256,512]{1,0:T(8,128)(2,1)S(1)}, u32[]{:S(2)}, u32[]{:S(2)}) collective-permute-start(bf16[256,512]{1,0:T(8,128)(2,1)} %bitcast.14), channel_id=1, source_target_pairs={{0,8},{8,0},{16,24},{24,16},{1,9},{9,1},{17,25},{25,17},{2,10},{10... | collective-permute-start | bytes 786440 | tf_op jit(solution)/shard_map/ppermute | solution.py:564
  5.7 0.9 %copy-done = bf16[512,1536]{1,0:T(8,128)(2,1)S(1)} copy-done((bf16[512,1536]{1,0:T(8,128)(2,1)S(1)}, bf16[512,1536]{1,0:T(8,128)(2,1)}, u32[]{:S(2)}) %copy-start) | copy-done | bytes 1572888
  6.6 1.9 %shard_map.101 = (bf16[256,512]{1,0:T(8,128)(2,1)S(1)}, bf16[256,512]{1,0:T(8,128)(2,1)S(1)}, bf16[256,512]{1,0:T(8,128)(2,1)S(1)}, bf16[16,256,256]{2,1,0:T(8,1...) custom-call(bf16[256,512]{1,0:T(8,128)(2,1)S(1)} %bitcast.16, ...), custom_call_target="tpu_custom_call" | custom-call | flops 2147483648 | bytes 4194304 | tf_op jit(solution)/shard_map/pallas_call | solution.py:626
  8.6 1.0 %collective-permute-done.refs_3_.refs_0_ = bf16[256,512]{1,0:T(8,128)(2,1)S(1)} collective-permute-done((bf16[256,512]{1,0:T(8,128)(2,1)}, bf16[256,512]{1,0:T(8,128)(2,1)S(1)}, u32[]{:S(2)}, u32[]{:S(2)}) %collective-permute-start) | collective-permute-done | bytes 262176 | tf_op jit(solution)/shard_map/ppermute | solution.py:564
  9.5 1.8 %shard_map.103 = (bf16[256,512]{1,0:T(8,128)(2,1)S(1)}, bf16[256,512]{1,0:T(8,128)(2,1)S(1)}, bf16[16,256,256]{2,1,0:T(8,128)(2,1)S(1)}, f32[256,512]{1,0:T(8,128)S(1)}, f32[256,512]{1,0:T(8,128)S(1)}) custom-call(bf16[256,512]{1,0:T(8,128)(2,1)S(1)} %collective-permute-done.refs_3_.refs_0_, f32[1,512]{1,0:T(1,128)S(1)} %bitcast.9, ...), custom_call_target="tpu_custom_call" | custom-call | flops 2147483648 | bytes 4194304 | tf_op jit(solution)/shard_map/pallas_call | solution.py:634
  11.3 1.1 %collective-permute-done.1.refs_4_.refs_0_ = bf16[256,512]{1,0:T(8,128)(2,1)S(1)} collective-permute-done((bf16[256,512]{1,0:T(8,128)(2,1)}, bf16[256,512]{1,0:T(8,128)(2,1)S(1)}, u32[]{:S(2)}, u32[]{:S(2)}) %collective-permute-start.1) | collective-permute-done | bytes 262176 | tf_op jit(solution)/shard_map/ppermute | solution.py:564
  12.4 1.8 %shard_map.104 = (bf16[256,512]{1,0:T(8,128)(2,1)S(1)}, bf16[256,512]{1,0:T(8,128)(2,1)S(1)}, bf16[16,256,256]{2,1,0:T(8,128)(2,1)S(1)}, f32[256,512]{1,0:T(8,128)S(1)}, f32[256,512]{1,0:T(8,128)S(1)}) custom-call(bf16[256,512]{1,0:T(8,128)(2,1)S(1)} %collective-permute-done.1.refs_4_.refs_0_, f32[1,512]{1,0:T(1,128)S(1)} %bitcast.10, ...), custom_call_target="tpu_custom_call" | custom-call | flops 2147483648 | bytes 4194304 | tf_op jit(solution)/shard_map/pallas_call | solution.py:634
  14.2 2.1 %collective-permute-done.2.refs_5_.refs_15_ = bf16[256,512]{1,0:T(8,128)(2,1)S(1)} collective-permute-done((bf16[256,512]{1,0:T(8,128)(2,1)}, bf16[256,512]{1,0:T(8,128)(2,1)S(1)}, u32[]{:S(2)}, u32[]{:S(2)}) %collective-permute-start.2) | collective-permute-done | bytes 262176 | tf_op jit(solution)/shard_map/ppermute | solution.py:564
  16.4 2.8 %shard_map.105 = (bf16[256,512]{1,0:T(8,128)(2,1)S(1)}, bf16[256,512]{1,0:T(8,128)(2,1)S(1)}, bf16[16,256,256]{2,1,0:T(8,128)(2,1)S(1)}, f32[256,512]{1,0:T(8,12...) custom-call(bf16[256,512]{1,0:T(8,128)(2,1)S(1)} %bitcast.17, ...), custom_call_target="tpu_custom_call", output_to_operand_aliasing={{6}: (16, {}), {7}: (17, {}), {8}: (18, {})} | custom-call | flops 8589934592 | bytes 8388608 | tf_op jit(solution)/shard_map/pallas_call | solution.py:649
  19.1 1.2 %collective-permute-start.10 = (bf16[264,128]{1,0:T(8,128)(2,1)S(1)}, bf16[264,128]{1,0:T(8,128)(2,1)S(1)}, u32[]{:S(2)}, u32[]{:S(2)}) collective-permute-start(bf16[264,128]{1,0:T(8,128)(2,1)S(1)} %get-tuple-element.110), channel_id=1, source_target_pairs={{0,5},{1,4},{2,7},{3,6},{4,1},{5,0},{6,3},{7,2},{8,13},{9,12},{10,... | collective-permute-start | bytes 202760 | tf_op jit(solution)/shard_map/ppermute | solution.py:564
  20.3 2.8 %collective-permute-start.11 = (bf16[264,128]{1,0:T(8,128)(2,1)S(1)}, bf16[264,128]{1,0:T(8,128)(2,1)S(1)}, u32[]{:S(2)}, u32[]{:S(2)}) collective-permute-start(bf16[264,128]{1,0:T(8,128)(2,1)S(1)} %get-tuple-element.111), channel_id=1, source_target_pairs={{0,6},{1,7},{2,4},{3,5},{4,2},{5,3},{6,0},{7,1},{8,14},{9,15},{10,... | collective-permute-start | bytes 202760 | tf_op jit(solution)/shard_map/ppermute | solution.py:564
  23.1 2.2 %collective-permute-start.12 = (bf16[264,128]{1,0:T(8,128)(2,1)S(1)}, bf16[264,128]{1,0:T(8,128)(2,1)S(1)}, u32[]{:S(2)}, u32[]{:S(2)}) collective-permute-start(bf16[264,128]{1,0:T(8,128)(2,1)S(1)} %get-tuple-element.112), channel_id=1, source_target_pairs={{0,7},{1,6},{2,5},{3,4},{4,3},{5,2},{6,1},{7,0},{8,15},{9,14},{10,... | collective-permute-start | bytes 202760 | tf_op jit(solution)/shard_map/ppermute | solution.py:564
  25.3 2.8 %collective-permute-start.8 = (bf16[264,128]{1,0:T(8,128)(2,1)S(1)}, bf16[264,128]{1,0:T(8,128)(2,1)S(1)}, u32[]{:S(2)}, u32[]{:S(2)}) collective-permute-start(bf16[264,128]{1,0:T(8,128)(2,1)S(1)} %get-tuple-element.108), channel_id=1, source_target_pairs={{0,3},{1,2},{2,1},{3,0},{4,7},{5,6},{6,5},{7,4},{8,11},{9,10},{10,... | collective-permute-start | bytes 202760 | tf_op jit(solution)/shard_map/ppermute | solution.py:564
  28.1 3.6 %collective-permute-start.9 = (bf16[264,128]{1,0:T(8,128)(2,1)S(1)}, bf16[264,128]{1,0:T(8,128)(2,1)S(1)}, u32[]{:S(2)}, u32[]{:S(2)}) collective-permute-start(bf16[264,128]{1,0:T(8,128)(2,1)S(1)} %get-tuple-element.109), channel_id=1, source_target_pairs={{0,4},{1,5},{2,6},{3,7},{4,0},{5,1},{6,2},{7,3},{8,12},{9,13},{10,... | collective-permute-start | bytes 202760 | tf_op jit(solution)/shard_map/ppermute | solution.py:564
  32.3 3.5 %collective-permute-done.9.refs_10_ = bf16[264,128]{1,0:T(8,128)(2,1)S(1)} collective-permute-done((bf16[264,128]{1,0:T(8,128)(2,1)S(1)}, bf16[264,128]{1,0:T(8,128)(2,1)S(1)}, u32[]{:S(2)}, u32[]{:S(2)}) %collective-permute-start.9) | collective-permute-done | bytes 67616 | tf_op jit(solution)/shard_map/ppermute | solution.py:564
  35.8 5.6 %shard_map.108 = (bf16[64,512]{1,0:T(8,128)(2,1)S(1)}, bf16[64,512]{1,0:T(8,128)(2,1)S(1)}, bf16[64,512]{1,0:T(8,128)(2,1)S(1)}, bf16[64,512]{1,0:T(8,128)(2,1)S...) custom-call(f32[1,512]{1,0:T(1,128)S(1)} %get-tuple-element.76.refs_, ...), custom_call_target="tpu_custom_call" | custom-call | flops 8589934592 | bytes 4194304 | tf_op jit(solution)/shard_map/pallas_call | solution.py:704
  41.9 2.0 %collective-permute-start.3 = (f32[16,256]{1,0:T(8,128)S(1)}, f32[16,256]{1,0:T(8,128)S(1)}, u32[]{:S(2)}, u32[]{:S(2)}) collective-permute-start(f32[16,256]{1,0:T(8,128)S(1)} %get-tuple-element.91.refs_2_), channel_id=1, source_target_pairs={{0,16},{8,24},{16,0},{24,8},{1,17},{9,25},{17,1},{25,9},{2,18},{10... | collective-permute-start | bytes 49160 | tf_op jit(solution)/shard_map/ppermute | solution.py:564
  43.9 1.5 %collective-permute-start.4 = (f32[16,256]{1,0:T(8,128)S(1)}, f32[16,256]{1,0:T(8,128)S(1)}, u32[]{:S(2)}, u32[]{:S(2)}) collective-permute-start(f32[16,256]{1,0:T(8,128)S(1)} %get-tuple-element.91.refs_2_), channel_id=1, source_target_pairs={{0,8},{8,0},{16,24},{24,16},{1,9},{9,1},{17,25},{25,17},{2,10},{10... | collective-permute-start | bytes 49160 | tf_op jit(solution)/shard_map/ppermute | solution.py:564
  46.8 1.0 %collective-permute-done.4.refs_4_ = f32[16,256]{1,0:T(8,128)S(1)} collective-permute-done((f32[16,256]{1,0:T(8,128)S(1)}, f32[16,256]{1,0:T(8,128)S(1)}, u32[]{:S(2)}, u32[]{:S(2)}) %collective-permute-start.4) | collective-permute-done | bytes 16416 | tf_op jit(solution)/shard_map/ppermute | solution.py:564
  47.7 0.8 %collective-permute-start.16 = (bf16[64,512]{1,0:T(8,128)(2,1)S(1)}, bf16[64,512]{1,0:T(8,128)(2,1)S(1)}, u32[]{:S(2)}, u32[]{:S(2)}) collective-permute-start(bf16[64,512]{1,0:T(8,128)(2,1)S(1)} %get-tuple-element.117), channel_id=1, source_target_pairs={{0,4},{1,5},{2,6},{3,7},{4,0},{5,1},{6,2},{7,3},{8,12},{9,13},{10,... | collective-permute-start | bytes 196616 | tf_op jit(solution)/shard_map/ppermute | solution.py:564
  48.6 1.5 %collective-permute-done.5.refs_5_ = f32[16,256]{1,0:T(8,128)S(1)} collective-permute-done((f32[16,256]{1,0:T(8,128)S(1)}, f32[16,256]{1,0:T(8,128)S(1)}, u32[]{:S(2)}, u32[]{:S(2)}) %collective-permute-start.5) | collective-permute-done | bytes 16416 | tf_op jit(solution)/shard_map/ppermute | solution.py:564
  50.2 2.1 %collective-permute-start.18 = (bf16[64,512]{1,0:T(8,128)(2,1)S(1)}, bf16[64,512]{1,0:T(8,128)(2,1)S(1)}, u32[]{:S(2)}, u32[]{:S(2)}) collective-permute-start(bf16[64,512]{1,0:T(8,128)(2,1)S(1)} %get-tuple-element.119), channel_id=1, source_target_pairs={{0,6},{1,7},{2,4},{3,5},{4,2},{5,3},{6,0},{7,1},{8,14},{9,15},{10,... | collective-permute-start | bytes 196616 | tf_op jit(solution)/shard_map/ppermute | solution.py:564
  52.3 1.9 %collective-permute-start.19 = (bf16[64,512]{1,0:T(8,128)(2,1)S(1)}, bf16[64,512]{1,0:T(8,128)(2,1)S(1)}, u32[]{:S(2)}, u32[]{:S(2)}) collective-permute-start(bf16[64,512]{1,0:T(8,128)(2,1)S(1)} %get-tuple-element.120), channel_id=1, source_target_pairs={{0,7},{1,6},{2,5},{3,4},{4,3},{5,2},{6,1},{7,0},{8,15},{9,14},{10,... | collective-permute-start | bytes 196616 | tf_op jit(solution)/shard_map/ppermute | solution.py:564
  54.2 2.3 %shard_map.106.refs_13_.refs_0_ = bf16[16,256,1024]{2,1,0:T(8,128)(2,1)S(1)} custom-call(bf16[256,512]{1,0:T(8,128)(2,1)S(1)} %get-tuple-element.73.refs_9_.refs_0_.refs_4_, bf16[1024,512]{1,0:T(8,128)(2,1)S(1)} %shard_map.102.refs_1_.refs_2_, f32[16,256]{1,0:T(8,128)S(1)} %get-tuple-element.91.refs_2_, f32[16,256]{1,0:T(8,128)S(1)} %collective-permute-done.3.refs_3_, ...), custom_call_target="tpu_custom_call" | custom-call | flops 4294967296 | bytes 10485760 | tf_op jit(solution)/shard_map/pallas_call | solution.py:694
  57.1 2.5 %collective-permute-done.17.refs_8_ = bf16[64,512]{1,0:T(8,128)(2,1)S(1)} collective-permute-done((bf16[64,512]{1,0:T(8,128)(2,1)S(1)}, bf16[64,512]{1,0:T(8,128)(2,1)S(1)}, u32[]{:S(2)}, u32[]{:S(2)}) %collective-permute-start.17) | collective-permute-done | bytes 65568 | tf_op jit(solution)/shard_map/ppermute | solution.py:564
  61.1 1.5 %collective-permute-start.21 = (bf16[272,512]{1,0:T(8,128)(2,1)S(1)}, bf16[272,512]{1,0:T(8,128)(2,1)S(1)}, u32[]{:S(2)}, u32[]{:S(2)}) collective-permute-start(bf16[272,512]{1,0:T(8,128)(2,1)S(1)} %get-tuple-element.121.refs_14_), channel_id=1, source_target_pairs={{0,8},{8,0},{16,24},{24,16},{1,9},{9,1},{17,25},{25,17},{2,10},{10... | collective-permute-start | bytes 835592 | tf_op jit(solution)/shard_map/ppermute | solution.py:564
  62.6 1.3 %collective-permute-start.22 = (bf16[272,512]{1,0:T(8,128)(2,1)S(1)}, bf16[272,512]{1,0:T(8,128)(2,1)S(1)}, u32[]{:S(2)}, u32[]{:S(2)}) collective-permute-start(bf16[272,512]{1,0:T(8,128)(2,1)S(1)} %get-tuple-element.121.refs_14_), channel_id=1, source_target_pairs={{0,24},{8,16},{16,8},{24,0},{1,25},{9,17},{17,9},{25,1},{2,26},{10... | collective-permute-start | bytes 835592 | tf_op jit(solution)/shard_map/ppermute | solution.py:564
  63.9 7.2 %shard_map.110 = (f32[256,512]{1,0:T(8,128)S(1)}, f32[256,512]{1,0:T(8,128)S(1)}, f32[256,512]{1,0:T(8,128)S(1)}) custom-call(bf16[16,256,256]{2,1,0:T(8,128)(2,1)S(1)} %get-tuple-element.92.refs_0_, bf16[16,256,256]{2,1,0:T(8,128)(2,1)S(1)} %get-tuple-element.93.refs_1_, bf16[16,256,256]{2,1,0:T(8,128)(2,1)S(1)} %get-tuple-element.94.refs_2_, ...), custom_call_target="tpu_custom_call" | custom-call | flops 8589934592 | bytes 10485760 | tf_op jit(solution)/shard_map/pallas_call | solution.py:729
  71.2 2.3 %shard_map.111 = (f32[256,512]{1,0:T(8,128)S(1)}, f32[256,512]{1,0:T(8,128)S(1)}) custom-call(bf16[16,256,1024]{2,1,0:T(8,128)(2,1)S(1)} %shard_map.106.refs_13_.refs_0_, bf16[256,512]{1,0:T(8,128)(2,1)S(1)} %get-tuple-element.85.refs_12_.refs_8_.refs_1_, bf16[1024,512]{1,0:T(8,128)(2,1)S(1)} %shard_map.102.refs_1_.refs_2_, ...), custom_call_target="tpu_custom_call" | custom-call | flops 2147483648 | bytes 4194304 | tf_op jit(solution)/shard_map/pallas_call | solution.py:740
  73.5 2.3 %shard_map.112 = (f32[256,512]{1,0:T(8,128)S(1)}, f32[256,512]{1,0:T(8,128)S(1)}) custom-call(bf16[16,256,1024]{2,1,0:T(8,128)(2,1)S(1)} %shard_map.106.refs_13_.refs_0_, bf16[256,512]{1,0:T(8,128)(2,1)S(1)} %get-tuple-element.85.refs_12_.refs_8_.refs_1_, bf16[1024,512]{1,0:T(8,128)(2,1)S(1)} %shard_map.102.refs_1_.refs_2_, ...), custom_call_target="tpu_custom_call" | custom-call | flops 2147483648 | bytes 4194304 | tf_op jit(solution)/shard_map/pallas_call | solution.py:740
  76.3 3.4 %shard_map.113 = bf16[256,512]{1,0:T(8,128)(2,1)} custom-call(bf16[16,256,1024]{2,1,0:T(8,128)(2,1)S(1)} %shard_map.106.refs_13_.refs_0_, bf16[256,512]{1,0:T(8,128)(2,1)S(1)} %get-tuple-element.85.refs_12_.refs_8_.refs_1_, bf16[1024,512]{1,0:T(8,128)(2,1)S(1)} %shard_map.102.refs_1_.refs_2_, f32[256,512]{1,0:T(8,128)S(1)} %get-tuple-element.123.refs_3_, ...), custom_call_target="tpu_custom_call" | custom-call | flops 8589934592 | bytes 14680064 | tf_op jit(solution)/shard_map/pallas_call | solution.py:747
  (48 shorter events, 6.6 us)
Async XLA Ops:
  0.0 9.5 %collective-permute-start = (bf16[256,512]{1,0:T(8,128)(2,1)}, bf16[256,512]{1,0:T(8,128)(2,1)S(1)}, u32[]{:S(2)}, u32[]{:S(2)}) collective-permute-start(bf16[256,512]{1,0:T(8,128)(2,1)} %bitcast.13), channel_id=1, source_target_pairs={{0,16},{8,24},{16,0},{24,8},{1,17},{9,25},{17,1},{25,9},{2,18},{10... | collective-permute-start | bytes 786440 | tf_op jit(solution)/shard_map/ppermute | solution.py:564
  3.0 9.4 %collective-permute-start.1 = (bf16[256,512]{1,0:T(8,128)(2,1)}, bf16[256,512]{1,0:T(8,128)(2,1)S(1)}, u32[]{:S(2)}, u32[]{:S(2)}) collective-permute-start(bf16[256,512]{1,0:T(8,128)(2,1)} %bitcast.14), channel_id=1, source_target_pairs={{0,8},{8,0},{16,24},{24,16},{1,9},{9,1},{17,25},{25,17},{2,10},{10... | collective-permute-start | bytes 786440 | tf_op jit(solution)/shard_map/ppermute | solution.py:564
  4.5 11.8 %collective-permute-start.2 = (bf16[256,512]{1,0:T(8,128)(2,1)}, bf16[256,512]{1,0:T(8,128)(2,1)S(1)}, u32[]{:S(2)}, u32[]{:S(2)}) collective-permute-start(bf16[256,512]{1,0:T(8,128)(2,1)} %bitcast.15), channel_id=1, source_target_pairs={{0,24},{8,16},{16,8},{24,0},{1,25},{9,17},{17,9},{25,1},{2,26},{10... | collective-permute-start | bytes 786440 | tf_op jit(solution)/shard_map/ppermute | solution.py:564
  5.2 1.4 %copy-start = (bf16[512,1536]{1,0:T(8,128)(2,1)S(1)}, bf16[512,1536]{1,0:T(8,128)(2,1)}, u32[]{:S(2)}) copy-start(bf16[512,1536]{1,0:T(8,128)(2,1)} %refs_8_.1) | copy-start | bytes 4718596
  5.2 1.4 %copy-start.1 = (f32[512]{0:T(512)S(1)}, f32[512]{0:T(512)}, u32[]{:S(2)}) copy-start(f32[512]{0:T(512)} %param.11) | copy-start | bytes 6148
  5.2 1.4 %copy-start.5 = (bf16[1,1,256,512]{3,2,1,0:T(8,128)(2,1)S(1)}, bf16[1,1,256,512]{3,2,1,0:T(8,128)(2,1)}, u32[]{:S(2)}) copy-start(bf16[1,1,256,512]{3,2,1,0:T(8,128)(2,1)} %param.10) | copy-start | bytes 786436
  12.4 3.9 %copy-start.4 = (bf16[512,512]{1,0:T(8,128)(2,1)S(1)}, bf16[512,512]{1,0:T(8,128)(2,1)}, u32[]{:S(2)}) copy-start(bf16[512,512]{1,0:T(8,128)(2,1)} %refs_2_.11) | copy-start | bytes 1572868
  16.3 15.3 %copy-start.3 = (bf16[512,512]{1,0:T(8,128)(2,1)S(1)}, bf16[512,512]{1,0:T(8,128)(2,1)}, u32[]{:S(2)}) copy-start(bf16[512,512]{1,0:T(8,128)(2,1)} %out_w_ref.1) | copy-start | bytes 1572868
  16.3 15.3 %copy-start.6 = (bf16[1,1,256,512]{3,2,1,0:T(8,128)(2,1)S(1)}, bf16[1,1,256,512]{3,2,1,0:T(8,128)(2,1)}, u32[]{:S(2)}) copy-start(bf16[1,1,256,512]{3,2,1,0:T(8,128)(2,1)} %param.19) | copy-start | bytes 786436
  16.3 15.3 %copy-start.9 = (s32[1,1,256]{2,1,0:T(1,128)S(1)}, s32[1,1,256]{2,1,0:T(1,128)}, u32[]{:S(2)}) copy-start(s32[1,1,256]{2,1,0:T(1,128)} %param.18) | copy-start | bytes 3076
  16.3 19.5 %copy-start.2 = (bf16[512,1536]{1,0:T(8,128)(2,1)S(1)}, bf16[512,1536]{1,0:T(8,128)(2,1)}, u32[]{:S(2)}) copy-start(bf16[512,1536]{1,0:T(8,128)(2,1)} %refs_2_.10) | copy-start | bytes 4718596
  16.3 19.5 %copy-start.7 = (f32[512]{0:T(512)S(1)}, f32[512]{0:T(512)}, u32[]{:S(2)}) copy-start(f32[512]{0:T(512)} %param.15) | copy-start | bytes 6148
  19.1 6.2 %collective-permute-start.10 = (bf16[264,128]{1,0:T(8,128)(2,1)S(1)}, bf16[264,128]{1,0:T(8,128)(2,1)S(1)}, u32[]{:S(2)}, u32[]{:S(2)}) collective-permute-start(bf16[264,128]{1,0:T(8,128)(2,1)S(1)} %get-tuple-element.110), channel_id=1, source_target_pairs={{0,5},{1,4},{2,7},{3,6},{4,1},{5,0},{6,3},{7,2},{8,13},{9,12},{10,... | collective-permute-start | bytes 202760 | tf_op jit(solution)/shard_map/ppermute | solution.py:564
  20.3 7.7 %collective-permute-start.11 = (bf16[264,128]{1,0:T(8,128)(2,1)S(1)}, bf16[264,128]{1,0:T(8,128)(2,1)S(1)}, u32[]{:S(2)}, u32[]{:S(2)}) collective-permute-start(bf16[264,128]{1,0:T(8,128)(2,1)S(1)} %get-tuple-element.111), channel_id=1, source_target_pairs={{0,6},{1,7},{2,4},{3,5},{4,2},{5,3},{6,0},{7,1},{8,14},{9,15},{10,... | collective-permute-start | bytes 202760 | tf_op jit(solution)/shard_map/ppermute | solution.py:564
  23.1 8.9 %collective-permute-start.12 = (bf16[264,128]{1,0:T(8,128)(2,1)S(1)}, bf16[264,128]{1,0:T(8,128)(2,1)S(1)}, u32[]{:S(2)}, u32[]{:S(2)}) collective-permute-start(bf16[264,128]{1,0:T(8,128)(2,1)S(1)} %get-tuple-element.112), channel_id=1, source_target_pairs={{0,7},{1,6},{2,5},{3,4},{4,3},{5,2},{6,1},{7,0},{8,15},{9,14},{10,... | collective-permute-start | bytes 202760 | tf_op jit(solution)/shard_map/ppermute | solution.py:564
  25.3 6.7 %collective-permute-start.6 = (bf16[264,128]{1,0:T(8,128)(2,1)S(1)}, bf16[264,128]{1,0:T(8,128)(2,1)S(1)}, u32[]{:S(2)}, u32[]{:S(2)}) collective-permute-start(bf16[264,128]{1,0:T(8,128)(2,1)S(1)} %get-tuple-element.106), channel_id=1, source_target_pairs={{0,1},{1,0},{2,3},{3,2},{4,5},{5,4},{6,7},{7,6},{8,9},{9,8},{10,11... | collective-permute-start | bytes 202760 | tf_op jit(solution)/shard_map/ppermute | solution.py:564
  25.3 6.7 %collective-permute-start.7 = (bf16[264,128]{1,0:T(8,128)(2,1)S(1)}, bf16[264,128]{1,0:T(8,128)(2,1)S(1)}, u32[]{:S(2)}, u32[]{:S(2)}) collective-permute-start(bf16[264,128]{1,0:T(8,128)(2,1)S(1)} %get-tuple-element.107), channel_id=1, source_target_pairs={{0,2},{1,3},{2,0},{3,1},{4,6},{5,7},{6,4},{7,5},{8,10},{9,11},{10,... | collective-permute-start | bytes 202760 | tf_op jit(solution)/shard_map/ppermute | solution.py:564
  25.3 7.0 %collective-permute-start.8 = (bf16[264,128]{1,0:T(8,128)(2,1)S(1)}, bf16[264,128]{1,0:T(8,128)(2,1)S(1)}, u32[]{:S(2)}, u32[]{:S(2)}) collective-permute-start(bf16[264,128]{1,0:T(8,128)(2,1)S(1)} %get-tuple-element.108), channel_id=1, source_target_pairs={{0,3},{1,2},{2,1},{3,0},{4,7},{5,6},{6,5},{7,4},{8,11},{9,10},{10,... | collective-permute-start | bytes 202760 | tf_op jit(solution)/shard_map/ppermute | solution.py:564
  28.1 7.8 %collective-permute-start.9 = (bf16[264,128]{1,0:T(8,128)(2,1)S(1)}, bf16[264,128]{1,0:T(8,128)(2,1)S(1)}, u32[]{:S(2)}, u32[]{:S(2)}) collective-permute-start(bf16[264,128]{1,0:T(8,128)(2,1)S(1)} %get-tuple-element.109), channel_id=1, source_target_pairs={{0,4},{1,5},{2,6},{3,7},{4,0},{5,1},{6,2},{7,3},{8,12},{9,13},{10,... | collective-permute-start | bytes 202760 | tf_op jit(solution)/shard_map/ppermute | solution.py:564
  41.4 8.8 %collective-permute-start.13 = (bf16[64,512]{1,0:T(8,128)(2,1)S(1)}, bf16[64,512]{1,0:T(8,128)(2,1)S(1)}, u32[]{:S(2)}, u32[]{:S(2)}) collective-permute-start(bf16[64,512]{1,0:T(8,128)(2,1)S(1)} %get-tuple-element.114), channel_id=1, source_target_pairs={{0,1},{1,0},{2,3},{3,2},{4,5},{5,4},{6,7},{7,6},{8,9},{9,8},{10,11... | collective-permute-start | bytes 196616 | tf_op jit(solution)/shard_map/ppermute | solution.py:564
  41.6 10.7 %collective-permute-start.14 = (bf16[64,512]{1,0:T(8,128)(2,1)S(1)}, bf16[64,512]{1,0:T(8,128)(2,1)S(1)}, u32[]{:S(2)}, u32[]{:S(2)}) collective-permute-start(bf16[64,512]{1,0:T(8,128)(2,1)S(1)} %get-tuple-element.115), channel_id=1, source_target_pairs={{0,2},{1,3},{2,0},{3,1},{4,6},{5,7},{6,4},{7,5},{8,10},{9,11},{10,... | collective-permute-start | bytes 196616 | tf_op jit(solution)/shard_map/ppermute | solution.py:564
  41.9 4.2 %collective-permute-start.3 = (f32[16,256]{1,0:T(8,128)S(1)}, f32[16,256]{1,0:T(8,128)S(1)}, u32[]{:S(2)}, u32[]{:S(2)}) collective-permute-start(f32[16,256]{1,0:T(8,128)S(1)} %get-tuple-element.91.refs_2_), channel_id=1, source_target_pairs={{0,16},{8,24},{16,0},{24,8},{1,17},{9,25},{17,1},{25,9},{2,18},{10... | collective-permute-start | bytes 49160 | tf_op jit(solution)/shard_map/ppermute | solution.py:564
  43.9 3.9 %collective-permute-start.4 = (f32[16,256]{1,0:T(8,128)S(1)}, f32[16,256]{1,0:T(8,128)S(1)}, u32[]{:S(2)}, u32[]{:S(2)}) collective-permute-start(f32[16,256]{1,0:T(8,128)S(1)} %get-tuple-element.91.refs_2_), channel_id=1, source_target_pairs={{0,8},{8,0},{16,24},{24,16},{1,9},{9,1},{17,25},{25,17},{2,10},{10... | collective-permute-start | bytes 49160 | tf_op jit(solution)/shard_map/ppermute | solution.py:564
  45.4 4.6 %collective-permute-start.5 = (f32[16,256]{1,0:T(8,128)S(1)}, f32[16,256]{1,0:T(8,128)S(1)}, u32[]{:S(2)}, u32[]{:S(2)}) collective-permute-start(f32[16,256]{1,0:T(8,128)S(1)} %get-tuple-element.91.refs_2_), channel_id=1, source_target_pairs={{0,24},{8,16},{16,8},{24,0},{1,25},{9,17},{17,9},{25,1},{2,26},{10... | collective-permute-start | bytes 49160 | tf_op jit(solution)/shard_map/ppermute | solution.py:564
  46.1 10.5 %collective-permute-start.15 = (bf16[64,512]{1,0:T(8,128)(2,1)S(1)}, bf16[64,512]{1,0:T(8,128)(2,1)S(1)}, u32[]{:S(2)}, u32[]{:S(2)}) collective-permute-start(bf16[64,512]{1,0:T(8,128)(2,1)S(1)} %get-tuple-element.116), channel_id=1, source_target_pairs={{0,3},{1,2},{2,1},{3,0},{4,7},{5,6},{6,5},{7,4},{8,11},{9,10},{10,... | collective-permute-start | bytes 196616 | tf_op jit(solution)/shard_map/ppermute | solution.py:564
  47.7 9.4 %collective-permute-start.16 = (bf16[64,512]{1,0:T(8,128)(2,1)S(1)}, bf16[64,512]{1,0:T(8,128)(2,1)S(1)}, u32[]{:S(2)}, u32[]{:S(2)}) collective-permute-start(bf16[64,512]{1,0:T(8,128)(2,1)S(1)} %get-tuple-element.117), channel_id=1, source_target_pairs={{0,4},{1,5},{2,6},{3,7},{4,0},{5,1},{6,2},{7,3},{8,12},{9,13},{10,... | collective-permute-start | bytes 196616 | tf_op jit(solution)/shard_map/ppermute | solution.py:564
  50.0 9.6 %collective-permute-start.17 = (bf16[64,512]{1,0:T(8,128)(2,1)S(1)}, bf16[64,512]{1,0:T(8,128)(2,1)S(1)}, u32[]{:S(2)}, u32[]{:S(2)}) collective-permute-start(bf16[64,512]{1,0:T(8,128)(2,1)S(1)} %get-tuple-element.118), channel_id=1, source_target_pairs={{0,5},{1,4},{2,7},{3,6},{4,1},{5,0},{6,3},{7,2},{8,13},{9,12},{10,... | collective-permute-start | bytes 196616 | tf_op jit(solution)/shard_map/ppermute | solution.py:564
  50.2 9.4 %collective-permute-start.18 = (bf16[64,512]{1,0:T(8,128)(2,1)S(1)}, bf16[64,512]{1,0:T(8,128)(2,1)S(1)}, u32[]{:S(2)}, u32[]{:S(2)}) collective-permute-start(bf16[64,512]{1,0:T(8,128)(2,1)S(1)} %get-tuple-element.119), channel_id=1, source_target_pairs={{0,6},{1,7},{2,4},{3,5},{4,2},{5,3},{6,0},{7,1},{8,14},{9,15},{10,... | collective-permute-start | bytes 196616 | tf_op jit(solution)/shard_map/ppermute | solution.py:564
  52.3 7.3 %collective-permute-start.19 = (bf16[64,512]{1,0:T(8,128)(2,1)S(1)}, bf16[64,512]{1,0:T(8,128)(2,1)S(1)}, u32[]{:S(2)}, u32[]{:S(2)}) collective-permute-start(bf16[64,512]{1,0:T(8,128)(2,1)S(1)} %get-tuple-element.120), channel_id=1, source_target_pairs={{0,7},{1,6},{2,5},{3,4},{4,3},{5,2},{6,1},{7,0},{8,15},{9,14},{10,... | collective-permute-start | bytes 196616 | tf_op jit(solution)/shard_map/ppermute | solution.py:564
  60.4 10.8 %collective-permute-start.20 = (bf16[272,512]{1,0:T(8,128)(2,1)S(1)}, bf16[272,512]{1,0:T(8,128)(2,1)S(1)}, u32[]{:S(2)}, u32[]{:S(2)}) collective-permute-start(bf16[272,512]{1,0:T(8,128)(2,1)S(1)} %get-tuple-element.121.refs_14_), channel_id=1, source_target_pairs={{0,16},{8,24},{16,0},{24,8},{1,17},{9,25},{17,1},{25,9},{2,18},{10... | collective-permute-start | bytes 835592 | tf_op jit(solution)/shard_map/ppermute | solution.py:564
  61.1 12.3 %collective-permute-start.21 = (bf16[272,512]{1,0:T(8,128)(2,1)S(1)}, bf16[272,512]{1,0:T(8,128)(2,1)S(1)}, u32[]{:S(2)}, u32[]{:S(2)}) collective-permute-start(bf16[272,512]{1,0:T(8,128)(2,1)S(1)} %get-tuple-element.121.refs_14_), channel_id=1, source_target_pairs={{0,8},{8,0},{16,24},{24,16},{1,9},{9,1},{17,25},{25,17},{2,10},{10... | collective-permute-start | bytes 835592 | tf_op jit(solution)/shard_map/ppermute | solution.py:564
  62.6 13.7 %collective-permute-start.22 = (bf16[272,512]{1,0:T(8,128)(2,1)S(1)}, bf16[272,512]{1,0:T(8,128)(2,1)S(1)}, u32[]{:S(2)}, u32[]{:S(2)}) collective-permute-start(bf16[272,512]{1,0:T(8,128)(2,1)S(1)} %get-tuple-element.121.refs_14_), channel_id=1, source_target_pairs={{0,24},{8,16},{16,8},{24,0},{1,25},{9,17},{17,9},{25,1},{2,26},{10... | collective-permute-start | bytes 835592 | tf_op jit(solution)/shard_map/ppermute | solution.py:564
  (1 other events, 0.7 us)

commit v5 on v4

--- a/solution.py
+++ b/solution.py
@@ -431,17 +431,19 @@
 def key_tile(depth, t, v_tile, weights_ref, columns, queries, grads, deltas_ref):
     count = v_tile.shape[0]
     heads = LANES // depth
-    dk = jnp.zeros((count, LANES), F32)
-    dv = jnp.zeros((count, LANES), F32)
-    for j in range(heads):
-        h = t * heads + j
-        mask = head_mask(count, j, depth)
-        weights = weights_ref[h, :, columns]
-        weight_grad = dot_nt(only(mask, v_tile), grads)
-        delta = deltas_ref[pl.ds(h, 1)]
-        score_grad = (weights.astype(F32) * (weight_grad - delta)).astype(BF16)
-        dv = jnp.where(mask, dot_nn(weights, grads), dv)
-        dk = jnp.where(mask, dot_nn(score_grad, queries), dk)
+    masks = [head_mask(count, j, depth) for j in range(heads)]
+    v_heads = jnp.concatenate([only(mask, v_tile) for mask in masks], axis=0)
+    weights = weights_ref[t * heads : (t + 1) * heads, :, columns]
+    weight_grad = dot_nt(v_heads, grads).reshape(weights.shape)
+    delta = deltas_ref[t * heads : (t + 1) * heads][:, None, :]
+    score_grad = (weights.astype(F32) * (weight_grad - delta)).astype(BF16)
+    dv_heads = dot_nn(weights.reshape(heads * count, -1), grads)
+    dk_heads = dot_nn(score_grad.reshape(heads * count, -1), queries)
+    dk, dv = dk_heads[:count], dv_heads[:count]
+    for j in range(1, heads):
+        part = slice(j * count, (j + 1) * count)
+        dk = jnp.where(masks[j], dk_heads[part], dk)
+        dv = jnp.where(masks[j], dv_heads[part], dv)
     return dk, dv
 
 

time: 80.2 us -> 79.8 us (level)
  Pallas kernels: 33.7 us -> 32.1 us
  waiting for transfers between devices: 14 us -> 15.3 us
    ppermute x23, waiting for transfers between devices: 14 us -> 15.3 us  [by_xor(): return lax.ppermute(array, axis, [(i, i ^ step) for i in range(size)])]
    pallas_call x2, Pallas kernels: 4.56 us -> 3.69 us  [shards(): vmem_call(functools.partial(key_middle_body, index, depth), (rows_f32, ro...]
  transfers between devices with their start and end apart: 23 -> 23, of which waited for: 10 -> 10; matrix products, arithmetic and copies ran while one was open for 0% -> 0% of each run, Pallas kernels for 27% -> 25%
where the time goes in v5:
time: 79.8 us; the launch traced here: 79.3 us
  Pallas kernels  32.1 us (40%)
  starting transfers between devices  30.1 us (38%)
  waiting for transfers between devices  15.3 us (19%)
  local copies, waits for them, and re-layouts  1.61 us (2%)
    ppermute x23, starting transfers between devices, by_xor(): return lax.ppermute(array, axis, [(i, i ^ step) for i in range(size)])  30.1 us
    ppermute x23, waiting for transfers between devices, by_xor(): return lax.ppermute(array, axis, [(i, i ^ step) for i in range(size)])  15.3 us
    pallas_call x1, Pallas kernels, shards(): vmem_call(functools.partial(query_grad_body, len(all_keys), depth), (rows...  6.84 us
    pallas_call x1, Pallas kernels, shards(): vmem_call(functools.partial(second_body, chunks, depth), (chunk_bf16,) *...  5.58 us
    pallas_call x2, Pallas kernels, shards(): vmem_call(functools.partial(key_middle_body, index, depth), (rows_f32, ro...  3.69 us
    pallas_call x2, Pallas kernels, shards(): vmem_call(functools.partial(middle_body, depth), (rows_bf16,) * 2 + (squa...  3.58 us
    pallas_call x1, Pallas kernels, shards(): vmem_call(functools.partial(key_grad_body, early, peers, depth), rows_bf1...  3.01 us
    pallas_call x1, Pallas kernels, shards(): vmem_call(functools.partial(forward_body, early, peers, chunks, capacity,...  2.77 us
  transfers between devices with their start and end apart: 23, of which 10 were waited for; matrix products, arithmetic and copies ran while one was open for 0% of the time, Pallas kernels for 25%

profile of v5, /device:TPU:0, one launch (start us, length us, event | category | flops | bytes accessed | tf_op | source)
XLA Modules:
  0.0 79.3 jit_solution(10467809758532546111)
XLA Ops:
  0.0 3.0 %collective-permute-start = (bf16[256,512]{1,0:T(8,128)(2,1)}, bf16[256,512]{1,0:T(8,128)(2,1)S(1)}, u32[]{:S(2)}, u32[]{:S(2)}) collective-permute-start(bf16[256,512]{1,0:T(8,128)(2,1)} %bitcast.13), channel_id=1, source_target_pairs={{0,16},{8,24},{16,0},{24,8},{1,17},{9,25},{17,1},{25,9},{2,18},{10... | collective-permute-start | bytes 786440 | tf_op jit(solution)/shard_map/ppermute | solution.py:566
  3.0 1.5 %collective-permute-start.1 = (bf16[256,512]{1,0:T(8,128)(2,1)}, bf16[256,512]{1,0:T(8,128)(2,1)S(1)}, u32[]{:S(2)}, u32[]{:S(2)}) collective-permute-start(bf16[256,512]{1,0:T(8,128)(2,1)} %bitcast.14), channel_id=1, source_target_pairs={{0,8},{8,0},{16,24},{24,16},{1,9},{9,1},{17,25},{25,17},{2,10},{10... | collective-permute-start | bytes 786440 | tf_op jit(solution)/shard_map/ppermute | solution.py:566
  5.7 0.9 %copy-done = bf16[512,1536]{1,0:T(8,128)(2,1)S(1)} copy-done((bf16[512,1536]{1,0:T(8,128)(2,1)S(1)}, bf16[512,1536]{1,0:T(8,128)(2,1)}, u32[]{:S(2)}) %copy-start) | copy-done | bytes 1572888
  6.6 1.9 %shard_map.101 = (bf16[256,512]{1,0:T(8,128)(2,1)S(1)}, bf16[256,512]{1,0:T(8,128)(2,1)S(1)}, bf16[256,512]{1,0:T(8,128)(2,1)S(1)}, bf16[16,256,256]{2,1,0:T(8,1...) custom-call(bf16[256,512]{1,0:T(8,128)(2,1)S(1)} %bitcast.16, ...), custom_call_target="tpu_custom_call" | custom-call | flops 2147483648 | bytes 4194304 | tf_op jit(solution)/shard_map/pallas_call | solution.py:628
  8.6 1.0 %collective-permute-done.refs_3_.refs_0_ = bf16[256,512]{1,0:T(8,128)(2,1)S(1)} collective-permute-done((bf16[256,512]{1,0:T(8,128)(2,1)}, bf16[256,512]{1,0:T(8,128)(2,1)S(1)}, u32[]{:S(2)}, u32[]{:S(2)}) %collective-permute-start) | collective-permute-done | bytes 262176 | tf_op jit(solution)/shard_map/ppermute | solution.py:566
  9.5 1.8 %shard_map.103 = (bf16[256,512]{1,0:T(8,128)(2,1)S(1)}, bf16[256,512]{1,0:T(8,128)(2,1)S(1)}, bf16[16,256,256]{2,1,0:T(8,128)(2,1)S(1)}, f32[256,512]{1,0:T(8,128)S(1)}, f32[256,512]{1,0:T(8,128)S(1)}) custom-call(bf16[256,512]{1,0:T(8,128)(2,1)S(1)} %collective-permute-done.refs_3_.refs_0_, f32[1,512]{1,0:T(1,128)S(1)} %bitcast.9, ...), custom_call_target="tpu_custom_call" | custom-call | flops 2147483648 | bytes 4194304 | tf_op jit(solution)/shard_map/pallas_call | solution.py:636
  11.3 1.1 %collective-permute-done.1.refs_4_.refs_0_ = bf16[256,512]{1,0:T(8,128)(2,1)S(1)} collective-permute-done((bf16[256,512]{1,0:T(8,128)(2,1)}, bf16[256,512]{1,0:T(8,128)(2,1)S(1)}, u32[]{:S(2)}, u32[]{:S(2)}) %collective-permute-start.1) | collective-permute-done | bytes 262176 | tf_op jit(solution)/shard_map/ppermute | solution.py:566
  12.4 1.8 %shard_map.104 = (bf16[256,512]{1,0:T(8,128)(2,1)S(1)}, bf16[256,512]{1,0:T(8,128)(2,1)S(1)}, bf16[16,256,256]{2,1,0:T(8,128)(2,1)S(1)}, f32[256,512]{1,0:T(8,128)S(1)}, f32[256,512]{1,0:T(8,128)S(1)}) custom-call(bf16[256,512]{1,0:T(8,128)(2,1)S(1)} %collective-permute-done.1.refs_4_.refs_0_, f32[1,512]{1,0:T(1,128)S(1)} %bitcast.10, ...), custom_call_target="tpu_custom_call" | custom-call | flops 2147483648 | bytes 4194304 | tf_op jit(solution)/shard_map/pallas_call | solution.py:636
  14.2 2.1 %collective-permute-done.2.refs_5_.refs_15_ = bf16[256,512]{1,0:T(8,128)(2,1)S(1)} collective-permute-done((bf16[256,512]{1,0:T(8,128)(2,1)}, bf16[256,512]{1,0:T(8,128)(2,1)S(1)}, u32[]{:S(2)}, u32[]{:S(2)}) %collective-permute-start.2) | collective-permute-done | bytes 262176 | tf_op jit(solution)/shard_map/ppermute | solution.py:566
  16.4 2.8 %shard_map.105 = (bf16[256,512]{1,0:T(8,128)(2,1)S(1)}, bf16[256,512]{1,0:T(8,128)(2,1)S(1)}, bf16[16,256,256]{2,1,0:T(8,128)(2,1)S(1)}, f32[256,512]{1,0:T(8,12...) custom-call(bf16[256,512]{1,0:T(8,128)(2,1)S(1)} %bitcast.17, ...), custom_call_target="tpu_custom_call", output_to_operand_aliasing={{6}: (16, {}), {7}: (17, {}), {8}: (18, {})} | custom-call | flops 8589934592 | bytes 8388608 | tf_op jit(solution)/shard_map/pallas_call | solution.py:651
  19.1 1.2 %collective-permute-start.10 = (bf16[264,128]{1,0:T(8,128)(2,1)S(1)}, bf16[264,128]{1,0:T(8,128)(2,1)S(1)}, u32[]{:S(2)}, u32[]{:S(2)}) collective-permute-start(bf16[264,128]{1,0:T(8,128)(2,1)S(1)} %get-tuple-element.110), channel_id=1, source_target_pairs={{0,5},{1,4},{2,7},{3,6},{4,1},{5,0},{6,3},{7,2},{8,13},{9,12},{10,... | collective-permute-start | bytes 202760 | tf_op jit(solution)/shard_map/ppermute | solution.py:566
  20.3 2.8 %collective-permute-start.11 = (bf16[264,128]{1,0:T(8,128)(2,1)S(1)}, bf16[264,128]{1,0:T(8,128)(2,1)S(1)}, u32[]{:S(2)}, u32[]{:S(2)}) collective-permute-start(bf16[264,128]{1,0:T(8,128)(2,1)S(1)} %get-tuple-element.111), channel_id=1, source_target_pairs={{0,6},{1,7},{2,4},{3,5},{4,2},{5,3},{6,0},{7,1},{8,14},{9,15},{10,... | collective-permute-start | bytes 202760 | tf_op jit(solution)/shard_map/ppermute | solution.py:566
  23.1 2.2 %collective-permute-start.12 = (bf16[264,128]{1,0:T(8,128)(2,1)S(1)}, bf16[264,128]{1,0:T(8,128)(2,1)S(1)}, u32[]{:S(2)}, u32[]{:S(2)}) collective-permute-start(bf16[264,128]{1,0:T(8,128)(2,1)S(1)} %get-tuple-element.112), channel_id=1, source_target_pairs={{0,7},{1,6},{2,5},{3,4},{4,3},{5,2},{6,1},{7,0},{8,15},{9,14},{10,... | collective-permute-start | bytes 202760 | tf_op jit(solution)/shard_map/ppermute | solution.py:566
  25.3 2.8 %collective-permute-start.8 = (bf16[264,128]{1,0:T(8,128)(2,1)S(1)}, bf16[264,128]{1,0:T(8,128)(2,1)S(1)}, u32[]{:S(2)}, u32[]{:S(2)}) collective-permute-start(bf16[264,128]{1,0:T(8,128)(2,1)S(1)} %get-tuple-element.108), channel_id=1, source_target_pairs={{0,3},{1,2},{2,1},{3,0},{4,7},{5,6},{6,5},{7,4},{8,11},{9,10},{10,... | collective-permute-start | bytes 202760 | tf_op jit(solution)/shard_map/ppermute | solution.py:566
  28.1 3.6 %collective-permute-start.9 = (bf16[264,128]{1,0:T(8,128)(2,1)S(1)}, bf16[264,128]{1,0:T(8,128)(2,1)S(1)}, u32[]{:S(2)}, u32[]{:S(2)}) collective-permute-start(bf16[264,128]{1,0:T(8,128)(2,1)S(1)} %get-tuple-element.109), channel_id=1, source_target_pairs={{0,4},{1,5},{2,6},{3,7},{4,0},{5,1},{6,2},{7,3},{8,12},{9,13},{10,... | collective-permute-start | bytes 202760 | tf_op jit(solution)/shard_map/ppermute | solution.py:566
  32.3 3.5 %collective-permute-done.9.refs_10_ = bf16[264,128]{1,0:T(8,128)(2,1)S(1)} collective-permute-done((bf16[264,128]{1,0:T(8,128)(2,1)S(1)}, bf16[264,128]{1,0:T(8,128)(2,1)S(1)}, u32[]{:S(2)}, u32[]{:S(2)}) %collective-permute-start.9) | collective-permute-done | bytes 67616 | tf_op jit(solution)/shard_map/ppermute | solution.py:566
  35.8 5.6 %shard_map.108 = (bf16[64,512]{1,0:T(8,128)(2,1)S(1)}, bf16[64,512]{1,0:T(8,128)(2,1)S(1)}, bf16[64,512]{1,0:T(8,128)(2,1)S(1)}, bf16[64,512]{1,0:T(8,128)(2,1)S...) custom-call(f32[1,512]{1,0:T(1,128)S(1)} %get-tuple-element.76.refs_, ...), custom_call_target="tpu_custom_call" | custom-call | flops 8589934592 | bytes 4194304 | tf_op jit(solution)/shard_map/pallas_call | solution.py:706
  41.9 2.0 %collective-permute-start.3 = (f32[16,256]{1,0:T(8,128)S(1)}, f32[16,256]{1,0:T(8,128)S(1)}, u32[]{:S(2)}, u32[]{:S(2)}) collective-permute-start(f32[16,256]{1,0:T(8,128)S(1)} %get-tuple-element.91.refs_2_), channel_id=1, source_target_pairs={{0,16},{8,24},{16,0},{24,8},{1,17},{9,25},{17,1},{25,9},{2,18},{10... | collective-permute-start | bytes 49160 | tf_op jit(solution)/shard_map/ppermute | solution.py:566
  43.9 1.5 %collective-permute-start.4 = (f32[16,256]{1,0:T(8,128)S(1)}, f32[16,256]{1,0:T(8,128)S(1)}, u32[]{:S(2)}, u32[]{:S(2)}) collective-permute-start(f32[16,256]{1,0:T(8,128)S(1)} %get-tuple-element.91.refs_2_), channel_id=1, source_target_pairs={{0,8},{8,0},{16,24},{24,16},{1,9},{9,1},{17,25},{25,17},{2,10},{10... | collective-permute-start | bytes 49160 | tf_op jit(solution)/shard_map/ppermute | solution.py:566
  46.8 1.0 %collective-permute-done.4.refs_4_ = f32[16,256]{1,0:T(8,128)S(1)} collective-permute-done((f32[16,256]{1,0:T(8,128)S(1)}, f32[16,256]{1,0:T(8,128)S(1)}, u32[]{:S(2)}, u32[]{:S(2)}) %collective-permute-start.4) | collective-permute-done | bytes 16416 | tf_op jit(solution)/shard_map/ppermute | solution.py:566
  48.6 1.5 %collective-permute-done.5.refs_5_ = f32[16,256]{1,0:T(8,128)S(1)} collective-permute-done((f32[16,256]{1,0:T(8,128)S(1)}, f32[16,256]{1,0:T(8,128)S(1)}, u32[]{:S(2)}, u32[]{:S(2)}) %collective-permute-start.5) | collective-permute-done | bytes 16416 | tf_op jit(solution)/shard_map/ppermute | solution.py:566
  50.2 2.1 %collective-permute-start.18 = (bf16[64,512]{1,0:T(8,128)(2,1)S(1)}, bf16[64,512]{1,0:T(8,128)(2,1)S(1)}, u32[]{:S(2)}, u32[]{:S(2)}) collective-permute-start(bf16[64,512]{1,0:T(8,128)(2,1)S(1)} %get-tuple-element.119), channel_id=1, source_target_pairs={{0,6},{1,7},{2,4},{3,5},{4,2},{5,3},{6,0},{7,1},{8,14},{9,15},{10,... | collective-permute-start | bytes 196616 | tf_op jit(solution)/shard_map/ppermute | solution.py:566
  52.3 1.9 %collective-permute-start.19 = (bf16[64,512]{1,0:T(8,128)(2,1)S(1)}, bf16[64,512]{1,0:T(8,128)(2,1)S(1)}, u32[]{:S(2)}, u32[]{:S(2)}) collective-permute-start(bf16[64,512]{1,0:T(8,128)(2,1)S(1)} %get-tuple-element.120), channel_id=1, source_target_pairs={{0,7},{1,6},{2,5},{3,4},{4,3},{5,2},{6,1},{7,0},{8,15},{9,14},{10,... | collective-permute-start | bytes 196616 | tf_op jit(solution)/shard_map/ppermute | solution.py:566
  54.2 2.3 %shard_map.106.refs_13_.refs_0_ = bf16[16,256,1024]{2,1,0:T(8,128)(2,1)S(1)} custom-call(bf16[256,512]{1,0:T(8,128)(2,1)S(1)} %get-tuple-element.73.refs_9_.refs_0_.refs_4_, bf16[1024,512]{1,0:T(8,128)(2,1)S(1)} %shard_map.102.refs_1_.refs_2_, f32[16,256]{1,0:T(8,128)S(1)} %get-tuple-element.91.refs_2_, f32[16,256]{1,0:T(8,128)S(1)} %collective-permute-done.3.refs_3_, ...), custom_call_target="tpu_custom_call" | custom-call | flops 4294967296 | bytes 10485760 | tf_op jit(solution)/shard_map/pallas_call | solution.py:696
  57.1 2.5 %collective-permute-done.17.refs_8_ = bf16[64,512]{1,0:T(8,128)(2,1)S(1)} collective-permute-done((bf16[64,512]{1,0:T(8,128)(2,1)S(1)}, bf16[64,512]{1,0:T(8,128)(2,1)S(1)}, u32[]{:S(2)}, u32[]{:S(2)}) %collective-permute-start.17) | collective-permute-done | bytes 65568 | tf_op jit(solution)/shard_map/ppermute | solution.py:566
  61.1 1.5 %collective-permute-start.21 = (bf16[272,512]{1,0:T(8,128)(2,1)S(1)}, bf16[272,512]{1,0:T(8,128)(2,1)S(1)}, u32[]{:S(2)}, u32[]{:S(2)}) collective-permute-start(bf16[272,512]{1,0:T(8,128)(2,1)S(1)} %get-tuple-element.121.refs_14_), channel_id=1, source_target_pairs={{0,8},{8,0},{16,24},{24,16},{1,9},{9,1},{17,25},{25,17},{2,10},{10... | collective-permute-start | bytes 835592 | tf_op jit(solution)/shard_map/ppermute | solution.py:566
  62.6 1.3 %collective-permute-start.22 = (bf16[272,512]{1,0:T(8,128)(2,1)S(1)}, bf16[272,512]{1,0:T(8,128)(2,1)S(1)}, u32[]{:S(2)}, u32[]{:S(2)}) collective-permute-start(bf16[272,512]{1,0:T(8,128)(2,1)S(1)} %get-tuple-element.121.refs_14_), channel_id=1, source_target_pairs={{0,24},{8,16},{16,8},{24,0},{1,25},{9,17},{17,9},{25,1},{2,26},{10... | collective-permute-start | bytes 835592 | tf_op jit(solution)/shard_map/ppermute | solution.py:566
  63.9 6.8 %shard_map.110 = (f32[256,512]{1,0:T(8,128)S(1)}, f32[256,512]{1,0:T(8,128)S(1)}, f32[256,512]{1,0:T(8,128)S(1)}) custom-call(bf16[16,256,256]{2,1,0:T(8,128)(2,1)S(1)} %get-tuple-element.92.refs_0_, bf16[16,256,256]{2,1,0:T(8,128)(2,1)S(1)} %get-tuple-element.93.refs_1_, bf16[16,256,256]{2,1,0:T(8,128)(2,1)S(1)} %get-tuple-element.94.refs_2_, ...), custom_call_target="tpu_custom_call" | custom-call | flops 8589934592 | bytes 10485760 | tf_op jit(solution)/shard_map/pallas_call | solution.py:731
  70.8 1.8 %shard_map.111 = (f32[256,512]{1,0:T(8,128)S(1)}, f32[256,512]{1,0:T(8,128)S(1)}) custom-call(bf16[16,256,1024]{2,1,0:T(8,128)(2,1)S(1)} %shard_map.106.refs_13_.refs_0_, bf16[256,512]{1,0:T(8,128)(2,1)S(1)} %get-tuple-element.85.refs_12_.refs_8_.refs_1_, bf16[1024,512]{1,0:T(8,128)(2,1)S(1)} %shard_map.102.refs_1_.refs_2_, ...), custom_call_target="tpu_custom_call" | custom-call | flops 2147483648 | bytes 4194304 | tf_op jit(solution)/shard_map/pallas_call | solution.py:742
  72.7 1.8 %shard_map.112 = (f32[256,512]{1,0:T(8,128)S(1)}, f32[256,512]{1,0:T(8,128)S(1)}) custom-call(bf16[16,256,1024]{2,1,0:T(8,128)(2,1)S(1)} %shard_map.106.refs_13_.refs_0_, bf16[256,512]{1,0:T(8,128)(2,1)S(1)} %get-tuple-element.85.refs_12_.refs_8_.refs_1_, bf16[1024,512]{1,0:T(8,128)(2,1)S(1)} %shard_map.102.refs_1_.refs_2_, ...), custom_call_target="tpu_custom_call" | custom-call | flops 2147483648 | bytes 4194304 | tf_op jit(solution)/shard_map/pallas_call | solution.py:742
  74.5 1.8 %collective-permute-done.22.refs_10_ = bf16[272,512]{1,0:T(8,128)(2,1)S(1)} collective-permute-done((bf16[272,512]{1,0:T(8,128)(2,1)S(1)}, bf16[272,512]{1,0:T(8,128)(2,1)S(1)}, u32[]{:S(2)}, u32[]{:S(2)}) %collective-permute-start.22) | collective-permute-done | bytes 278560 | tf_op jit(solution)/shard_map/ppermute | solution.py:566
  76.3 3.0 %shard_map.113 = bf16[256,512]{1,0:T(8,128)(2,1)} custom-call(bf16[16,256,1024]{2,1,0:T(8,128)(2,1)S(1)} %shard_map.106.refs_13_.refs_0_, bf16[256,512]{1,0:T(8,128)(2,1)S(1)} %get-tuple-element.85.refs_12_.refs_8_.refs_1_, bf16[1024,512]{1,0:T(8,128)(2,1)S(1)} %shard_map.102.refs_1_.refs_2_, f32[256,512]{1,0:T(8,128)S(1)} %get-tuple-element.123.refs_3_, ...), custom_call_target="tpu_custom_call" | custom-call | flops 8589934592 | bytes 14680064 | tf_op jit(solution)/shard_map/pallas_call | solution.py:749
  (48 shorter events, 6.9 us)
Async XLA Ops:
  0.0 9.5 %collective-permute-start = (bf16[256,512]{1,0:T(8,128)(2,1)}, bf16[256,512]{1,0:T(8,128)(2,1)S(1)}, u32[]{:S(2)}, u32[]{:S(2)}) collective-permute-start(bf16[256,512]{1,0:T(8,128)(2,1)} %bitcast.13), channel_id=1, source_target_pairs={{0,16},{8,24},{16,0},{24,8},{1,17},{9,25},{17,1},{25,9},{2,18},{10... | collective-permute-start | bytes 786440 | tf_op jit(solution)/shard_map/ppermute | solution.py:566
  3.0 9.4 %collective-permute-start.1 = (bf16[256,512]{1,0:T(8,128)(2,1)}, bf16[256,512]{1,0:T(8,128)(2,1)S(1)}, u32[]{:S(2)}, u32[]{:S(2)}) collective-permute-start(bf16[256,512]{1,0:T(8,128)(2,1)} %bitcast.14), channel_id=1, source_target_pairs={{0,8},{8,0},{16,24},{24,16},{1,9},{9,1},{17,25},{25,17},{2,10},{10... | collective-permute-start | bytes 786440 | tf_op jit(solution)/shard_map/ppermute | solution.py:566
  4.5 11.8 %collective-permute-start.2 = (bf16[256,512]{1,0:T(8,128)(2,1)}, bf16[256,512]{1,0:T(8,128)(2,1)S(1)}, u32[]{:S(2)}, u32[]{:S(2)}) collective-permute-start(bf16[256,512]{1,0:T(8,128)(2,1)} %bitcast.15), channel_id=1, source_target_pairs={{0,24},{8,16},{16,8},{24,0},{1,25},{9,17},{17,9},{25,1},{2,26},{10... | collective-permute-start | bytes 786440 | tf_op jit(solution)/shard_map/ppermute | solution.py:566
  5.2 1.4 %copy-start = (bf16[512,1536]{1,0:T(8,128)(2,1)S(1)}, bf16[512,1536]{1,0:T(8,128)(2,1)}, u32[]{:S(2)}) copy-start(bf16[512,1536]{1,0:T(8,128)(2,1)} %refs_8_.1) | copy-start | bytes 4718596
  5.2 1.4 %copy-start.1 = (f32[512]{0:T(512)S(1)}, f32[512]{0:T(512)}, u32[]{:S(2)}) copy-start(f32[512]{0:T(512)} %param.11) | copy-start | bytes 6148
  5.2 1.4 %copy-start.5 = (bf16[1,1,256,512]{3,2,1,0:T(8,128)(2,1)S(1)}, bf16[1,1,256,512]{3,2,1,0:T(8,128)(2,1)}, u32[]{:S(2)}) copy-start(bf16[1,1,256,512]{3,2,1,0:T(8,128)(2,1)} %param.10) | copy-start | bytes 786436
  12.4 3.9 %copy-start.4 = (bf16[512,512]{1,0:T(8,128)(2,1)S(1)}, bf16[512,512]{1,0:T(8,128)(2,1)}, u32[]{:S(2)}) copy-start(bf16[512,512]{1,0:T(8,128)(2,1)} %refs_2_.11) | copy-start | bytes 1572868
  16.3 15.3 %copy-start.3 = (bf16[512,512]{1,0:T(8,128)(2,1)S(1)}, bf16[512,512]{1,0:T(8,128)(2,1)}, u32[]{:S(2)}) copy-start(bf16[512,512]{1,0:T(8,128)(2,1)} %out_w_ref.1) | copy-start | bytes 1572868
  16.3 15.3 %copy-start.6 = (bf16[1,1,256,512]{3,2,1,0:T(8,128)(2,1)S(1)}, bf16[1,1,256,512]{3,2,1,0:T(8,128)(2,1)}, u32[]{:S(2)}) copy-start(bf16[1,1,256,512]{3,2,1,0:T(8,128)(2,1)} %param.19) | copy-start | bytes 786436
  16.3 15.3 %copy-start.9 = (s32[1,1,256]{2,1,0:T(1,128)S(1)}, s32[1,1,256]{2,1,0:T(1,128)}, u32[]{:S(2)}) copy-start(s32[1,1,256]{2,1,0:T(1,128)} %param.18) | copy-start | bytes 3076
  16.3 19.5 %copy-start.2 = (bf16[512,1536]{1,0:T(8,128)(2,1)S(1)}, bf16[512,1536]{1,0:T(8,128)(2,1)}, u32[]{:S(2)}) copy-start(bf16[512,1536]{1,0:T(8,128)(2,1)} %refs_2_.10) | copy-start | bytes 4718596
  16.3 19.5 %copy-start.7 = (f32[512]{0:T(512)S(1)}, f32[512]{0:T(512)}, u32[]{:S(2)}) copy-start(f32[512]{0:T(512)} %param.15) | copy-start | bytes 6148
  19.1 6.2 %collective-permute-start.10 = (bf16[264,128]{1,0:T(8,128)(2,1)S(1)}, bf16[264,128]{1,0:T(8,128)(2,1)S(1)}, u32[]{:S(2)}, u32[]{:S(2)}) collective-permute-start(bf16[264,128]{1,0:T(8,128)(2,1)S(1)} %get-tuple-element.110), channel_id=1, source_target_pairs={{0,5},{1,4},{2,7},{3,6},{4,1},{5,0},{6,3},{7,2},{8,13},{9,12},{10,... | collective-permute-start | bytes 202760 | tf_op jit(solution)/shard_map/ppermute | solution.py:566
  20.3 7.7 %collective-permute-start.11 = (bf16[264,128]{1,0:T(8,128)(2,1)S(1)}, bf16[264,128]{1,0:T(8,128)(2,1)S(1)}, u32[]{:S(2)}, u32[]{:S(2)}) collective-permute-start(bf16[264,128]{1,0:T(8,128)(2,1)S(1)} %get-tuple-element.111), channel_id=1, source_target_pairs={{0,6},{1,7},{2,4},{3,5},{4,2},{5,3},{6,0},{7,1},{8,14},{9,15},{10,... | collective-permute-start | bytes 202760 | tf_op jit(solution)/shard_map/ppermute | solution.py:566
  23.1 8.9 %collective-permute-start.12 = (bf16[264,128]{1,0:T(8,128)(2,1)S(1)}, bf16[264,128]{1,0:T(8,128)(2,1)S(1)}, u32[]{:S(2)}, u32[]{:S(2)}) collective-permute-start(bf16[264,128]{1,0:T(8,128)(2,1)S(1)} %get-tuple-element.112), channel_id=1, source_target_pairs={{0,7},{1,6},{2,5},{3,4},{4,3},{5,2},{6,1},{7,0},{8,15},{9,14},{10,... | collective-permute-start | bytes 202760 | tf_op jit(solution)/shard_map/ppermute | solution.py:566
  25.3 6.7 %collective-permute-start.6 = (bf16[264,128]{1,0:T(8,128)(2,1)S(1)}, bf16[264,128]{1,0:T(8,128)(2,1)S(1)}, u32[]{:S(2)}, u32[]{:S(2)}) collective-permute-start(bf16[264,128]{1,0:T(8,128)(2,1)S(1)} %get-tuple-element.106), channel_id=1, source_target_pairs={{0,1},{1,0},{2,3},{3,2},{4,5},{5,4},{6,7},{7,6},{8,9},{9,8},{10,11... | collective-permute-start | bytes 202760 | tf_op jit(solution)/shard_map/ppermute | solution.py:566
  25.3 6.7 %collective-permute-start.7 = (bf16[264,128]{1,0:T(8,128)(2,1)S(1)}, bf16[264,128]{1,0:T(8,128)(2,1)S(1)}, u32[]{:S(2)}, u32[]{:S(2)}) collective-permute-start(bf16[264,128]{1,0:T(8,128)(2,1)S(1)} %get-tuple-element.107), channel_id=1, source_target_pairs={{0,2},{1,3},{2,0},{3,1},{4,6},{5,7},{6,4},{7,5},{8,10},{9,11},{10,... | collective-permute-start | bytes 202760 | tf_op jit(solution)/shard_map/ppermute | solution.py:566
  25.3 7.0 %collective-permute-start.8 = (bf16[264,128]{1,0:T(8,128)(2,1)S(1)}, bf16[264,128]{1,0:T(8,128)(2,1)S(1)}, u32[]{:S(2)}, u32[]{:S(2)}) collective-permute-start(bf16[264,128]{1,0:T(8,128)(2,1)S(1)} %get-tuple-element.108), channel_id=1, source_target_pairs={{0,3},{1,2},{2,1},{3,0},{4,7},{5,6},{6,5},{7,4},{8,11},{9,10},{10,... | collective-permute-start | bytes 202760 | tf_op jit(solution)/shard_map/ppermute | solution.py:566
  28.1 7.8 %collective-permute-start.9 = (bf16[264,128]{1,0:T(8,128)(2,1)S(1)}, bf16[264,128]{1,0:T(8,128)(2,1)S(1)}, u32[]{:S(2)}, u32[]{:S(2)}) collective-permute-start(bf16[264,128]{1,0:T(8,128)(2,1)S(1)} %get-tuple-element.109), channel_id=1, source_target_pairs={{0,4},{1,5},{2,6},{3,7},{4,0},{5,1},{6,2},{7,3},{8,12},{9,13},{10,... | collective-permute-start | bytes 202760 | tf_op jit(solution)/shard_map/ppermute | solution.py:566
  41.4 8.8 %collective-permute-start.13 = (bf16[64,512]{1,0:T(8,128)(2,1)S(1)}, bf16[64,512]{1,0:T(8,128)(2,1)S(1)}, u32[]{:S(2)}, u32[]{:S(2)}) collective-permute-start(bf16[64,512]{1,0:T(8,128)(2,1)S(1)} %get-tuple-element.114), channel_id=1, source_target_pairs={{0,1},{1,0},{2,3},{3,2},{4,5},{5,4},{6,7},{7,6},{8,9},{9,8},{10,11... | collective-permute-start | bytes 196616 | tf_op jit(solution)/shard_map/ppermute | solution.py:566
  41.6 10.7 %collective-permute-start.14 = (bf16[64,512]{1,0:T(8,128)(2,1)S(1)}, bf16[64,512]{1,0:T(8,128)(2,1)S(1)}, u32[]{:S(2)}, u32[]{:S(2)}) collective-permute-start(bf16[64,512]{1,0:T(8,128)(2,1)S(1)} %get-tuple-element.115), channel_id=1, source_target_pairs={{0,2},{1,3},{2,0},{3,1},{4,6},{5,7},{6,4},{7,5},{8,10},{9,11},{10,... | collective-permute-start | bytes 196616 | tf_op jit(solution)/shard_map/ppermute | solution.py:566
  41.9 4.2 %collective-permute-start.3 = (f32[16,256]{1,0:T(8,128)S(1)}, f32[16,256]{1,0:T(8,128)S(1)}, u32[]{:S(2)}, u32[]{:S(2)}) collective-permute-start(f32[16,256]{1,0:T(8,128)S(1)} %get-tuple-element.91.refs_2_), channel_id=1, source_target_pairs={{0,16},{8,24},{16,0},{24,8},{1,17},{9,25},{17,1},{25,9},{2,18},{10... | collective-permute-start | bytes 49160 | tf_op jit(solution)/shard_map/ppermute | solution.py:566
  43.9 3.9 %collective-permute-start.4 = (f32[16,256]{1,0:T(8,128)S(1)}, f32[16,256]{1,0:T(8,128)S(1)}, u32[]{:S(2)}, u32[]{:S(2)}) collective-permute-start(f32[16,256]{1,0:T(8,128)S(1)} %get-tuple-element.91.refs_2_), channel_id=1, source_target_pairs={{0,8},{8,0},{16,24},{24,16},{1,9},{9,1},{17,25},{25,17},{2,10},{10... | collective-permute-start | bytes 49160 | tf_op jit(solution)/shard_map/ppermute | solution.py:566
  45.4 4.6 %collective-permute-start.5 = (f32[16,256]{1,0:T(8,128)S(1)}, f32[16,256]{1,0:T(8,128)S(1)}, u32[]{:S(2)}, u32[]{:S(2)}) collective-permute-start(f32[16,256]{1,0:T(8,128)S(1)} %get-tuple-element.91.refs_2_), channel_id=1, source_target_pairs={{0,24},{8,16},{16,8},{24,0},{1,25},{9,17},{17,9},{25,1},{2,26},{10... | collective-permute-start | bytes 49160 | tf_op jit(solution)/shard_map/ppermute | solution.py:566
  46.1 10.5 %collective-permute-start.15 = (bf16[64,512]{1,0:T(8,128)(2,1)S(1)}, bf16[64,512]{1,0:T(8,128)(2,1)S(1)}, u32[]{:S(2)}, u32[]{:S(2)}) collective-permute-start(bf16[64,512]{1,0:T(8,128)(2,1)S(1)} %get-tuple-element.116), channel_id=1, source_target_pairs={{0,3},{1,2},{2,1},{3,0},{4,7},{5,6},{6,5},{7,4},{8,11},{9,10},{10,... | collective-permute-start | bytes 196616 | tf_op jit(solution)/shard_map/ppermute | solution.py:566
  47.7 9.4 %collective-permute-start.16 = (bf16[64,512]{1,0:T(8,128)(2,1)S(1)}, bf16[64,512]{1,0:T(8,128)(2,1)S(1)}, u32[]{:S(2)}, u32[]{:S(2)}) collective-permute-start(bf16[64,512]{1,0:T(8,128)(2,1)S(1)} %get-tuple-element.117), channel_id=1, source_target_pairs={{0,4},{1,5},{2,6},{3,7},{4,0},{5,1},{6,2},{7,3},{8,12},{9,13},{10,... | collective-permute-start | bytes 196616 | tf_op jit(solution)/shard_map/ppermute | solution.py:566
  50.0 9.6 %collective-permute-start.17 = (bf16[64,512]{1,0:T(8,128)(2,1)S(1)}, bf16[64,512]{1,0:T(8,128)(2,1)S(1)}, u32[]{:S(2)}, u32[]{:S(2)}) collective-permute-start(bf16[64,512]{1,0:T(8,128)(2,1)S(1)} %get-tuple-element.118), channel_id=1, source_target_pairs={{0,5},{1,4},{2,7},{3,6},{4,1},{5,0},{6,3},{7,2},{8,13},{9,12},{10,... | collective-permute-start | bytes 196616 | tf_op jit(solution)/shard_map/ppermute | solution.py:566
  50.2 9.4 %collective-permute-start.18 = (bf16[64,512]{1,0:T(8,128)(2,1)S(1)}, bf16[64,512]{1,0:T(8,128)(2,1)S(1)}, u32[]{:S(2)}, u32[]{:S(2)}) collective-permute-start(bf16[64,512]{1,0:T(8,128)(2,1)S(1)} %get-tuple-element.119), channel_id=1, source_target_pairs={{0,6},{1,7},{2,4},{3,5},{4,2},{5,3},{6,0},{7,1},{8,14},{9,15},{10,... | collective-permute-start | bytes 196616 | tf_op jit(solution)/shard_map/ppermute | solution.py:566
  52.3 7.3 %collective-permute-start.19 = (bf16[64,512]{1,0:T(8,128)(2,1)S(1)}, bf16[64,512]{1,0:T(8,128)(2,1)S(1)}, u32[]{:S(2)}, u32[]{:S(2)}) collective-permute-start(bf16[64,512]{1,0:T(8,128)(2,1)S(1)} %get-tuple-element.120), channel_id=1, source_target_pairs={{0,7},{1,6},{2,5},{3,4},{4,3},{5,2},{6,1},{7,0},{8,15},{9,14},{10,... | collective-permute-start | bytes 196616 | tf_op jit(solution)/shard_map/ppermute | solution.py:566
  60.4 10.4 %collective-permute-start.20 = (bf16[272,512]{1,0:T(8,128)(2,1)S(1)}, bf16[272,512]{1,0:T(8,128)(2,1)S(1)}, u32[]{:S(2)}, u32[]{:S(2)}) collective-permute-start(bf16[272,512]{1,0:T(8,128)(2,1)S(1)} %get-tuple-element.121.refs_14_), channel_id=1, source_target_pairs={{0,16},{8,24},{16,0},{24,8},{1,17},{9,25},{17,1},{25,9},{2,18},{10... | collective-permute-start | bytes 835592 | tf_op jit(solution)/shard_map/ppermute | solution.py:566
  61.1 11.5 %collective-permute-start.21 = (bf16[272,512]{1,0:T(8,128)(2,1)S(1)}, bf16[272,512]{1,0:T(8,128)(2,1)S(1)}, u32[]{:S(2)}, u32[]{:S(2)}) collective-permute-start(bf16[272,512]{1,0:T(8,128)(2,1)S(1)} %get-tuple-element.121.refs_14_), channel_id=1, source_target_pairs={{0,8},{8,0},{16,24},{24,16},{1,9},{9,1},{17,25},{25,17},{2,10},{10... | collective-permute-start | bytes 835592 | tf_op jit(solution)/shard_map/ppermute | solution.py:566
  62.6 13.7 %collective-permute-start.22 = (bf16[272,512]{1,0:T(8,128)(2,1)S(1)}, bf16[272,512]{1,0:T(8,128)(2,1)S(1)}, u32[]{:S(2)}, u32[]{:S(2)}) collective-permute-start(bf16[272,512]{1,0:T(8,128)(2,1)S(1)} %get-tuple-element.121.refs_14_), channel_id=1, source_target_pairs={{0,24},{8,16},{16,8},{24,0},{1,25},{9,17},{17,9},{25,1},{2,26},{10... | collective-permute-start | bytes 835592 | tf_op jit(solution)/shard_map/ppermute | solution.py:566
  (1 other events, 0.7 us)

commit v6 on v5

--- a/solution.py
+++ b/solution.py
@@ -108,17 +108,17 @@
 def unshifted(depth, t, q_tile, k_tile, v_tile, weights_ref):
     count = q_tile.shape[0]
     scale = depth ** (-0.5) * LOG2E
-    right = with_ones(v_tile)
-    mixed = jnp.zeros((count, LANES), F32)
-    sums = jnp.zeros((count, LANES), F32)
-    for j in range(LANES // depth):
-        mask = head_mask(count, j, depth)
-        scores = dot_nt(only(mask, q_tile), k_tile)
-        shifted = jnp.exp2(scores * scale).astype(BF16)
-        weights_ref[t * (LANES // depth) + j] = shifted
-        both = dot_nn(shifted, right)
-        mixed = jnp.where(mask, both[:, :LANES], mixed)
-        sums = jnp.where(mask, both[:, LANES:], sums)
+    heads = LANES // depth
+    masks = [head_mask(count, j, depth) for j in range(heads)]
+    q_heads = jnp.concatenate([only(mask, q_tile) for mask in masks], axis=0)
+    shifted = jnp.exp2(dot_nt(q_heads, k_tile) * scale).astype(BF16)
+    weights_ref[t * heads : (t + 1) * heads] = shifted.reshape(heads, count, -1)
+    both = dot_nn(shifted, with_ones(v_tile))
+    mixed, sums = both[:count, :LANES], both[:count, LANES:]
+    for j in range(1, heads):
+        part = slice(j * count, (j + 1) * count)
+        mixed = jnp.where(masks[j], both[part, :LANES], mixed)
+        sums = jnp.where(masks[j], both[part, LANES:], sums)
     return mixed, sums
 
 

time: 79.8 us -> 79.8 us (level)
  no operation moved by 1% of the time
where the time goes in v6:
time: 79.8 us; the launch traced here: 79.3 us
  Pallas kernels  32 us (40%)
  starting transfers between devices  30.2 us (38%)
  waiting for transfers between devices  15.4 us (19%)
  local copies, waits for them, and re-layouts  1.61 us (2%)
    ppermute x23, starting transfers between devices, by_xor(): return lax.ppermute(array, axis, [(i, i ^ step) for i in range(size)])  30.2 us
    ppermute x23, waiting for transfers between devices, by_xor(): return lax.ppermute(array, axis, [(i, i ^ step) for i in range(size)])  15.4 us
    pallas_call x1, Pallas kernels, shards(): vmem_call(functools.partial(query_grad_body, len(all_keys), depth), (rows...  6.84 us
    pallas_call x1, Pallas kernels, shards(): vmem_call(functools.partial(second_body, chunks, depth), (chunk_bf16,) *...  5.58 us
    pallas_call x2, Pallas kernels, shards(): vmem_call(functools.partial(key_middle_body, index, depth), (rows_f32, ro...  3.69 us
    pallas_call x2, Pallas kernels, shards(): vmem_call(functools.partial(middle_body, depth), (rows_bf16,) * 2 + (squa...  3.54 us
    pallas_call x1, Pallas kernels, shards(): vmem_call(functools.partial(key_grad_body, early, peers, depth), rows_bf1...  3.01 us
    pallas_call x1, Pallas kernels, shards(): vmem_call(functools.partial(forward_body, early, peers, chunks, capacity,...  2.76 us
  transfers between devices with their start and end apart: 23, of which 10 were waited for; matrix products, arithmetic and copies ran while one was open for 0% of the time, Pallas kernels for 25%

profile of v6, /device:TPU:0, one launch (start us, length us, event | category | flops | bytes accessed | tf_op | source)
XLA Modules:
  0.0 79.3 jit_solution(5731075469186694015)
XLA Ops:
  0.0 3.0 %collective-permute-start = (bf16[256,512]{1,0:T(8,128)(2,1)}, bf16[256,512]{1,0:T(8,128)(2,1)S(1)}, u32[]{:S(2)}, u32[]{:S(2)}) collective-permute-start(bf16[256,512]{1,0:T(8,128)(2,1)} %bitcast.13), channel_id=1, source_target_pairs={{0,16},{8,24},{16,0},{24,8},{1,17},{9,25},{17,1},{25,9},{2,18},{10... | collective-permute-start | bytes 786440 | tf_op jit(solution)/shard_map/ppermute | solution.py:566
  3.0 1.5 %collective-permute-start.1 = (bf16[256,512]{1,0:T(8,128)(2,1)}, bf16[256,512]{1,0:T(8,128)(2,1)S(1)}, u32[]{:S(2)}, u32[]{:S(2)}) collective-permute-start(bf16[256,512]{1,0:T(8,128)(2,1)} %bitcast.14), channel_id=1, source_target_pairs={{0,8},{8,0},{16,24},{24,16},{1,9},{9,1},{17,25},{25,17},{2,10},{10... | collective-permute-start | bytes 786440 | tf_op jit(solution)/shard_map/ppermute | solution.py:566
  5.7 0.9 %copy-done = bf16[512,1536]{1,0:T(8,128)(2,1)S(1)} copy-done((bf16[512,1536]{1,0:T(8,128)(2,1)S(1)}, bf16[512,1536]{1,0:T(8,128)(2,1)}, u32[]{:S(2)}) %copy-start) | copy-done | bytes 1572888
  6.6 1.9 %shard_map.101 = (bf16[256,512]{1,0:T(8,128)(2,1)S(1)}, bf16[256,512]{1,0:T(8,128)(2,1)S(1)}, bf16[256,512]{1,0:T(8,128)(2,1)S(1)}, bf16[16,256,256]{2,1,0:T(8,1...) custom-call(bf16[256,512]{1,0:T(8,128)(2,1)S(1)} %bitcast.16, ...), custom_call_target="tpu_custom_call" | custom-call | flops 2147483648 | bytes 4194304 | tf_op jit(solution)/shard_map/pallas_call | solution.py:628
  8.6 1.0 %collective-permute-done.refs_3_.refs_0_ = bf16[256,512]{1,0:T(8,128)(2,1)S(1)} collective-permute-done((bf16[256,512]{1,0:T(8,128)(2,1)}, bf16[256,512]{1,0:T(8,128)(2,1)S(1)}, u32[]{:S(2)}, u32[]{:S(2)}) %collective-permute-start) | collective-permute-done | bytes 262176 | tf_op jit(solution)/shard_map/ppermute | solution.py:566
  9.5 1.8 %shard_map.103 = (bf16[256,512]{1,0:T(8,128)(2,1)S(1)}, bf16[256,512]{1,0:T(8,128)(2,1)S(1)}, bf16[16,256,256]{2,1,0:T(8,128)(2,1)S(1)}, f32[256,512]{1,0:T(8,128)S(1)}, f32[256,512]{1,0:T(8,128)S(1)}) custom-call(bf16[256,512]{1,0:T(8,128)(2,1)S(1)} %collective-permute-done.refs_3_.refs_0_, f32[1,512]{1,0:T(1,128)S(1)} %bitcast.9, ...), custom_call_target="tpu_custom_call" | custom-call | flops 2147483648 | bytes 4194304 | tf_op jit(solution)/shard_map/pallas_call | solution.py:636
  11.3 1.1 %collective-permute-done.1.refs_4_.refs_0_ = bf16[256,512]{1,0:T(8,128)(2,1)S(1)} collective-permute-done((bf16[256,512]{1,0:T(8,128)(2,1)}, bf16[256,512]{1,0:T(8,128)(2,1)S(1)}, u32[]{:S(2)}, u32[]{:S(2)}) %collective-permute-start.1) | collective-permute-done | bytes 262176 | tf_op jit(solution)/shard_map/ppermute | solution.py:566
  12.4 1.8 %shard_map.104 = (bf16[256,512]{1,0:T(8,128)(2,1)S(1)}, bf16[256,512]{1,0:T(8,128)(2,1)S(1)}, bf16[16,256,256]{2,1,0:T(8,128)(2,1)S(1)}, f32[256,512]{1,0:T(8,128)S(1)}, f32[256,512]{1,0:T(8,128)S(1)}) custom-call(bf16[256,512]{1,0:T(8,128)(2,1)S(1)} %collective-permute-done.1.refs_4_.refs_0_, f32[1,512]{1,0:T(1,128)S(1)} %bitcast.10, ...), custom_call_target="tpu_custom_call" | custom-call | flops 2147483648 | bytes 4194304 | tf_op jit(solution)/shard_map/pallas_call | solution.py:636
  14.2 2.1 %collective-permute-done.2.refs_5_.refs_15_ = bf16[256,512]{1,0:T(8,128)(2,1)S(1)} collective-permute-done((bf16[256,512]{1,0:T(8,128)(2,1)}, bf16[256,512]{1,0:T(8,128)(2,1)S(1)}, u32[]{:S(2)}, u32[]{:S(2)}) %collective-permute-start.2) | collective-permute-done | bytes 262176 | tf_op jit(solution)/shard_map/ppermute | solution.py:566
  16.4 2.8 %shard_map.105 = (bf16[256,512]{1,0:T(8,128)(2,1)S(1)}, bf16[256,512]{1,0:T(8,128)(2,1)S(1)}, bf16[16,256,256]{2,1,0:T(8,128)(2,1)S(1)}, f32[256,512]{1,0:T(8,12...) custom-call(bf16[256,512]{1,0:T(8,128)(2,1)S(1)} %bitcast.17, ...), custom_call_target="tpu_custom_call", output_to_operand_aliasing={{6}: (16, {}), {7}: (17, {}), {8}: (18, {})} | custom-call | flops 8589934592 | bytes 8388608 | tf_op jit(solution)/shard_map/pallas_call | solution.py:651
  19.1 1.2 %collective-permute-start.10 = (bf16[264,128]{1,0:T(8,128)(2,1)S(1)}, bf16[264,128]{1,0:T(8,128)(2,1)S(1)}, u32[]{:S(2)}, u32[]{:S(2)}) collective-permute-start(bf16[264,128]{1,0:T(8,128)(2,1)S(1)} %get-tuple-element.110), channel_id=1, source_target_pairs={{0,5},{1,4},{2,7},{3,6},{4,1},{5,0},{6,3},{7,2},{8,13},{9,12},{10,... | collective-permute-start | bytes 202760 | tf_op jit(solution)/shard_map/ppermute | solution.py:566
  20.3 2.8 %collective-permute-start.11 = (bf16[264,128]{1,0:T(8,128)(2,1)S(1)}, bf16[264,128]{1,0:T(8,128)(2,1)S(1)}, u32[]{:S(2)}, u32[]{:S(2)}) collective-permute-start(bf16[264,128]{1,0:T(8,128)(2,1)S(1)} %get-tuple-element.111), channel_id=1, source_target_pairs={{0,6},{1,7},{2,4},{3,5},{4,2},{5,3},{6,0},{7,1},{8,14},{9,15},{10,... | collective-permute-start | bytes 202760 | tf_op jit(solution)/shard_map/ppermute | solution.py:566
  23.1 2.2 %collective-permute-start.12 = (bf16[264,128]{1,0:T(8,128)(2,1)S(1)}, bf16[264,128]{1,0:T(8,128)(2,1)S(1)}, u32[]{:S(2)}, u32[]{:S(2)}) collective-permute-start(bf16[264,128]{1,0:T(8,128)(2,1)S(1)} %get-tuple-element.112), channel_id=1, source_target_pairs={{0,7},{1,6},{2,5},{3,4},{4,3},{5,2},{6,1},{7,0},{8,15},{9,14},{10,... | collective-permute-start | bytes 202760 | tf_op jit(solution)/shard_map/ppermute | solution.py:566
  25.3 2.8 %collective-permute-start.8 = (bf16[264,128]{1,0:T(8,128)(2,1)S(1)}, bf16[264,128]{1,0:T(8,128)(2,1)S(1)}, u32[]{:S(2)}, u32[]{:S(2)}) collective-permute-start(bf16[264,128]{1,0:T(8,128)(2,1)S(1)} %get-tuple-element.108), channel_id=1, source_target_pairs={{0,3},{1,2},{2,1},{3,0},{4,7},{5,6},{6,5},{7,4},{8,11},{9,10},{10,... | collective-permute-start | bytes 202760 | tf_op jit(solution)/shard_map/ppermute | solution.py:566
  28.0 3.6 %collective-permute-start.9 = (bf16[264,128]{1,0:T(8,128)(2,1)S(1)}, bf16[264,128]{1,0:T(8,128)(2,1)S(1)}, u32[]{:S(2)}, u32[]{:S(2)}) collective-permute-start(bf16[264,128]{1,0:T(8,128)(2,1)S(1)} %get-tuple-element.109), channel_id=1, source_target_pairs={{0,4},{1,5},{2,6},{3,7},{4,0},{5,1},{6,2},{7,3},{8,12},{9,13},{10,... | collective-permute-start | bytes 202760 | tf_op jit(solution)/shard_map/ppermute | solution.py:566
  32.3 3.5 %collective-permute-done.9.refs_10_ = bf16[264,128]{1,0:T(8,128)(2,1)S(1)} collective-permute-done((bf16[264,128]{1,0:T(8,128)(2,1)S(1)}, bf16[264,128]{1,0:T(8,128)(2,1)S(1)}, u32[]{:S(2)}, u32[]{:S(2)}) %collective-permute-start.9) | collective-permute-done | bytes 67616 | tf_op jit(solution)/shard_map/ppermute | solution.py:566
  35.8 5.6 %shard_map.108 = (bf16[64,512]{1,0:T(8,128)(2,1)S(1)}, bf16[64,512]{1,0:T(8,128)(2,1)S(1)}, bf16[64,512]{1,0:T(8,128)(2,1)S(1)}, bf16[64,512]{1,0:T(8,128)(2,1)S...) custom-call(f32[1,512]{1,0:T(1,128)S(1)} %get-tuple-element.76.refs_, ...), custom_call_target="tpu_custom_call" | custom-call | flops 8589934592 | bytes 4194304 | tf_op jit(solution)/shard_map/pallas_call | solution.py:706
  41.9 1.9 %collective-permute-start.3 = (f32[16,256]{1,0:T(8,128)S(1)}, f32[16,256]{1,0:T(8,128)S(1)}, u32[]{:S(2)}, u32[]{:S(2)}) collective-permute-start(f32[16,256]{1,0:T(8,128)S(1)} %get-tuple-element.91.refs_2_), channel_id=1, source_target_pairs={{0,16},{8,24},{16,0},{24,8},{1,17},{9,25},{17,1},{25,9},{2,18},{10... | collective-permute-start | bytes 49160 | tf_op jit(solution)/shard_map/ppermute | solution.py:566
  43.8 1.5 %collective-permute-start.4 = (f32[16,256]{1,0:T(8,128)S(1)}, f32[16,256]{1,0:T(8,128)S(1)}, u32[]{:S(2)}, u32[]{:S(2)}) collective-permute-start(f32[16,256]{1,0:T(8,128)S(1)} %get-tuple-element.91.refs_2_), channel_id=1, source_target_pairs={{0,8},{8,0},{16,24},{24,16},{1,9},{9,1},{17,25},{25,17},{2,10},{10... | collective-permute-start | bytes 49160 | tf_op jit(solution)/shard_map/ppermute | solution.py:566
  46.7 1.0 %collective-permute-done.4.refs_4_ = f32[16,256]{1,0:T(8,128)S(1)} collective-permute-done((f32[16,256]{1,0:T(8,128)S(1)}, f32[16,256]{1,0:T(8,128)S(1)}, u32[]{:S(2)}, u32[]{:S(2)}) %collective-permute-start.4) | collective-permute-done | bytes 16416 | tf_op jit(solution)/shard_map/ppermute | solution.py:566
  48.5 1.5 %collective-permute-done.5.refs_5_ = f32[16,256]{1,0:T(8,128)S(1)} collective-permute-done((f32[16,256]{1,0:T(8,128)S(1)}, f32[16,256]{1,0:T(8,128)S(1)}, u32[]{:S(2)}, u32[]{:S(2)}) %collective-permute-start.5) | collective-permute-done | bytes 16416 | tf_op jit(solution)/shard_map/ppermute | solution.py:566
  50.2 2.1 %collective-permute-start.18 = (bf16[64,512]{1,0:T(8,128)(2,1)S(1)}, bf16[64,512]{1,0:T(8,128)(2,1)S(1)}, u32[]{:S(2)}, u32[]{:S(2)}) collective-permute-start(bf16[64,512]{1,0:T(8,128)(2,1)S(1)} %get-tuple-element.119), channel_id=1, source_target_pairs={{0,6},{1,7},{2,4},{3,5},{4,2},{5,3},{6,0},{7,1},{8,14},{9,15},{10,... | collective-permute-start | bytes 196616 | tf_op jit(solution)/shard_map/ppermute | solution.py:566
  52.3 1.9 %collective-permute-start.19 = (bf16[64,512]{1,0:T(8,128)(2,1)S(1)}, bf16[64,512]{1,0:T(8,128)(2,1)S(1)}, u32[]{:S(2)}, u32[]{:S(2)}) collective-permute-start(bf16[64,512]{1,0:T(8,128)(2,1)S(1)} %get-tuple-element.120), channel_id=1, source_target_pairs={{0,7},{1,6},{2,5},{3,4},{4,3},{5,2},{6,1},{7,0},{8,15},{9,14},{10,... | collective-permute-start | bytes 196616 | tf_op jit(solution)/shard_map/ppermute | solution.py:566
  54.2 2.3 %shard_map.106.refs_13_.refs_0_ = bf16[16,256,1024]{2,1,0:T(8,128)(2,1)S(1)} custom-call(bf16[256,512]{1,0:T(8,128)(2,1)S(1)} %get-tuple-element.73.refs_9_.refs_0_.refs_4_, bf16[1024,512]{1,0:T(8,128)(2,1)S(1)} %shard_map.102.refs_1_.refs_2_, f32[16,256]{1,0:T(8,128)S(1)} %get-tuple-element.91.refs_2_, f32[16,256]{1,0:T(8,128)S(1)} %collective-permute-done.3.refs_3_, ...), custom_call_target="tpu_custom_call" | custom-call | flops 4294967296 | bytes 10485760 | tf_op jit(solution)/shard_map/pallas_call | solution.py:696
  57.1 2.6 %collective-permute-done.17.refs_8_ = bf16[64,512]{1,0:T(8,128)(2,1)S(1)} collective-permute-done((bf16[64,512]{1,0:T(8,128)(2,1)S(1)}, bf16[64,512]{1,0:T(8,128)(2,1)S(1)}, u32[]{:S(2)}, u32[]{:S(2)}) %collective-permute-start.17) | collective-permute-done | bytes 65568 | tf_op jit(solution)/shard_map/ppermute | solution.py:566
  61.1 1.5 %collective-permute-start.21 = (bf16[272,512]{1,0:T(8,128)(2,1)S(1)}, bf16[272,512]{1,0:T(8,128)(2,1)S(1)}, u32[]{:S(2)}, u32[]{:S(2)}) collective-permute-start(bf16[272,512]{1,0:T(8,128)(2,1)S(1)} %get-tuple-element.121.refs_14_), channel_id=1, source_target_pairs={{0,8},{8,0},{16,24},{24,16},{1,9},{9,1},{17,25},{25,17},{2,10},{10... | collective-permute-start | bytes 835592 | tf_op jit(solution)/shard_map/ppermute | solution.py:566
  62.6 1.4 %collective-permute-start.22 = (bf16[272,512]{1,0:T(8,128)(2,1)S(1)}, bf16[272,512]{1,0:T(8,128)(2,1)S(1)}, u32[]{:S(2)}, u32[]{:S(2)}) collective-permute-start(bf16[272,512]{1,0:T(8,128)(2,1)S(1)} %get-tuple-element.121.refs_14_), channel_id=1, source_target_pairs={{0,24},{8,16},{16,8},{24,0},{1,25},{9,17},{17,9},{25,1},{2,26},{10... | collective-permute-start | bytes 835592 | tf_op jit(solution)/shard_map/ppermute | solution.py:566
  64.0 6.8 %shard_map.110 = (f32[256,512]{1,0:T(8,128)S(1)}, f32[256,512]{1,0:T(8,128)S(1)}, f32[256,512]{1,0:T(8,128)S(1)}) custom-call(bf16[16,256,256]{2,1,0:T(8,128)(2,1)S(1)} %get-tuple-element.92.refs_0_, bf16[16,256,256]{2,1,0:T(8,128)(2,1)S(1)} %get-tuple-element.93.refs_1_, bf16[16,256,256]{2,1,0:T(8,128)(2,1)S(1)} %get-tuple-element.94.refs_2_, ...), custom_call_target="tpu_custom_call" | custom-call | flops 8589934592 | bytes 10485760 | tf_op jit(solution)/shard_map/pallas_call | solution.py:731
  70.8 1.8 %shard_map.111 = (f32[256,512]{1,0:T(8,128)S(1)}, f32[256,512]{1,0:T(8,128)S(1)}) custom-call(bf16[16,256,1024]{2,1,0:T(8,128)(2,1)S(1)} %shard_map.106.refs_13_.refs_0_, bf16[256,512]{1,0:T(8,128)(2,1)S(1)} %get-tuple-element.85.refs_12_.refs_8_.refs_1_, bf16[1024,512]{1,0:T(8,128)(2,1)S(1)} %shard_map.102.refs_1_.refs_2_, ...), custom_call_target="tpu_custom_call" | custom-call | flops 2147483648 | bytes 4194304 | tf_op jit(solution)/shard_map/pallas_call | solution.py:742
  72.7 1.8 %shard_map.112 = (f32[256,512]{1,0:T(8,128)S(1)}, f32[256,512]{1,0:T(8,128)S(1)}) custom-call(bf16[16,256,1024]{2,1,0:T(8,128)(2,1)S(1)} %shard_map.106.refs_13_.refs_0_, bf16[256,512]{1,0:T(8,128)(2,1)S(1)} %get-tuple-element.85.refs_12_.refs_8_.refs_1_, bf16[1024,512]{1,0:T(8,128)(2,1)S(1)} %shard_map.102.refs_1_.refs_2_, ...), custom_call_target="tpu_custom_call" | custom-call | flops 2147483648 | bytes 4194304 | tf_op jit(solution)/shard_map/pallas_call | solution.py:742
  74.5 1.8 %collective-permute-done.22.refs_10_ = bf16[272,512]{1,0:T(8,128)(2,1)S(1)} collective-permute-done((bf16[272,512]{1,0:T(8,128)(2,1)S(1)}, bf16[272,512]{1,0:T(8,128)(2,1)S(1)}, u32[]{:S(2)}, u32[]{:S(2)}) %collective-permute-start.22) | collective-permute-done | bytes 278560 | tf_op jit(solution)/shard_map/ppermute | solution.py:566
  76.3 3.0 %shard_map.113 = bf16[256,512]{1,0:T(8,128)(2,1)} custom-call(bf16[16,256,1024]{2,1,0:T(8,128)(2,1)S(1)} %shard_map.106.refs_13_.refs_0_, bf16[256,512]{1,0:T(8,128)(2,1)S(1)} %get-tuple-element.85.refs_12_.refs_8_.refs_1_, bf16[1024,512]{1,0:T(8,128)(2,1)S(1)} %shard_map.102.refs_1_.refs_2_, f32[256,512]{1,0:T(8,128)S(1)} %get-tuple-element.123.refs_3_, ...), custom_call_target="tpu_custom_call" | custom-call | flops 8589934592 | bytes 14680064 | tf_op jit(solution)/shard_map/pallas_call | solution.py:749
  (48 shorter events, 6.8 us)
Async XLA Ops:
  0.0 9.5 %collective-permute-start = (bf16[256,512]{1,0:T(8,128)(2,1)}, bf16[256,512]{1,0:T(8,128)(2,1)S(1)}, u32[]{:S(2)}, u32[]{:S(2)}) collective-permute-start(bf16[256,512]{1,0:T(8,128)(2,1)} %bitcast.13), channel_id=1, source_target_pairs={{0,16},{8,24},{16,0},{24,8},{1,17},{9,25},{17,1},{25,9},{2,18},{10... | collective-permute-start | bytes 786440 | tf_op jit(solution)/shard_map/ppermute | solution.py:566
  3.0 9.4 %collective-permute-start.1 = (bf16[256,512]{1,0:T(8,128)(2,1)}, bf16[256,512]{1,0:T(8,128)(2,1)S(1)}, u32[]{:S(2)}, u32[]{:S(2)}) collective-permute-start(bf16[256,512]{1,0:T(8,128)(2,1)} %bitcast.14), channel_id=1, source_target_pairs={{0,8},{8,0},{16,24},{24,16},{1,9},{9,1},{17,25},{25,17},{2,10},{10... | collective-permute-start | bytes 786440 | tf_op jit(solution)/shard_map/ppermute | solution.py:566
  4.5 11.8 %collective-permute-start.2 = (bf16[256,512]{1,0:T(8,128)(2,1)}, bf16[256,512]{1,0:T(8,128)(2,1)S(1)}, u32[]{:S(2)}, u32[]{:S(2)}) collective-permute-start(bf16[256,512]{1,0:T(8,128)(2,1)} %bitcast.15), channel_id=1, source_target_pairs={{0,24},{8,16},{16,8},{24,0},{1,25},{9,17},{17,9},{25,1},{2,26},{10... | collective-permute-start | bytes 786440 | tf_op jit(solution)/shard_map/ppermute | solution.py:566
  5.2 1.4 %copy-start = (bf16[512,1536]{1,0:T(8,128)(2,1)S(1)}, bf16[512,1536]{1,0:T(8,128)(2,1)}, u32[]{:S(2)}) copy-start(bf16[512,1536]{1,0:T(8,128)(2,1)} %refs_8_.1) | copy-start | bytes 4718596
  5.2 1.4 %copy-start.1 = (f32[512]{0:T(512)S(1)}, f32[512]{0:T(512)}, u32[]{:S(2)}) copy-start(f32[512]{0:T(512)} %param.11) | copy-start | bytes 6148
  5.2 1.4 %copy-start.5 = (bf16[1,1,256,512]{3,2,1,0:T(8,128)(2,1)S(1)}, bf16[1,1,256,512]{3,2,1,0:T(8,128)(2,1)}, u32[]{:S(2)}) copy-start(bf16[1,1,256,512]{3,2,1,0:T(8,128)(2,1)} %param.10) | copy-start | bytes 786436
  12.4 3.9 %copy-start.4 = (bf16[512,512]{1,0:T(8,128)(2,1)S(1)}, bf16[512,512]{1,0:T(8,128)(2,1)}, u32[]{:S(2)}) copy-start(bf16[512,512]{1,0:T(8,128)(2,1)} %refs_2_.11) | copy-start | bytes 1572868
  16.3 15.3 %copy-start.3 = (bf16[512,512]{1,0:T(8,128)(2,1)S(1)}, bf16[512,512]{1,0:T(8,128)(2,1)}, u32[]{:S(2)}) copy-start(bf16[512,512]{1,0:T(8,128)(2,1)} %out_w_ref.1) | copy-start | bytes 1572868
  16.3 15.3 %copy-start.6 = (bf16[1,1,256,512]{3,2,1,0:T(8,128)(2,1)S(1)}, bf16[1,1,256,512]{3,2,1,0:T(8,128)(2,1)}, u32[]{:S(2)}) copy-start(bf16[1,1,256,512]{3,2,1,0:T(8,128)(2,1)} %param.19) | copy-start | bytes 786436
  16.3 15.3 %copy-start.9 = (s32[1,1,256]{2,1,0:T(1,128)S(1)}, s32[1,1,256]{2,1,0:T(1,128)}, u32[]{:S(2)}) copy-start(s32[1,1,256]{2,1,0:T(1,128)} %param.18) | copy-start | bytes 3076
  16.3 19.5 %copy-start.2 = (bf16[512,1536]{1,0:T(8,128)(2,1)S(1)}, bf16[512,1536]{1,0:T(8,128)(2,1)}, u32[]{:S(2)}) copy-start(bf16[512,1536]{1,0:T(8,128)(2,1)} %refs_2_.10) | copy-start | bytes 4718596
  16.3 19.5 %copy-start.7 = (f32[512]{0:T(512)S(1)}, f32[512]{0:T(512)}, u32[]{:S(2)}) copy-start(f32[512]{0:T(512)} %param.15) | copy-start | bytes 6148
  19.1 6.2 %collective-permute-start.10 = (bf16[264,128]{1,0:T(8,128)(2,1)S(1)}, bf16[264,128]{1,0:T(8,128)(2,1)S(1)}, u32[]{:S(2)}, u32[]{:S(2)}) collective-permute-start(bf16[264,128]{1,0:T(8,128)(2,1)S(1)} %get-tuple-element.110), channel_id=1, source_target_pairs={{0,5},{1,4},{2,7},{3,6},{4,1},{5,0},{6,3},{7,2},{8,13},{9,12},{10,... | collective-permute-start | bytes 202760 | tf_op jit(solution)/shard_map/ppermute | solution.py:566
  20.3 7.7 %collective-permute-start.11 = (bf16[264,128]{1,0:T(8,128)(2,1)S(1)}, bf16[264,128]{1,0:T(8,128)(2,1)S(1)}, u32[]{:S(2)}, u32[]{:S(2)}) collective-permute-start(bf16[264,128]{1,0:T(8,128)(2,1)S(1)} %get-tuple-element.111), channel_id=1, source_target_pairs={{0,6},{1,7},{2,4},{3,5},{4,2},{5,3},{6,0},{7,1},{8,14},{9,15},{10,... | collective-permute-start | bytes 202760 | tf_op jit(solution)/shard_map/ppermute | solution.py:566
  23.1 8.9 %collective-permute-start.12 = (bf16[264,128]{1,0:T(8,128)(2,1)S(1)}, bf16[264,128]{1,0:T(8,128)(2,1)S(1)}, u32[]{:S(2)}, u32[]{:S(2)}) collective-permute-start(bf16[264,128]{1,0:T(8,128)(2,1)S(1)} %get-tuple-element.112), channel_id=1, source_target_pairs={{0,7},{1,6},{2,5},{3,4},{4,3},{5,2},{6,1},{7,0},{8,15},{9,14},{10,... | collective-permute-start | bytes 202760 | tf_op jit(solution)/shard_map/ppermute | solution.py:566
  25.3 6.7 %collective-permute-start.6 = (bf16[264,128]{1,0:T(8,128)(2,1)S(1)}, bf16[264,128]{1,0:T(8,128)(2,1)S(1)}, u32[]{:S(2)}, u32[]{:S(2)}) collective-permute-start(bf16[264,128]{1,0:T(8,128)(2,1)S(1)} %get-tuple-element.106), channel_id=1, source_target_pairs={{0,1},{1,0},{2,3},{3,2},{4,5},{5,4},{6,7},{7,6},{8,9},{9,8},{10,11... | collective-permute-start | bytes 202760 | tf_op jit(solution)/shard_map/ppermute | solution.py:566
  25.3 6.7 %collective-permute-start.7 = (bf16[264,128]{1,0:T(8,128)(2,1)S(1)}, bf16[264,128]{1,0:T(8,128)(2,1)S(1)}, u32[]{:S(2)}, u32[]{:S(2)}) collective-permute-start(bf16[264,128]{1,0:T(8,128)(2,1)S(1)} %get-tuple-element.107), channel_id=1, source_target_pairs={{0,2},{1,3},{2,0},{3,1},{4,6},{5,7},{6,4},{7,5},{8,10},{9,11},{10,... | collective-permute-start | bytes 202760 | tf_op jit(solution)/shard_map/ppermute | solution.py:566
  25.3 7.0 %collective-permute-start.8 = (bf16[264,128]{1,0:T(8,128)(2,1)S(1)}, bf16[264,128]{1,0:T(8,128)(2,1)S(1)}, u32[]{:S(2)}, u32[]{:S(2)}) collective-permute-start(bf16[264,128]{1,0:T(8,128)(2,1)S(1)} %get-tuple-element.108), channel_id=1, source_target_pairs={{0,3},{1,2},{2,1},{3,0},{4,7},{5,6},{6,5},{7,4},{8,11},{9,10},{10,... | collective-permute-start | bytes 202760 | tf_op jit(solution)/shard_map/ppermute | solution.py:566
  28.0 7.8 %collective-permute-start.9 = (bf16[264,128]{1,0:T(8,128)(2,1)S(1)}, bf16[264,128]{1,0:T(8,128)(2,1)S(1)}, u32[]{:S(2)}, u32[]{:S(2)}) collective-permute-start(bf16[264,128]{1,0:T(8,128)(2,1)S(1)} %get-tuple-element.109), channel_id=1, source_target_pairs={{0,4},{1,5},{2,6},{3,7},{4,0},{5,1},{6,2},{7,3},{8,12},{9,13},{10,... | collective-permute-start | bytes 202760 | tf_op jit(solution)/shard_map/ppermute | solution.py:566
  41.4 8.8 %collective-permute-start.13 = (bf16[64,512]{1,0:T(8,128)(2,1)S(1)}, bf16[64,512]{1,0:T(8,128)(2,1)S(1)}, u32[]{:S(2)}, u32[]{:S(2)}) collective-permute-start(bf16[64,512]{1,0:T(8,128)(2,1)S(1)} %get-tuple-element.114), channel_id=1, source_target_pairs={{0,1},{1,0},{2,3},{3,2},{4,5},{5,4},{6,7},{7,6},{8,9},{9,8},{10,11... | collective-permute-start | bytes 196616 | tf_op jit(solution)/shard_map/ppermute | solution.py:566
  41.6 10.7 %collective-permute-start.14 = (bf16[64,512]{1,0:T(8,128)(2,1)S(1)}, bf16[64,512]{1,0:T(8,128)(2,1)S(1)}, u32[]{:S(2)}, u32[]{:S(2)}) collective-permute-start(bf16[64,512]{1,0:T(8,128)(2,1)S(1)} %get-tuple-element.115), channel_id=1, source_target_pairs={{0,2},{1,3},{2,0},{3,1},{4,6},{5,7},{6,4},{7,5},{8,10},{9,11},{10,... | collective-permute-start | bytes 196616 | tf_op jit(solution)/shard_map/ppermute | solution.py:566
  41.9 4.2 %collective-permute-start.3 = (f32[16,256]{1,0:T(8,128)S(1)}, f32[16,256]{1,0:T(8,128)S(1)}, u32[]{:S(2)}, u32[]{:S(2)}) collective-permute-start(f32[16,256]{1,0:T(8,128)S(1)} %get-tuple-element.91.refs_2_), channel_id=1, source_target_pairs={{0,16},{8,24},{16,0},{24,8},{1,17},{9,25},{17,1},{25,9},{2,18},{10... | collective-permute-start | bytes 49160 | tf_op jit(solution)/shard_map/ppermute | solution.py:566
  43.8 3.8 %collective-permute-start.4 = (f32[16,256]{1,0:T(8,128)S(1)}, f32[16,256]{1,0:T(8,128)S(1)}, u32[]{:S(2)}, u32[]{:S(2)}) collective-permute-start(f32[16,256]{1,0:T(8,128)S(1)} %get-tuple-element.91.refs_2_), channel_id=1, source_target_pairs={{0,8},{8,0},{16,24},{24,16},{1,9},{9,1},{17,25},{25,17},{2,10},{10... | collective-permute-start | bytes 49160 | tf_op jit(solution)/shard_map/ppermute | solution.py:566
  45.3 4.6 %collective-permute-start.5 = (f32[16,256]{1,0:T(8,128)S(1)}, f32[16,256]{1,0:T(8,128)S(1)}, u32[]{:S(2)}, u32[]{:S(2)}) collective-permute-start(f32[16,256]{1,0:T(8,128)S(1)} %get-tuple-element.91.refs_2_), channel_id=1, source_target_pairs={{0,24},{8,16},{16,8},{24,0},{1,25},{9,17},{17,9},{25,1},{2,26},{10... | collective-permute-start | bytes 49160 | tf_op jit(solution)/shard_map/ppermute | solution.py:566
  46.1 10.5 %collective-permute-start.15 = (bf16[64,512]{1,0:T(8,128)(2,1)S(1)}, bf16[64,512]{1,0:T(8,128)(2,1)S(1)}, u32[]{:S(2)}, u32[]{:S(2)}) collective-permute-start(bf16[64,512]{1,0:T(8,128)(2,1)S(1)} %get-tuple-element.116), channel_id=1, source_target_pairs={{0,3},{1,2},{2,1},{3,0},{4,7},{5,6},{6,5},{7,4},{8,11},{9,10},{10,... | collective-permute-start | bytes 196616 | tf_op jit(solution)/shard_map/ppermute | solution.py:566
  47.7 9.4 %collective-permute-start.16 = (bf16[64,512]{1,0:T(8,128)(2,1)S(1)}, bf16[64,512]{1,0:T(8,128)(2,1)S(1)}, u32[]{:S(2)}, u32[]{:S(2)}) collective-permute-start(bf16[64,512]{1,0:T(8,128)(2,1)S(1)} %get-tuple-element.117), channel_id=1, source_target_pairs={{0,4},{1,5},{2,6},{3,7},{4,0},{5,1},{6,2},{7,3},{8,12},{9,13},{10,... | collective-permute-start | bytes 196616 | tf_op jit(solution)/shard_map/ppermute | solution.py:566
  50.0 9.7 %collective-permute-start.17 = (bf16[64,512]{1,0:T(8,128)(2,1)S(1)}, bf16[64,512]{1,0:T(8,128)(2,1)S(1)}, u32[]{:S(2)}, u32[]{:S(2)}) collective-permute-start(bf16[64,512]{1,0:T(8,128)(2,1)S(1)} %get-tuple-element.118), channel_id=1, source_target_pairs={{0,5},{1,4},{2,7},{3,6},{4,1},{5,0},{6,3},{7,2},{8,13},{9,12},{10,... | collective-permute-start | bytes 196616 | tf_op jit(solution)/shard_map/ppermute | solution.py:566
  50.2 9.4 %collective-permute-start.18 = (bf16[64,512]{1,0:T(8,128)(2,1)S(1)}, bf16[64,512]{1,0:T(8,128)(2,1)S(1)}, u32[]{:S(2)}, u32[]{:S(2)}) collective-permute-start(bf16[64,512]{1,0:T(8,128)(2,1)S(1)} %get-tuple-element.119), channel_id=1, source_target_pairs={{0,6},{1,7},{2,4},{3,5},{4,2},{5,3},{6,0},{7,1},{8,14},{9,15},{10,... | collective-permute-start | bytes 196616 | tf_op jit(solution)/shard_map/ppermute | solution.py:566
  52.3 7.3 %collective-permute-start.19 = (bf16[64,512]{1,0:T(8,128)(2,1)S(1)}, bf16[64,512]{1,0:T(8,128)(2,1)S(1)}, u32[]{:S(2)}, u32[]{:S(2)}) collective-permute-start(bf16[64,512]{1,0:T(8,128)(2,1)S(1)} %get-tuple-element.120), channel_id=1, source_target_pairs={{0,7},{1,6},{2,5},{3,4},{4,3},{5,2},{6,1},{7,0},{8,15},{9,14},{10,... | collective-permute-start | bytes 196616 | tf_op jit(solution)/shard_map/ppermute | solution.py:566
  60.5 10.4 %collective-permute-start.20 = (bf16[272,512]{1,0:T(8,128)(2,1)S(1)}, bf16[272,512]{1,0:T(8,128)(2,1)S(1)}, u32[]{:S(2)}, u32[]{:S(2)}) collective-permute-start(bf16[272,512]{1,0:T(8,128)(2,1)S(1)} %get-tuple-element.121.refs_14_), channel_id=1, source_target_pairs={{0,16},{8,24},{16,0},{24,8},{1,17},{9,25},{17,1},{25,9},{2,18},{10... | collective-permute-start | bytes 835592 | tf_op jit(solution)/shard_map/ppermute | solution.py:566
  61.1 11.6 %collective-permute-start.21 = (bf16[272,512]{1,0:T(8,128)(2,1)S(1)}, bf16[272,512]{1,0:T(8,128)(2,1)S(1)}, u32[]{:S(2)}, u32[]{:S(2)}) collective-permute-start(bf16[272,512]{1,0:T(8,128)(2,1)S(1)} %get-tuple-element.121.refs_14_), channel_id=1, source_target_pairs={{0,8},{8,0},{16,24},{24,16},{1,9},{9,1},{17,25},{25,17},{2,10},{10... | collective-permute-start | bytes 835592 | tf_op jit(solution)/shard_map/ppermute | solution.py:566
  62.6 13.7 %collective-permute-start.22 = (bf16[272,512]{1,0:T(8,128)(2,1)S(1)}, bf16[272,512]{1,0:T(8,128)(2,1)S(1)}, u32[]{:S(2)}, u32[]{:S(2)}) collective-permute-start(bf16[272,512]{1,0:T(8,128)(2,1)S(1)} %get-tuple-element.121.refs_14_), channel_id=1, source_target_pairs={{0,24},{8,16},{16,8},{24,0},{1,25},{9,17},{17,9},{25,1},{2,26},{10... | collective-permute-start | bytes 835592 | tf_op jit(solution)/shard_map/ppermute | solution.py:566
  (1 other events, 0.7 us)
